TPU v7x, 128 devices: a whole 4x4x4 slice. The times are simulated.
128 devices in a mesh: row: 8 (over y, core), col: 16 (over z, x).
Axes of the slice: x: 4, y: 4, z: 4, core: 2. Of those that a mesh axis runs over, the one named last changes fastest.
Arguments:
- question_vectors: bfloat16 [2048, 2048], P('row', 'col'), may hold values from -0.5 to 0.5
- document_vectors: bfloat16 [2048, 2048], P('col', 'row'), may hold values from -0.5 to 0.5
- positive: int32 [2048], P('row'), may hold values from 0 to 2047
- tokens: bfloat16 [16384, 2048], P(('row', 'col')), may hold values from -6 to 6
- expert_ids: int32 [16384, 8], P(('row', 'col')), may hold values from 0 to 127, all different within a row; in each aligned block of 128 rows (0 to 127, 128 to 255, ...) at most 9 rows name the same one
- route_weights: float32 [16384, 8], P(('row', 'col')), may hold values from 0.03 to 0.3
- expert_gate_up: bfloat16 [128, 2048, 1536], P(('row', 'col')), may hold values from -0.125 to 0.125
- expert_down: bfloat16 [128, 768, 2048], P(('row', 'col')), may hold values from -0.21875 to 0.21875
Outputs:
- passage_grad: float32 [2048, 2048], P('col', 'row')
- token_grad: bfloat16 [16384, 2048], P(('row', 'col'))
- gate_up_grad: bfloat16 [128, 2048, 1536], P(('row', 'col'))
- down_grad: bfloat16 [128, 768, 2048], P(('row', 'col'))
Inputs may be any that keep to these rules, and one draw needn't show every extreme that they name: `expert_ids`: each token names 8 different experts; among the 128 tokens of one device no expert is named more than 9 times, a bound that some block reaches.
All inputs are finite; a program needn't handle non-finite values.
Results may differ from a plain program's by a relative error of at most 0.018.
Values may be sent and summed in bfloat16 or wider, within the bound.
No kernel may reach another device: no remote copies, remote signals or barrier semaphores. Data moves between devices by JAX's collectives and lax.ppermute only.
A program may use at most 192 MiB of HBM per device.

v0:
```python
import jax
import jax.numpy as jnp
from jax import lax
from jax.sharding import PartitionSpec as P

SEQ_LEN = 8


sharpness_divisor = 0.02


def sent_to_all(value, axis):
    peers = lax.axis_size(axis)
    return lax.all_to_all(
        jnp.broadcast_to(value[None], (peers, *value.shape)), axis, 0, 0, tiled=True
    )


def joined_along(tiles, dim):
    tiles = jnp.moveaxis(tiles, 0, dim)
    lengths = tiles.shape
    return tiles.reshape(*lengths[:dim], lengths[dim] * lengths[dim + 1], *lengths[dim + 2 :])


def gathered_copies(value, axis, dim):
    tiles = sent_to_all(value, axis)
    return joined_along(tiles, dim)


def collected_together(value, axis):
    leaves = jax.tree.leaves(value)
    turns = sorted(range(len(leaves)), key=lambda k: -leaves[k].size)
    width = (1, *leaves[turns[0]].shape)[-1]
    lines = [
        jnp.pad(leaves[k].reshape(-1), (0, -leaves[k].size % width)).reshape(-1, width)
        for k in turns
    ]
    both, at, found = (sent_to_all(jnp.concatenate(lines), axis), 0, {})
    for k, line in zip(turns, lines):
        piece = both[:, at : at + len(line)].reshape(len(both), -1)
        found[k] = piece[:, : leaves[k].size].reshape(-1, *leaves[k].shape)
        at += len(line)
    numbers = iter(range(len(leaves)))
    return jax.tree.map(lambda _: found[next(numbers)], value)


def folded_in_pairs(pieces, combine):
    while len(jax.tree.leaves(pieces)[0]) > 1:
        pieces = jax.vmap(combine)(
            *(jax.tree.map(lambda part: part[side::2], pieces) for side in (0, 1))
        )
    return jax.tree.map(lambda part: part[0], pieces)


def combined_all(value, axis, combine):
    pieces = collected_together(value, axis)
    return folded_in_pairs(pieces, combine)


def split_up(value, dim, peers):
    lengths = value.shape
    tiles = value.reshape(*lengths[:dim], peers, lengths[dim] // peers, *lengths[dim + 1 :])
    return jnp.moveaxis(tiles, dim, 0)


def sent_and_summed(value, axis, dim):
    peers = lax.axis_size(axis)
    tiles = lax.all_to_all(split_up(value, dim, peers), axis, 0, 0, tiled=True)
    return jnp.sum(tiles.astype(jnp.float32), axis=0)


def expert_backward(slot_inputs, slot_grads, gate_up, down_proj):
    projected = jnp.dot(slot_inputs, gate_up, preferred_element_type=jnp.float32)
    hidden_width = down_proj.shape[0]
    gate_part = projected[:, :hidden_width]
    up_part = projected[:, hidden_width:]
    sigmoid_gate = jax.nn.sigmoid(gate_part)
    activated = gate_part * sigmoid_gate
    hidden = (activated * up_part).astype(jnp.bfloat16)
    down_grad = lax.dot_general(
        hidden, slot_grads, (((0,), (0,)), ((), ())), preferred_element_type=jnp.float32
    ).astype(jnp.bfloat16)
    hidden_grad = lax.dot_general(
        slot_grads, down_proj, (((1,), (1,)), ((), ())), preferred_element_type=jnp.float32
    )
    slope = sigmoid_gate * (1.0 + gate_part * (1.0 - sigmoid_gate))
    pre_grad = jnp.concatenate(
        [hidden_grad * up_part * slope, hidden_grad * activated], axis=1
    ).astype(jnp.bfloat16)
    gate_up_grad = lax.dot_general(
        slot_inputs, pre_grad, (((0,), (0,)), ((), ())), preferred_element_type=jnp.float32
    ).astype(jnp.bfloat16)
    input_grad = lax.dot_general(
        pre_grad, gate_up, (((1,), (1,)), ((), ())), preferred_element_type=jnp.float32
    ).astype(jnp.bfloat16)
    return (input_grad, gate_up_grad, down_grad)


def combine_stats(first, second):
    peak_first, total_first = first
    peak_second, total_second = second
    joined = jnp.maximum(peak_first, peak_second)
    merged_total = total_first * jnp.exp(peak_first - joined) + total_second * jnp.exp(
        peak_second - joined
    )
    return (joined, merged_total)


def shards(
    question_vectors,
    document_vectors,
    positive,
    tokens,
    expert_ids,
    route_weights,
    expert_gate_up,
    expert_down,
):
    row_size = lax.axis_size("row")
    col_size = lax.axis_size("col")
    devices_all = row_size * col_size
    pass_full = gathered_copies(document_vectors, "row", 1)
    query_full = gathered_copies(question_vectors, "col", 1)
    similarity_entries = (
        lax.dot_general(
            query_full, pass_full, (((1,), (1,)), ((), ())), preferred_element_type=jnp.float32
        )
        / sharpness_divisor
    )
    local_peak = jnp.max(similarity_entries, axis=1)
    local_total = jnp.sum(jnp.exp(similarity_entries - local_peak[:, None]), axis=1)
    row_peak, partition_normalizer = combined_all((local_peak, local_total), "col", combine_stats)
    coefficient_entries = jnp.exp(similarity_entries - row_peak[:, None])
    pass_count = pass_full.shape[0]
    columns = lax.axis_index("col") * pass_count + jnp.arange(pass_count, dtype=jnp.int32)
    membership_table = (positive[:, None] == columns[None, :]).astype(jnp.float32)
    similarity_derivative = (
        (coefficient_entries / partition_normalizer[:, None] - membership_table) / sharpness_divisor
    ).astype(jnp.bfloat16)
    tok_count, model_width = tokens.shape
    query_grad = sent_and_summed(
        jnp.dot(similarity_derivative, pass_full, preferred_element_type=jnp.float32).astype(
            jnp.bfloat16
        ),
        "col",
        0,
    )
    passage_term = lax.dot_general(
        similarity_derivative,
        query_full,
        (((0,), (0,)), ((), ())),
        preferred_element_type=jnp.float32,
    )
    passage_grad = sent_and_summed(passage_term.astype(jnp.bfloat16), "row", 1)
    cotangent = jnp.repeat(query_grad / SEQ_LEN, SEQ_LEN, axis=0).astype(jnp.bfloat16)
    top_count = expert_ids.shape[1]
    experts_all = devices_all * expert_gate_up.shape[0]
    capacity = max(2, (tok_count * top_count * 9 + 8 * experts_all - 1) // (8 * experts_all))
    flat_ids = expert_ids.reshape(-1)
    expert_hit = (flat_ids[:, None] == jnp.arange(experts_all, dtype=jnp.int32)[None, :]).astype(
        jnp.int32
    )
    before = jnp.cumsum(expert_hit, axis=0) - expert_hit
    slot_number = jnp.sum(before * expert_hit, axis=1)
    slot_index = flat_ids * capacity + slot_number
    token_row = jnp.arange(tok_count * top_count, dtype=jnp.int32) // top_count
    routed_input = (
        jnp.zeros((experts_all * capacity, model_width), jnp.bfloat16)
        .at[slot_index]
        .set(tokens[token_row])
    )
    pair_grads = (
        route_weights.reshape(-1)[:, None] * cotangent[token_row].astype(jnp.float32)
    ).astype(jnp.bfloat16)
    routed_grad = (
        jnp.zeros((experts_all * capacity, model_width), jnp.bfloat16)
        .at[slot_index]
        .set(pair_grads)
    )
    flat_shape = (experts_all, capacity, model_width)
    got_input, got_grad = (
        lax.all_to_all(
            routed_input.reshape(flat_shape),
            ("row", "col"),
            split_axis=0,
            concat_axis=0,
            tiled=True,
        ),
        lax.all_to_all(
            routed_grad.reshape(flat_shape), ("row", "col"), split_axis=0, concat_axis=0, tiled=True
        ),
    )
    slot_inputs = got_input.reshape(-1, model_width)
    slot_grads = got_grad.reshape(-1, model_width)
    input_grad, gate_up_grad, down_grad = expert_backward(
        slot_inputs, slot_grads, expert_gate_up[0], expert_down[0]
    )
    returned = lax.all_to_all(
        input_grad.reshape((experts_all, capacity, model_width)),
        ("row", "col"),
        split_axis=0,
        concat_axis=0,
        tiled=True,
    )
    returned = returned.reshape(experts_all * capacity, model_width)
    summed = jnp.sum(
        returned[slot_index].astype(jnp.float32).reshape(tok_count, top_count, model_width), axis=1
    )
    token_grad = (cotangent.astype(jnp.float32) + summed).astype(jnp.bfloat16)
    return (passage_grad, token_grad, gate_up_grad[None], down_grad[None])


def solution(mesh):
    in_specs = (
        P("row", "col"),
        P("col", "row"),
        P("row"),
        P(("row", "col"), None),
        P(("row", "col"), None),
        P(("row", "col"), None),
        P(("row", "col"), None, None),
        P(("row", "col"), None, None),
    )
    out_specs = (
        P("col", "row"),
        P(("row", "col"), None),
        P(("row", "col"), None, None),
        P(("row", "col"), None, None),
    )
    return jax.shard_map(shards, mesh=mesh, in_specs=in_specs, out_specs=out_specs, check_vma=False)
```

profile of v0, /device:TPU:37, one launch (start us, length us, event | category | flops | bytes accessed | tf_op | source)
XLA Modules:
  0.0 524.7 jit_solution(16506023052876675139)
XLA Ops:
  8.7 8.6 %all-to-all-done.1 = bf16[8,128,256]{1,2,0:T(8,128)(2,1)} async-done(((bf16[8,128,256]{1,2,0:T(8,128)(2,1)}), bf16[8,128,256]{1,2,0:T(8,128)(2,1)}, u32[]{:S(2)}, u32[]{:S(2)}) %all-to-all-start.1) | async-done | bytes 524320 | tf_op jit(solution)/shard_map/all_to_all | solution.py:14
  18.4 7.3 %all-to-all-start = ((bf16[16,256,128]{1,2,0:T(8,128)(2,1)}), bf16[16,256,128]{1,2,0:T(8,128)(2,1)}, u32[]{:S(2)}, u32[]{:S(2)}) async-start(bf16[16,256,128]{1,2,0:T(8,128)(2,1)} %broadcast_in_dim.12), calls=%async_computation | async-start | bytes 2097152 | tf_op jit(solution)/shard_map/all_to_all | solution.py:14
  27.0 13.1 %all-to-all-done = bf16[16,256,128]{1,2,0:T(8,128)(2,1)} async-done(((bf16[16,256,128]{1,2,0:T(8,128)(2,1)}), bf16[16,256,128]{1,2,0:T(8,128)(2,1)}, u32[]{:S(2)}, u32[]{:S(2)}) %all-to-all-start) | async-done | bytes 1048608 | tf_op jit(solution)/shard_map/all_to_all | solution.py:14
  54.9 7.6 %all-to-all-start.4 = ((bf16[16,16,2048]{2,1,0:T(8,128)(2,1)}), bf16[16,16,2048]{2,1,0:T(8,128)(2,1)}, u32[]{:S(2)}, u32[]{:S(2)}) async-start(bf16[16,16,2048]{2,1,0:T(8,128)(2,1)} %bitcast.65), calls=%async_computation.4 | async-start | bytes 2097152 | tf_op jit(solution)/shard_map/all_to_all | solution.py:68
  65.1 22.9 %scatter_custom_fusion.1 = bf16[1152,2048]{1,0:T(8,128)(2,1)} fusion(s32[1024]{0:T(1024)S(1)} %bitcast.69, bf16[128,2048]{1,0:T(8,128)(2,1)} %param.11, s32[1024]{0:T(1024)S(1)} %broadcast_clamp_fusion.1, bf16[]{:T(256)} %constant.41.clone.1), kind=kCustom, calls=%fused_computation.14 | custom fusion | bytes 4719104 | tf_op jit(solution)/shard_map/scatter | solution.py:170
  88.0 8.1 %reshape.168 = bf16[128,9,2048]{2,1,0:T(8,128)(2,1)} reshape(bf16[1152,2048]{1,0:T(8,128)(2,1)} %scatter_custom_fusion.1) | data formatting | bytes 9437184 | tf_op jit(solution)/shard_map/reshape | solution.py:183
  96.0 11.5 %all-to-all-start.6 = ((bf16[128,9,2048]{2,1,0:T(8,128)(2,1)}), bf16[128,9,2048]{2,1,0:T(8,128)(2,1)}, u32[]{:S(2)}, u32[]{:S(2)}) async-start(bf16[128,9,2048]{2,1,0:T(8,128)(2,1)} %reshape.168), calls=%async_computation.6 | async-start | bytes 16777216 | tf_op jit(solution)/shard_map/all_to_all | solution.py:182
  110.0 23.5 %scatter_custom_fusion = bf16[1152,2048]{1,0:T(8,128)(2,1)} fusion(s32[1024]{0:T(1024)S(1)} %bitcast.70, f32[1024]{0:T(1024)S(1)} %mul.90, bf16[]{:T(256)} %constant.41.clone.1, bf16[128,2048]{1,0:T(8,128)(2,1)} %broadcast_bitcast_fusion, s32[1024]{0:T(1024)S(1)} %broadcast_clamp_fusion.1), kind=kCustom, calls=%fused_computation.13 | custom fusion | flops 6291456 | bytes 5251074 | tf_op jit(solution)/shard_map/scatter | solution.py:178
  133.4 8.1 %reshape.166 = bf16[128,9,2048]{2,1,0:T(8,128)(2,1)} reshape(bf16[1152,2048]{1,0:T(8,128)(2,1)} %scatter_custom_fusion) | data formatting | bytes 9437184 | tf_op jit(solution)/shard_map/reshape | solution.py:190
  141.5 76.6 %all-to-all-done.6 = bf16[128,9,2048]{2,1,0:T(8,128)(2,1)} async-done(((bf16[128,9,2048]{2,1,0:T(8,128)(2,1)}), bf16[128,9,2048]{2,1,0:T(8,128)(2,1)}, u32[]{:S(2)}, u32[]{:S(2)}) %all-to-all-start.6) | async-done | bytes 4718624 | tf_op jit(solution)/shard_map/all_to_all | solution.py:182
  218.2 7.3 %all-to-all-start.5 = ((bf16[128,9,2048]{2,1,0:T(8,128)(2,1)}), bf16[128,9,2048]{2,1,0:T(8,128)(2,1)}, u32[]{:S(2)}, u32[]{:S(2)}) async-start(bf16[128,9,2048]{2,1,0:T(8,128)(2,1)} %reshape.166), calls=%async_computation.5 | async-start | bytes 16777216 | tf_op jit(solution)/shard_map/all_to_all | solution.py:189
  228.0 8.5 %reshape.169 = bf16[1152,2048]{1,0:T(8,128)(2,1)} reshape(bf16[128,9,2048]{2,1,0:T(8,128)(2,1)} %all-to-all-done.6) | data formatting | bytes 9437184 | tf_op jit(solution)/shard_map/reshape | solution.py:193
  236.5 13.7 %fusion.2 = f32[1152,1536]{0,1:T(8,128)} fusion(bf16[1152,2048]{1,0:T(8,128)(2,1)} %reshape.169, bf16[1,2048,1536]{2,1,0:T(8,128)(2,1)} %param.14), kind=kOutput, calls=%fused_computation.11 | convolution fusion | flops 7247757312 | bytes 18087936 | tf_op jit(solution)/shard_map/dot_general | solution.py:73
  250.2 85.9 %all-to-all-done.5 = bf16[128,9,2048]{2,1,0:T(8,128)(2,1)} async-done(((bf16[128,9,2048]{2,1,0:T(8,128)(2,1)}), bf16[128,9,2048]{2,1,0:T(8,128)(2,1)}, u32[]{:S(2)}, u32[]{:S(2)}) %all-to-all-start.5) | async-done | bytes 4718624 | tf_op jit(solution)/shard_map/all_to_all | solution.py:189
  340.2 8.5 %reshape.167 = bf16[1152,2048]{1,0:T(8,128)(2,1)} reshape(bf16[128,9,2048]{2,1,0:T(8,128)(2,1)} %all-to-all-done.5) | data formatting | bytes 9437184 | tf_op jit(solution)/shard_map/reshape | solution.py:194
  348.7 8.6 %multiply_convert_fusion.4 = (bf16[1152,768]{0,1:T(8,128)(2,1)S(1)}, bf16[1152,768]{0,1:T(8,128)(2,1)S(1)}) fusion(f32[1152,1536]{0,1:T(8,128)} %fusion.2, bf16[1152,2048]{1,0:T(8,128)(2,1)} %reshape.167, bf16[1,768,2048]{2,1,0:T(8,128)(2,1)S(1)} %copy-done), kind=kOutput, calls=%fused_computation.20 | convolution fusion | flops 3635380224 | bytes 18481152 | tf_op jit(solution)/shard_map/dot_general | solution.py:83
  359.1 12.1 %convolution_convert_fusion.1 = bf16[1152,2048]{1,0:T(8,128)(2,1)} fusion(bf16[1,2048,1536]{2,1,0:T(8,128)(2,1)} %param.14, bf16[1152,768]{0,1:T(8,128)(2,1)S(1)} %get-tuple-element.13, bf16[1152,768]{0,1:T(8,128)(2,1)S(1)} %get-tuple-element.12), kind=kOutput, calls=%fused_computation.8 | convolution fusion | flops 7257194496 | bytes 14548992 | tf_op jit(solution)/shard_map/dot_general | solution.py:93
  371.2 8.1 %reshape.170 = bf16[128,9,2048]{2,1,0:T(8,128)(2,1)} reshape(bf16[1152,2048]{1,0:T(8,128)(2,1)} %convolution_convert_fusion.1) | data formatting | bytes 9437184 | tf_op jit(solution)/shard_map/reshape | solution.py:199
  379.3 8.0 %all-to-all-start.7 = ((bf16[128,9,2048]{2,1,0:T(8,128)(2,1)}), bf16[128,9,2048]{2,1,0:T(8,128)(2,1)}, u32[]{:S(2)}, u32[]{:S(2)}) async-start(bf16[128,9,2048]{2,1,0:T(8,128)(2,1)} %reshape.170), calls=%async_computation.7 | async-start | bytes 16777216 | tf_op jit(solution)/shard_map/all_to_all | solution.py:198
  389.1 10.5 %fusion.11 = bf16[1,768,2048]{2,1,0:T(8,128)(2,1)} fusion(bf16[1152,2048]{1,0:T(8,128)(2,1)} %reshape.167, f32[1152,1536]{0,1:T(8,128)} %fusion.2), kind=kOutput, calls=%fused_computation.26 | convolution fusion | flops 3630759936 | bytes 14942208 | tf_op jit(solution)/shard_map/dot_general | solution.py:80
  399.6 13.9 %fusion = bf16[1,2048,1536]{2,1,0:T(8,128)(2,1)} fusion(bf16[1152,2048]{1,0:T(8,128)(2,1)} %reshape.169, bf16[1152,768]{0,1:T(8,128)(2,1)S(1)} %copy-done.8, bf16[1152,768]{0,1:T(8,128)(2,1)S(1)} %copy-done.6), kind=kOutput, calls=%fused_computation.9 | convolution fusion | flops 7257980928 | bytes 14548992 | tf_op jit(solution)/shard_map/dot_general | solution.py:90
  413.4 84.5 %all-to-all-done.7 = bf16[128,9,2048]{2,1,0:T(8,128)(2,1)} async-done(((bf16[128,9,2048]{2,1,0:T(8,128)(2,1)}), bf16[128,9,2048]{2,1,0:T(8,128)(2,1)}, u32[]{:S(2)}, u32[]{:S(2)}) %all-to-all-start.7) | async-done | bytes 4718624 | tf_op jit(solution)/shard_map/all_to_all | solution.py:198
  498.0 8.4 %reshape.171 = bf16[1152,2048]{1,0:T(8,128)(2,1)} reshape(bf16[128,9,2048]{2,1,0:T(8,128)(2,1)} %all-to-all-done.7) | data formatting | bytes 9437184 | tf_op jit(solution)/shard_map/reshape | solution.py:205
  506.4 11.9 %gather_fusion = bf16[1024,2048]{1,0:T(8,128)(2,1)} fusion(bf16[1152,2048]{1,0:T(8,128)(2,1)} %reshape.171, s32[1024]{0:T(1024)S(1)} %broadcast_clamp_fusion), kind=kCustom, calls=%fused_computation.2 | custom fusion | bytes 8392704 | tf_op jit(solution)/shard_map/gather | solution.py:207
  (80 shorter events, 46.4 us)
Async XLA Ops:
  0.6 348.1 %copy-start = (bf16[1,768,2048]{2,1,0:T(8,128)(2,1)S(1)}, bf16[1,768,2048]{2,1,0:T(8,128)(2,1)}, u32[]{:S(2)}) copy-start(bf16[1,768,2048]{2,1,0:T(8,128)(2,1)} %param.15) | copy-start | bytes 9437188
  0.6 25.1 %copy-start.2 = (s32[128,8]{0,1:T(8,128)S(1)}, s32[128,8]{0,1:T(8,128)}, u32[]{:S(2)}) copy-start(s32[128,8]{0,1:T(8,128)} %param.12) | copy-start | bytes 12292
  0.7 51.7 %copy-start.4 = (s32[256]{0:T(256)S(1)}, s32[256]{0:T(256)}, u32[]{:S(2)}) copy-start(s32[256]{0:T(256)} %param.10) | copy-start | bytes 3076
  2.6 14.7 %all-to-all-start.1 = ((bf16[8,128,256]{1,2,0:T(8,128)(2,1)}), bf16[8,128,256]{1,2,0:T(8,128)(2,1)}, u32[]{:S(2)}, u32[]{:S(2)}) async-start(bf16[8,128,256]{1,2,0:T(8,128)(2,1)} %broadcast_in_dim.13), calls=%async_computation.1 | async-start | bytes 1048576 | tf_op jit(solution)/shard_map/all_to_all | solution.py:14
  18.4 21.7 %all-to-all-start = ((bf16[16,256,128]{1,2,0:T(8,128)(2,1)}), bf16[16,256,128]{1,2,0:T(8,128)(2,1)}, u32[]{:S(2)}, u32[]{:S(2)}) async-start(bf16[16,256,128]{1,2,0:T(8,128)(2,1)} %broadcast_in_dim.12), calls=%async_computation | async-start | bytes 2097152 | tf_op jit(solution)/shard_map/all_to_all | solution.py:14
  42.5 9.5 %all-to-all-start.2 = ((f32[16,2,256]{2,1,0:T(2,128)}), f32[16,2,256]{2,1,0:T(2,128)S(1)}, u32[]{:S(2)}, u32[]{:S(2)}) async-start(f32[16,2,256]{2,1,0:T(2,128)} %broadcast_in_dim.14), calls=%async_computation.2 | async-start | bytes 65536 | tf_op jit(solution)/shard_map/all_to_all | solution.py:14
  54.9 41.1 %all-to-all-start.4 = ((bf16[16,16,2048]{2,1,0:T(8,128)(2,1)}), bf16[16,16,2048]{2,1,0:T(8,128)(2,1)}, u32[]{:S(2)}, u32[]{:S(2)}) async-start(bf16[16,16,2048]{2,1,0:T(8,128)(2,1)} %bitcast.65), calls=%async_computation.4 | async-start | bytes 2097152 | tf_op jit(solution)/shard_map/all_to_all | solution.py:68
  96.0 11.5 %copy-start.3 = (f32[128,8]{0,1:T(8,128)S(1)}, f32[128,8]{0,1:T(8,128)}, u32[]{:S(2)}) copy-start(f32[128,8]{0,1:T(8,128)} %param.13) | copy-start | bytes 12292
  96.0 122.1 %all-to-all-start.6 = ((bf16[128,9,2048]{2,1,0:T(8,128)(2,1)}), bf16[128,9,2048]{2,1,0:T(8,128)(2,1)}, u32[]{:S(2)}, u32[]{:S(2)}) async-start(bf16[128,9,2048]{2,1,0:T(8,128)(2,1)} %reshape.168), calls=%async_computation.6 | async-start | bytes 16777216 | tf_op jit(solution)/shard_map/all_to_all | solution.py:182
  218.2 117.9 %all-to-all-start.5 = ((bf16[128,9,2048]{2,1,0:T(8,128)(2,1)}), bf16[128,9,2048]{2,1,0:T(8,128)(2,1)}, u32[]{:S(2)}, u32[]{:S(2)}) async-start(bf16[128,9,2048]{2,1,0:T(8,128)(2,1)} %reshape.166), calls=%async_computation.5 | async-start | bytes 16777216 | tf_op jit(solution)/shard_map/all_to_all | solution.py:189
  336.1 43.3 %all-to-all-start.3 = ((bf16[8,128,256]{2,1,0:T(8,128)(2,1)}), bf16[8,128,256]{2,1,0:T(8,128)(2,1)}, u32[]{:S(2)}, u32[]{:S(2)}) async-start(bf16[8,128,256]{2,1,0:T(8,128)(2,1)} %bitcast.66), calls=%async_computation.3 | async-start | bytes 1048576 | tf_op jit(solution)/shard_map/all_to_all | solution.py:68
  357.3 1.2 copy-start.5
  357.3 1.8 copy-start.7
  379.3 118.6 %all-to-all-start.7 = ((bf16[128,9,2048]{2,1,0:T(8,128)(2,1)}), bf16[128,9,2048]{2,1,0:T(8,128)(2,1)}, u32[]{:S(2)}, u32[]{:S(2)}) async-start(bf16[128,9,2048]{2,1,0:T(8,128)(2,1)} %reshape.170), calls=%async_computation.7 | async-start | bytes 16777216 | tf_op jit(solution)/shard_map/all_to_all | solution.py:198
  389.1 10.5 %copy-start.6 = (bf16[1152,768]{0,1:T(8,128)(2,1)S(1)}, bf16[1152,768]{0,1:T(8,128)(2,1)}, u32[]{:S(2)}) copy-start(bf16[1152,768]{0,1:T(8,128)(2,1)} %copy-done.5) | copy-start | bytes 5308420
  389.1 10.5 %copy-start.8 = (bf16[1152,768]{0,1:T(8,128)(2,1)S(1)}, bf16[1152,768]{0,1:T(8,128)(2,1)}, u32[]{:S(2)}) copy-start(bf16[1152,768]{0,1:T(8,128)(2,1)} %copy-done.7) | copy-start | bytes 5308420
  506.4 17.9 %copy-start.1 = (bf16[1,768,2048]{2,1,0:T(8,128)(2,1)S(1)}, bf16[1,768,2048]{2,1,0:T(8,128)(2,1)}, u32[]{:S(2)}) copy-start(bf16[1,768,2048]{2,1,0:T(8,128)(2,1)} %param.15) | copy-start | bytes 9437188
where the time goes:
time: 530 us; the launch traced here: 525 us
  waiting for transfers between devices  272 us (51%)
  local copies, waits for them, and re-layouts  94.4 us (18%)
  matrix products  64.7 us (12%)
  starting transfers between devices  56.5 us (11%)
  other arithmetic  35.2 us (7%)
    all_to_all x1, waiting for transfers between devices, shards(): lax.all_to_all(routed_grad.reshape(flat_shape), ('row', 'col'), split_axi...  85.9 us
    all_to_all x1, waiting for transfers between devices, shards(): lax.all_to_all(input_grad.reshape((experts_all, capacity, model_width)),...  84.5 us
    all_to_all x1, waiting for transfers between devices, shards(): lax.all_to_all(routed_input.reshape(flat_shape), ('row', 'col'), split_ax...  76.6 us
    all_to_all x3, waiting for transfers between devices, sent_to_all(): lax.all_to_all(jnp.broadcast_to(value[None], (peers, *value.shape)), axis...  25.4 us
    scatter x1, other arithmetic, shards(): routed_grad = jnp.zeros((experts_all * capacity, model_width), jnp.bfloat...  23.5 us
    scatter x1, local copies, waits for them, and re-layouts, shards(): routed_input = jnp.zeros((experts_all * capacity, model_width), jnp.bfloa...  22.9 us
    all_to_all x3, starting transfers between devices, sent_to_all(): lax.all_to_all(jnp.broadcast_to(value[None], (peers, *value.shape)), axis...  18.2 us
    dot_general x1, matrix products, expert_backward(): lax.dot_general(slot_inputs, pre_grad, (((0,), (0,)), ((), ())), preferre...  13.9 us
  transfers between devices with their start and end apart: 8, of which 6 were waited for; matrix products, arithmetic and copies ran while one was open for 30% of the time, Pallas kernels for 0%

commit v1 on v0

v1 whole, which is shorter than its diff:
```python
import functools
import jax
import jax.numpy as jnp
from jax import lax
from jax.experimental import pallas as pl
from jax.experimental.pallas import tpu as pltpu
from jax.sharding import PartitionSpec as P

SEQ_LEN = 8
SHARPNESS = 0.02
MAIN = 8
LANES = 128
B16 = jnp.bfloat16
F32 = jnp.float32
VMEM_LIMIT = 56 * 1024 * 1024


def iota(shape, dim):
    return lax.broadcasted_iota(jnp.int32, shape, dim)


def params():
    return pltpu.CompilerParams(vmem_limit_bytes=VMEM_LIMIT)


def whole(shape):
    zeros = (0,) * len(shape)
    return pl.BlockSpec(shape, lambda *_: zeros, pipeline_mode=pl.Buffered(1))


def dot(a, b, dims=((1,), (0,))):
    return lax.dot_general(a, b, (dims, ((), ())), preferred_element_type=F32)


def one_hot(mask):
    return jnp.where(mask, 1.0, 0.0).astype(B16)


def slot_keys(ids_t, experts):
    toks = ids_t.shape[1]
    expert = iota((experts, toks), 0)
    hit = jnp.zeros((experts, toks), F32)
    for k in range(ids_t.shape[0]):
        hit += jnp.where(ids_t[k : k + 1, :] == expert, 1.0, 0.0)
    earlier = one_hot(iota((toks, toks), 0) < iota((toks, toks), 1))
    rank = dot(hit.astype(B16), earlier)
    return jnp.where(hit > 0.0, rank, -1.0).astype(jnp.int32)


def per_slot(value):
    experts, toks = value.shape
    return jnp.broadcast_to(value[:, None, :], (experts, MAIN, toks)).reshape(
        experts * MAIN, toks
    )


def send_tokens_kernel(ids_ref, tok_ref, out_ref, key_ref):
    j = pl.program_id(0)
    tiles = pl.num_programs(0) - 1
    width = out_ref.shape[1]
    experts = out_ref.shape[0] // MAIN

    @pl.when(j == 0)
    def _():
        key_ref[...] = per_slot(slot_keys(ids_ref[...], experts))

    slot = iota(key_ref.shape, 0) % MAIN

    @pl.when(j < tiles)
    def _():
        cols = pl.ds(pl.multiple_of(j * width, width), width)
        out_ref[...] = dot(one_hot(key_ref[...] == slot), tok_ref[:, cols]).astype(B16)

    @pl.when(j == tiles)
    def _():
        ninth = key_ref[...] == MAIN
        total = jnp.zeros(out_ref.shape, F32)
        for i in range(MAIN):
            total += dot(one_hot(ninth & (slot == i)), tok_ref[:, i * width : (i + 1) * width])
        out_ref[...] = total.astype(B16)


def send_tokens(ids_t, tokens, experts):
    toks, depth = tokens.shape
    width = depth // MAIN
    return pl.pallas_call(
        send_tokens_kernel,
        grid=(MAIN + 1,),
        in_specs=[whole(ids_t.shape), whole(tokens.shape)],
        out_specs=pl.BlockSpec((experts * MAIN, width), lambda j: (0, j)),
        out_shape=jax.ShapeDtypeStruct((experts * MAIN, depth + width), B16),
        scratch_shapes=[pltpu.VMEM((experts * MAIN, toks), jnp.int32)],
        compiler_params=params(),
        name="send_tokens",
    )(ids_t, tokens)


def send_grads_kernel(ids_ref, weight_ref, part_ref, out_ref, cot_ref, key_ref, row_ref, rep_ref):
    j = pl.program_id(0)
    tiles = pl.num_programs(0) - 1
    width = out_ref.shape[1]
    experts = out_ref.shape[0] // MAIN
    slots, toks = key_ref.shape

    @pl.when(j == 0)
    def _():
        ids = ids_ref[...]
        key = per_slot(slot_keys(ids, experts))
        key_ref[...] = key
        expert = iota((experts, toks), 0)
        weight = jnp.zeros((experts, toks), F32)
        for k in range(ids.shape[0]):
            weight += jnp.where(ids[k : k + 1, :] == expert, weight_ref[k : k + 1, :], 0.0)
        weight = per_slot(weight)
        slot = iota((slots, toks), 0) % MAIN
        main = jnp.sum(jnp.where(key == slot, weight, 0.0), axis=1, keepdims=True)
        ninth = jnp.sum(jnp.where(key == MAIN, weight, 0.0), axis=1, keepdims=True)
        row_ref[...] = jnp.where(iota(row_ref.shape, 1) == 0, main, ninth)
        total = part_ref[0].astype(F32)
        for c in range(1, part_ref.shape[0]):
            total += part_ref[c].astype(F32)
        cot = (total / SEQ_LEN).astype(B16)
        cot_ref[...] = cot
        spread = one_hot(iota((toks, cot.shape[0]), 0) // SEQ_LEN == iota((toks, cot.shape[0]), 1))
        rep_ref[...] = dot(spread, cot).astype(B16)

    slot = iota((slots, toks), 0) % MAIN

    @pl.when(j < tiles)
    def _():
        cols = pl.ds(pl.multiple_of(j * width, width), width)
        rows = dot(one_hot(key_ref[...] == slot), rep_ref[:, cols])
        out_ref[...] = (rows * row_ref[:, 0:1]).astype(B16)

    @pl.when(j == tiles)
    def _():
        ninth = key_ref[...] == MAIN
        total = jnp.zeros(out_ref.shape, F32)
        for i in range(MAIN):
            total += dot(one_hot(ninth & (slot == i)), rep_ref[:, i * width : (i + 1) * width])
        out_ref[...] = (total * row_ref[:, 1:2]).astype(B16)


def send_grads(ids_t, weights_t, parts, experts):
    toks = ids_t.shape[1]
    _, queries, depth = parts.shape
    width = depth // MAIN
    return pl.pallas_call(
        send_grads_kernel,
        grid=(MAIN + 1,),
        in_specs=[whole(ids_t.shape), whole(weights_t.shape), whole(parts.shape)],
        out_specs=[
            pl.BlockSpec((experts * MAIN, width), lambda j: (0, j)),
            pl.BlockSpec((queries, depth), lambda j: (0, 0)),
        ],
        out_shape=[
            jax.ShapeDtypeStruct((experts * MAIN, depth + width), B16),
            jax.ShapeDtypeStruct((queries, depth), B16),
        ],
        scratch_shapes=[
            pltpu.VMEM((experts * MAIN, toks), jnp.int32),
            pltpu.VMEM((experts * MAIN, 128), F32),
            pltpu.VMEM((toks, depth), B16),
        ],
        compiler_params=params(),
        name="send_grads",
    )(ids_t, weights_t, parts)


def unfold(fold, fold_ref, out_ref):
    sources, depth = out_ref.shape
    width = depth // MAIN
    for half in range(width // LANES):
        at = slice(half * LANES, (half + 1) * LANES)
        fold_ref[half] = fold[:, at].astype(F32)
        for i in range(MAIN):
            piece = fold_ref[half, pl.ds(i, sources, stride=MAIN), :]
            start = i * width + half * LANES
            out_ref[:, start : start + LANES] = piece.astype(B16)


def forward_kernel(x_ref, gate_ref, up_ref, hid_ref, cg_ref, cu_ref, x9_ref, fold_ref):
    j = pl.program_id(0)
    depth = gate_ref.shape[0]
    rows = x_ref.shape[0]

    @pl.when(j == 0)
    def _():
        unfold(x_ref[:, depth:], fold_ref, x9_ref)

    def finish(at, gate, up):
        sig = 1.0 / (1.0 + jnp.exp(-gate))
        act = gate * sig
        hid_ref[at, :] = (act * up).astype(B16)
        cg_ref[at, :] = (up * (sig * (1.0 + gate * (1.0 - sig)))).astype(B16)
        cu_ref[at, :] = act.astype(B16)

    step = rows // 4
    for m in range(4):
        x = x_ref[m * step : (m + 1) * step, :depth]
        finish(slice(m * step, (m + 1) * step), dot(x, gate_ref[...]), dot(x, up_ref[...]))
    x = x9_ref[...]
    finish(slice(rows, hid_ref.shape[0]), dot(x, gate_ref[...]), dot(x, up_ref[...]))


def forward(x, gate_up, hidden):
    rows, _ = x.shape
    depth = gate_up.shape[0]
    sources = rows // MAIN
    tile = 256
    tiles = hidden // tile
    col = lambda j: (0, j)
    part = pl.BlockSpec((rows + sources, tile), col)
    shape = jax.ShapeDtypeStruct((rows + sources, hidden), B16)
    return pl.pallas_call(
        forward_kernel,
        grid=(tiles,),
        in_specs=[
            whole(x.shape),
            pl.BlockSpec((depth, tile), col),
            pl.BlockSpec((depth, tile), lambda j: (0, j + tiles)),
        ],
        out_specs=[part, part, part, pl.BlockSpec((sources, depth), lambda j: (0, 0))],
        out_shape=[shape, shape, shape, jax.ShapeDtypeStruct((sources, depth), B16)],
        scratch_shapes=[pltpu.VMEM((depth // MAIN // LANES, rows, LANES), F32)],
        compiler_params=params(),
        cost_estimate=pl.CostEstimate(
            flops=2 * (rows + sources) * depth * 2 * hidden,
            bytes_accessed=2 * (x.size + gate_up.size + 3 * (rows + sources) * hidden),
            transcendentals=(rows + sources) * hidden,
        ),
        name="expert_forward",
    )(x, gate_up, gate_up)


def backward_kernel(
    first, g_ref, down_ref, cg_ref, cu_ref, w_ref, out_ref, pg_ref, g9_ref, fold_ref
):
    j = pl.program_id(0)
    rows = g_ref.shape[0]
    sources, depth = g9_ref.shape
    width = out_ref.shape[1]
    total = rows + sources
    tile = down_ref.shape[0]
    hidden = pg_ref.shape[1] // 2

    @pl.when(j == 0)
    def _():
        unfold(g_ref[:, depth:], fold_ref, g9_ref)

    @pl.when(j < first)
    def _():
        def finish(at, grad):
            gate_cols = pl.ds(pl.multiple_of(j * tile, tile), tile)
            up_cols = pl.ds(pl.multiple_of(hidden + j * tile, tile), tile)
            pg_ref[at, gate_cols] = (grad * cg_ref[at, :].astype(F32)).astype(B16)
            pg_ref[at, up_cols] = (grad * cu_ref[at, :].astype(F32)).astype(B16)

        step = rows // 4
        for m in range(4):
            at = slice(m * step, (m + 1) * step)
            finish(at, dot(g_ref[at, :depth], down_ref[...], ((1,), (1,))))
        finish(slice(rows, total), dot(g9_ref[...], down_ref[...], ((1,), (1,))))

    @pl.when((j >= first) & (j < first + MAIN))
    def _():
        step = rows // 4
        for m in range(4):
            at = slice(m * step, (m + 1) * step)
            out_ref[at, :] = dot(pg_ref[at, :], w_ref[...], ((1,), (1,))).astype(B16)
        ninth = dot(pg_ref[rows:total, :], w_ref[...], ((1,), (1,)))
        for half in range(width // LANES):
            fold_ref[half, pl.ds(j - first, sources, stride=MAIN), :] = ninth[
                :, half * LANES : (half + 1) * LANES
            ]

    @pl.when(j == first + MAIN)
    def _():
        for half in range(width // LANES):
            out_ref[:, half * LANES : (half + 1) * LANES] = fold_ref[half].astype(B16)


def backward(g, down, cg, cu, gate_up):
    rows, _ = g.shape
    hidden, depth = down.shape
    sources = rows // MAIN
    width = depth // MAIN
    tile = 256
    first = hidden // tile
    head = lambda j: (0, jnp.minimum(j, first - 1))
    part = pl.BlockSpec((rows + sources, tile), head)
    return pl.pallas_call(
        functools.partial(backward_kernel, first),
        grid=(first + MAIN + 1,),
        in_specs=[
            whole(g.shape),
            pl.BlockSpec((tile, depth), lambda j: (jnp.minimum(j, first - 1), 0)),
            part,
            part,
            pl.BlockSpec(
                (width, 2 * hidden), lambda j: (jnp.clip(j - first, 0, MAIN - 1), 0)
            ),
        ],
        out_specs=[
            pl.BlockSpec((rows, width), lambda j: (0, jnp.maximum(j - first, 0))),
            pl.BlockSpec((rows + sources, 2 * hidden), lambda j: (0, 0)),
            pl.BlockSpec((sources, depth), lambda j: (0, 0)),
        ],
        out_shape=[
            jax.ShapeDtypeStruct((rows, depth + width), B16),
            jax.ShapeDtypeStruct((rows + sources, 2 * hidden), B16),
            jax.ShapeDtypeStruct((sources, depth), B16),
        ],
        scratch_shapes=[pltpu.VMEM((width // LANES, rows, LANES), F32)],
        compiler_params=params(),
        cost_estimate=pl.CostEstimate(
            flops=6 * (rows + sources) * depth * hidden,
            bytes_accessed=2 * (2 * g.size + down.size + gate_up.size),
            transcendentals=0,
        ),
        name="expert_backward",
    )(g, down, cg, cu, gate_up)


def weight_grad_kernel(a_ref, a9_ref, b_ref, b9_ref, out_ref):
    rows = b_ref.shape[0]
    width = out_ref.shape[0]
    out_ref[...] = (
        dot(a_ref[:, :width], b_ref[...], ((0,), (0,))) + dot(a9_ref[...], b9_ref[...], ((0,), (0,)))
    ).astype(B16)


def weight_grad(a, a9, b, b9, columns, a9_block, b9_block, name):
    sources = a9.shape[0] if a9_block == 0 else a.shape[0] - 8 * (a.shape[0] // 9)
    rows = sources * MAIN
    width = a9.shape[1]
    tile = 256
    return pl.pallas_call(
        weight_grad_kernel,
        grid=(columns // tile,),
        in_specs=[
            pl.BlockSpec((rows, a.shape[1]), lambda j: (0, 0), pipeline_mode=pl.Buffered(1)),
            pl.BlockSpec(
                (sources, width), lambda j: (a9_block, 0), pipeline_mode=pl.Buffered(1)
            ),
            pl.BlockSpec((rows, tile), lambda j: (0, j)),
            pl.BlockSpec((sources, tile), lambda j: (b9_block, j)),
        ],
        out_specs=pl.BlockSpec((width, tile), lambda j: (0, j)),
        out_shape=jax.ShapeDtypeStruct((width, columns), B16),
        compiler_params=params(),
        cost_estimate=pl.CostEstimate(
            flops=2 * 9 * sources * width * columns,
            bytes_accessed=2 * (9 * sources * (width + columns) + width * columns),
            transcendentals=0,
        ),
        name=name,
    )(a, a9, b, b9)


def combine_kernel(ids_ref, cot_ref, got_ref, fold_ref, out_ref, key_ref):
    j = pl.program_id(0)
    toks, slots = key_ref.shape
    experts = slots // MAIN

    @pl.when(j == 0)
    def _():
        ids = ids_ref[...]
        expert = iota((toks, experts), 1)
        hit = jnp.zeros((toks, experts), F32)
        for k in range(ids.shape[1]):
            hit += jnp.where(ids[:, k : k + 1] == expert, 1.0, 0.0)
        earlier = one_hot(iota((toks, toks), 1) < iota((toks, toks), 0))
        rank = dot(earlier, hit.astype(B16))
        key = jnp.where(hit > 0.0, rank, -1.0).astype(B16)
        spread = one_hot(iota((experts, slots), 0) == iota((experts, slots), 1) // MAIN)
        key_ref[...] = dot(key, spread).astype(jnp.int32)

    key = key_ref[...]
    slot = iota(key.shape, 1) % MAIN
    queries = cot_ref.shape[0]
    spread = one_hot(iota((toks, queries), 0) // SEQ_LEN == iota((toks, queries), 1))
    total = dot(one_hot(key == slot), got_ref[...])
    total += dot(one_hot((key == MAIN) & (slot == j)), fold_ref[...])
    out_ref[...] = (dot(spread, cot_ref[...]) + total).astype(B16)


def combine(ids, cot, got):
    toks = ids.shape[0]
    queries, depth = cot.shape
    rows = got.shape[0]
    width = depth // MAIN
    return pl.pallas_call(
        combine_kernel,
        grid=(MAIN,),
        in_specs=[
            whole(ids.shape),
            pl.BlockSpec((queries, width), lambda j: (0, j)),
            pl.BlockSpec((rows, width), lambda j: (0, j)),
            pl.BlockSpec((rows, width), lambda j: (0, MAIN), pipeline_mode=pl.Buffered(1)),
        ],
        out_specs=pl.BlockSpec((toks, width), lambda j: (0, j)),
        out_shape=jax.ShapeDtypeStruct((toks, depth), B16),
        scratch_shapes=[pltpu.VMEM((toks, rows), jnp.int32)],
        compiler_params=params(),
        name="combine",
    )(ids, cot, got, got)


def sent_to_all(value, axis):
    peers = lax.axis_size(axis)
    return lax.all_to_all(
        jnp.broadcast_to(value[None], (peers, *value.shape)), axis, 0, 0, tiled=True
    )


def gathered_copies(value, axis):
    tiles = jnp.moveaxis(sent_to_all(value, axis), 0, 1)
    return tiles.reshape(tiles.shape[0], -1)


def split_up(value, dim, peers):
    lengths = value.shape
    tiles = value.reshape(*lengths[:dim], peers, lengths[dim] // peers, *lengths[dim + 1 :])
    return jnp.moveaxis(tiles, dim, 0)


def exchanged(block, experts):
    rows, width = block.shape
    got = lax.all_to_all(
        block.reshape(experts, rows // experts, width), ("row", "col"), 0, 0, tiled=True
    )
    return got.reshape(rows, width)


def shards(
    question_vectors,
    document_vectors,
    positive,
    tokens,
    expert_ids,
    route_weights,
    expert_gate_up,
    expert_down,
):
    row_size = lax.axis_size("row")
    col_size = lax.axis_size("col")
    experts = row_size * col_size
    gate_up, down = expert_gate_up[0], expert_down[0]
    hidden = down.shape[0]

    ids_t, weights_t = expert_ids.T, route_weights.T
    tokens_out = send_tokens(ids_t, tokens, experts)

    passages = gathered_copies(document_vectors, "row")
    queries = gathered_copies(question_vectors, "col")
    scores = dot(queries, passages, ((1,), (1,))) / SHARPNESS
    local_peak = jnp.max(scores, axis=1)
    local_total = jnp.sum(jnp.exp(scores - local_peak[:, None]), axis=1)
    stats = sent_to_all(jnp.stack([local_peak, local_total]), "col")
    peak = jnp.max(stats[:, 0], axis=0)
    total = jnp.sum(stats[:, 1] * jnp.exp(stats[:, 0] - peak[None]), axis=0)
    count = passages.shape[0]
    columns = lax.axis_index("col") * count + jnp.arange(count, dtype=jnp.int32)
    chosen = (positive[:, None] == columns[None, :]).astype(F32)
    dscore = ((jnp.exp(scores - peak[:, None]) / total[:, None] - chosen) / SHARPNESS).astype(B16)
    query_part = dot(dscore, passages).astype(B16)
    query_parts = lax.all_to_all(split_up(query_part, 0, col_size), "col", 0, 0, tiled=True)

    slot_inputs = exchanged(tokens_out, experts)
    grads_out, cot = send_grads(ids_t, weights_t, query_parts, experts)
    slot_grads = exchanged(grads_out, experts)

    passage_part = dot(dscore, queries, ((0,), (0,))).astype(B16)
    passage_parts = lax.all_to_all(split_up(passage_part, 1, row_size), "row", 0, 0, tiled=True)
    passage_grad = jnp.sum(passage_parts.astype(F32), axis=0)

    hid, cg, cu, inputs9 = forward(slot_inputs, gate_up, hidden)
    back_out, pre_grad, grads9 = backward(slot_grads, down, cg, cu, gate_up)
    returned = exchanged(back_out, experts)
    down_grad = weight_grad(hid, hid, slot_grads, grads9, down.shape[1], MAIN, 0, "down_grad")
    gate_up_grad = weight_grad(
        slot_inputs, inputs9, pre_grad, pre_grad, 2 * hidden, 0, MAIN, "gate_up_grad"
    )
    token_grad = combine(expert_ids, cot, returned)
    return (passage_grad, token_grad, gate_up_grad[None], down_grad[None])


def solution(mesh):
    in_specs = (
        P("row", "col"),
        P("col", "row"),
        P("row"),
        P(("row", "col"), None),
        P(("row", "col"), None),
        P(("row", "col"), None),
        P(("row", "col"), None, None),
        P(("row", "col"), None, None),
    )
    out_specs = (
        P("col", "row"),
        P(("row", "col"), None),
        P(("row", "col"), None, None),
        P(("row", "col"), None, None),
    )
    return jax.shard_map(shards, mesh=mesh, in_specs=in_specs, out_specs=out_specs, check_vma=False)
```

time: 530 us -> 302 us (0.57)
  waiting for transfers between devices: 272 us -> 149 us
  local copies, waits for them, and re-layouts: 94.4 us -> 6.99 us
  Pallas kernels: 0 us -> 81.6 us
  matrix products: 64.7 us -> 2.34 us
  other arithmetic: 35.2 us -> 0.86 us
    all_to_all x5, waiting for transfers between devices: 247 us -> 122 us  [the longest x3 119 us: exchanged(): lax.all_to_all(block.reshape(experts, rows // experts, width), ('row', 'c...]
    pallas_call x0 -> x7, Pallas kernels: none -> 81.6 us  [the longest x2 22.9 us: weight_grad(): pl.pallas_call(weight_grad_kernel, grid=(columns // tile,), in_specs=[pl....]
    dot_general x8 -> x3, matrix products: 64.7 us -> 2.34 us  [dot(): return lax.dot_general(a, b, (dims, ((), ())), preferred_element_type=F32)]
    reshape x7 -> x0, local copies, waits for them, and re-layouts: 49.7 us -> none  [the longest x1 8.53 us: shards(): slot_grads = got_grad.reshape(-1, model_width)]
    scatter x1 -> x0, other arithmetic: 23.5 us -> none  [shards(): routed_grad = jnp.zeros((experts_all * capacity, model_width), jnp.bfloat...]
    scatter x1 -> x0, local copies, waits for them, and re-layouts: 22.9 us -> none  [shards(): routed_input = jnp.zeros((experts_all * capacity, model_width), jnp.bfloa...]
    gather x1 -> x0, local copies, waits for them, and re-layouts: 11.9 us -> none  [shards(): returned[slot_index].astype(jnp.float32)]
    reduce_sum x5 -> x3, other arithmetic: 8.62 us -> 0.8 us  [the longest x1 0.72 us: shards(): passage_grad = jnp.sum(passage_parts.astype(F32), axis=0)]
  transfers between devices with their start and end apart: 8 -> 8, of which waited for: 6 -> 7; matrix products, arithmetic and copies ran while one was open for 30% -> 1% of each run, Pallas kernels for 0% -> 25%
where the time goes in v1:
time: 302 us; the launch traced here: 298 us
  waiting for transfers between devices  149 us (49%)
  Pallas kernels  81.6 us (27%)
  starting transfers between devices  56.7 us (19%)
  local copies, waits for them, and re-layouts  6.99 us (2%)
    all_to_all x3, waiting for transfers between devices, exchanged(): lax.all_to_all(block.reshape(experts, rows // experts, width), ('row', 'c...  119 us
    all_to_all x3, starting transfers between devices, exchanged(): lax.all_to_all(block.reshape(experts, rows // experts, width), ('row', 'c...  28.4 us
    all_to_all x3, waiting for transfers between devices, sent_to_all(): lax.all_to_all(jnp.broadcast_to(value[None], (peers, *value.shape)), axis...  26.5 us
    pallas_call x2, Pallas kernels, weight_grad(): pl.pallas_call(weight_grad_kernel, grid=(columns // tile,), in_specs=[pl....  22.9 us
    pallas_call x1, Pallas kernels, backward(): pl.pallas_call(functools.partial(backward_kernel, first), grid=(first + M...  21.2 us
    all_to_all x3, starting transfers between devices, sent_to_all(): lax.all_to_all(jnp.broadcast_to(value[None], (peers, *value.shape)), axis...  18.2 us
    pallas_call x1, Pallas kernels, forward(): pl.pallas_call(forward_kernel, grid=(tiles,), in_specs=[whole(x.shape), p...  12.8 us
    pallas_call x1, Pallas kernels, send_grads(): pl.pallas_call(send_grads_kernel, grid=(MAIN + 1,), in_specs=[whole(ids_t...  8.65 us
  transfers between devices with their start and end apart: 8, of which 7 were waited for; matrix products, arithmetic and copies ran while one was open for 1% of the time, Pallas kernels for 25%

profile of v1, /device:TPU:37, one launch (start us, length us, event | category | flops | bytes accessed | tf_op | source)
XLA Modules:
  0.0 298.0 jit_solution(2335414981230902136)
XLA Ops:
  2.5 5.1 %all-to-all-start.1 = ((bf16[8,128,256]{1,2,0:T(8,128)(2,1)}), bf16[8,128,256]{1,2,0:T(8,128)(2,1)S(1)}, u32[]{:S(2)}, u32[]{:S(2)}) async-start(bf16[8,128,256]{1,2,0:T(8,128)(2,1)} %broadcast_in_dim.11), calls=%async_computation.1 | async-start | bytes 1048576 | tf_op jit(solution)/shard_map/all_to_all | solution.py:412
  8.6 8.5 %all-to-all-done.1 = bf16[8,128,256]{1,2,0:T(8,128)(2,1)S(1)} async-done(((bf16[8,128,256]{1,2,0:T(8,128)(2,1)}), bf16[8,128,256]{1,2,0:T(8,128)(2,1)S(1)}, u32[]{:S(2)}, u32[]{:S(2)}) %all-to-all-start.1) | async-done | bytes 524320 | tf_op jit(solution)/shard_map/all_to_all | solution.py:412
  17.1 1.1 broadcast_in_dim.10
  18.2 7.3 %all-to-all-start = ((bf16[16,256,128]{1,2,0:T(8,128)(2,1)}), bf16[16,256,128]{1,2,0:T(8,128)(2,1)S(1)}, u32[]{:S(2)}, u32[]{:S(2)}) async-start(bf16[16,256,128]{1,2,0:T(8,128)(2,1)} %broadcast_in_dim.10), calls=%async_computation | async-start | bytes 2097152 | tf_op jit(solution)/shard_map/all_to_all | solution.py:412
  25.4 14.3 %all-to-all-done = bf16[16,256,128]{1,2,0:T(8,128)(2,1)S(1)} async-done(((bf16[16,256,128]{1,2,0:T(8,128)(2,1)}), bf16[16,256,128]{1,2,0:T(8,128)(2,1)S(1)}, u32[]{:S(2)}, u32[]{:S(2)}) %all-to-all-start) | async-done | bytes 1048608 | tf_op jit(solution)/shard_map/all_to_all | solution.py:412
  40.8 5.8 %all-to-all-start.2 = ((f32[16,2,256]{2,1,0:T(2,128)}), f32[16,2,256]{2,1,0:T(2,128)S(1)}, u32[]{:S(2)}, u32[]{:S(2)}) async-start(f32[16,2,256]{2,1,0:T(2,128)} %broadcast_in_dim.12), calls=%async_computation.2 | async-start | bytes 65536 | tf_op jit(solution)/shard_map/all_to_all | solution.py:412
  46.5 3.7 %all-to-all-done.2 = f32[16,2,256]{2,1,0:T(2,128)S(1)} async-done(((f32[16,2,256]{2,1,0:T(2,128)}), f32[16,2,256]{2,1,0:T(2,128)S(1)}, u32[]{:S(2)}, u32[]{:S(2)}) %all-to-all-start.2) | async-done | bytes 32800 | tf_op jit(solution)/shard_map/all_to_all | solution.py:412
  50.3 1.5 convolution_convert_fusion
  51.8 6.3 %all-to-all-start.4 = ((bf16[16,16,2048]{2,1,0:T(8,128)(2,1)}), bf16[16,16,2048]{2,1,0:T(8,128)(2,1)S(1)}, u32[]{:S(2)}, u32[]{:S(2)}) async-start(bf16[16,16,2048]{2,1,0:T(8,128)(2,1)} %bitcast.11), calls=%async_computation.4 | async-start | bytes 2097152 | tf_op jit(solution)/shard_map/all_to_all | solution.py:468
  58.1 8.2 %send_tokens.1 = bf16[1024,2304]{1,0:T(8,128)(2,1)} custom-call(s32[8,128]{1,0:T(8,128)} %bitcast.52, bf16[128,2048]{1,0:T(8,128)(2,1)} %tok_ref.1), custom_call_target="tpu_custom_call" | custom-call | tf_op jit(solution)/shard_map/send_tokens/pallas_call | solution.py:86
  66.4 3.3 %all-to-all-done.4.part_ref = bf16[16,16,2048]{2,1,0:T(8,128)(2,1)S(1)} async-done(((bf16[16,16,2048]{2,1,0:T(8,128)(2,1)}), bf16[16,16,2048]{2,1,0:T(8,128)(2,1)S(1)}, u32[]{:S(2)}, u32[]{:S(2)}) %all-to-all-start.4) | async-done | bytes 1048608 | tf_op jit(solution)/shard_map/all_to_all | solution.py:468
  70.6 11.9 %all-to-all-start.6 = ((bf16[128,8,2304]{2,1,0:T(8,128)(2,1)}), bf16[128,8,2304]{2,1,0:T(8,128)(2,1)}, u32[]{:S(2)}, u32[]{:S(2)}) async-start(bf16[128,8,2304]{2,1,0:T(8,128)(2,1)} %bitcast.44), calls=%async_computation.6 | async-start | bytes 9437184 | tf_op jit(solution)/shard_map/all_to_all | solution.py:430
  82.5 8.6 %send_grads.1 = (bf16[1024,2304]{1,0:T(8,128)(2,1)}, bf16[16,2048]{1,0:T(8,128)(2,1)}) custom-call(s32[8,128]{1,0:T(8,128)} %bitcast.53, f32[8,128]{1,0:T(8,128)} %bitcast.55, bf16[16,16,2048]{2,1,0:T(8,128)(2,1)} %copy-done), custom_call_target="tpu_custom_call" | custom-call | tf_op jit(solution)/shard_map/send_grads/pallas_call | solution.py:148
  91.2 46.7 %all-to-all-done.6 = bf16[128,8,2304]{2,1,0:T(8,128)(2,1)} async-done(((bf16[128,8,2304]{2,1,0:T(8,128)(2,1)}), bf16[128,8,2304]{2,1,0:T(8,128)(2,1)}, u32[]{:S(2)}, u32[]{:S(2)}) %all-to-all-start.6) | async-done | bytes 4718624 | tf_op jit(solution)/shard_map/all_to_all | solution.py:430
  137.9 7.3 %all-to-all-start.5 = ((bf16[128,8,2304]{2,1,0:T(8,128)(2,1)}), bf16[128,8,2304]{2,1,0:T(8,128)(2,1)}, u32[]{:S(2)}, u32[]{:S(2)}) async-start(bf16[128,8,2304]{2,1,0:T(8,128)(2,1)} %bitcast.47), calls=%async_computation.5 | async-start | bytes 9437184 | tf_op jit(solution)/shard_map/all_to_all | solution.py:430
  146.5 12.8 %expert_forward.1 = (bf16[1152,768]{1,0:T(8,128)(2,1)}, bf16[1152,768]{1,0:T(8,128)(2,1)}, bf16[1152,768]{1,0:T(8,128)(2,1)}, bf16[128,2048]{1,0:T(8,128)(2,1)}) custom-call(bf16[1024,2304]{1,0:T(8,128)(2,1)} %bitcast.16.x_ref.a_ref, bf16[2048,1536]{1,0:T(8,128)(2,1)} %bitcast.57, bf16[2048,1536]{1,0:T(8,128)(2,1)} %bitcast.58), custom_call_target="tpu_custom_call" | custom-call | flops 7247757312 | bytes 16318464 | tf_op jit(solution)/shard_map/expert_forward/pallas_call | solution.py:215
  159.3 41.3 %all-to-all-done.5 = bf16[128,8,2304]{2,1,0:T(8,128)(2,1)} async-done(((bf16[128,8,2304]{2,1,0:T(8,128)(2,1)}), bf16[128,8,2304]{2,1,0:T(8,128)(2,1)}, u32[]{:S(2)}, u32[]{:S(2)}) %all-to-all-start.5) | async-done | bytes 4718624 | tf_op jit(solution)/shard_map/all_to_all | solution.py:430
  200.6 3.9 %all-to-all-start.3 = ((bf16[8,128,256]{2,1,0:T(8,128)(2,1)}), bf16[8,128,256]{2,1,0:T(8,128)(2,1)S(1)}, u32[]{:S(2)}, u32[]{:S(2)}) async-start(bf16[8,128,256]{2,1,0:T(8,128)(2,1)} %bitcast.43), calls=%async_computation.3 | async-start | bytes 1048576 | tf_op jit(solution)/shard_map/all_to_all | solution.py:475
  204.5 21.2 %expert_backward.1 = (bf16[1024,2304]{1,0:T(8,128)(2,1)}, bf16[1152,1536]{1,0:T(8,128)(2,1)}, bf16[128,2048]{1,0:T(8,128)(2,1)}) custom-call(bf16[1024,2304]{1,0:T(8,128)(2,1)} %bitcast.13.g_ref.b_ref, bf16[768,2048]{1,0:T(8,128)(2,1)} %bitcast.60, bf16[1152,768]{1,0:T(8,128)(2,1)} %get-tuple-element.15.cg_ref, bf16[1152,768]{1,0:T(8,128)(2,1)} %get-tuple-element.16.cu_ref, ...), custom_call_target="tpu_custom_call" | custom-call | flops 10871635968 | bytes 18874368 | tf_op jit(solution)/shard_map/expert_backward/pallas_call | solution.py:292
  225.7 9.2 %all-to-all-start.7 = ((bf16[128,8,2304]{2,1,0:T(8,128)(2,1)}), bf16[128,8,2304]{2,1,0:T(8,128)(2,1)}, u32[]{:S(2)}, u32[]{:S(2)}) async-start(bf16[128,8,2304]{2,1,0:T(8,128)(2,1)} %bitcast.48), calls=%async_computation.7 | async-start | bytes 9437184 | tf_op jit(solution)/shard_map/all_to_all | solution.py:430
  236.3 9.6 %down_grad.1 = bf16[768,2048]{1,0:T(8,128)(2,1)} custom-call(bf16[1152,768]{1,0:T(8,128)(2,1)} %get-tuple-element.20.a_ref.a9_ref, bf16[1152,768]{1,0:T(8,128)(2,1)} %get-tuple-element.20.a_ref.a9_ref, bf16[1024,2304]{1,0:T(8,128)(2,1)} %bitcast.13.g_ref.b_ref, bf16[128,2048]{1,0:T(8,128)(2,1)} %get-tuple-element.21.b9_ref), custom_call_target="tpu_custom_call" | custom-call | flops 3623878656 | bytes 9633792 | tf_op jit(solution)/shard_map/down_grad/pallas_call | solution.py:338
  246.0 13.2 %gate_up_grad.1 = bf16[2048,1536]{1,0:T(8,128)(2,1)} custom-call(bf16[1024,2304]{1,0:T(8,128)(2,1)} %bitcast.16.x_ref.a_ref, bf16[128,2048]{1,0:T(8,128)(2,1)} %get-tuple-element.18.a9_ref, bf16[1152,1536]{1,0:T(8,128)(2,1)} %get-tuple-element.19.b_ref.b9_ref, bf16[1152,1536]{1,0:T(8,128)(2,1)} %get-tuple-element.19.b_ref.b9_ref), custom_call_target="tpu_custom_call" | custom-call | flops 7247757312 | bytes 14548992 | tf_op jit(solution)/shard_map/gate_up_grad/pallas_call | solution.py:338
  259.2 31.0 %all-to-all-done.7 = bf16[128,8,2304]{2,1,0:T(8,128)(2,1)} async-done(((bf16[128,8,2304]{2,1,0:T(8,128)(2,1)}), bf16[128,8,2304]{2,1,0:T(8,128)(2,1)}, u32[]{:S(2)}, u32[]{:S(2)}) %all-to-all-start.7) | async-done | bytes 4718624 | tf_op jit(solution)/shard_map/all_to_all | solution.py:430
  290.3 7.8 %combine.1 = bf16[128,2048]{1,0:T(8,128)(2,1)} custom-call(s32[128,8]{1,0:T(8,128)} %copy.31.ids_ref, bf16[16,2048]{1,0:T(8,128)(2,1)} %get-tuple-element.13.cot_ref, bf16[1024,2304]{1,0:T(8,128)(2,1)} %bitcast.19.got_ref.fold_ref, bf16[1024,2304]{1,0:T(8,128)(2,1)} %bitcast.19.got_ref.fold_ref), custom_call_target="tpu_custom_call" | custom-call | tf_op jit(solution)/shard_map/combine/pallas_call | solution.py:393
  (21 shorter events, 7.6 us)
Async XLA Ops:
  0.6 49.7 %copy-start.2 = (s32[256]{0:T(256)S(1)}, s32[256]{0:T(256)}, u32[]{:S(2)}) copy-start(s32[256]{0:T(256)} %param.10) | copy-start | bytes 3076
  2.5 14.6 %all-to-all-start.1 = ((bf16[8,128,256]{1,2,0:T(8,128)(2,1)}), bf16[8,128,256]{1,2,0:T(8,128)(2,1)S(1)}, u32[]{:S(2)}, u32[]{:S(2)}) async-start(bf16[8,128,256]{1,2,0:T(8,128)(2,1)} %broadcast_in_dim.11), calls=%async_computation.1 | async-start | bytes 1048576 | tf_op jit(solution)/shard_map/all_to_all | solution.py:412
  18.2 21.6 %all-to-all-start = ((bf16[16,256,128]{1,2,0:T(8,128)(2,1)}), bf16[16,256,128]{1,2,0:T(8,128)(2,1)S(1)}, u32[]{:S(2)}, u32[]{:S(2)}) async-start(bf16[16,256,128]{1,2,0:T(8,128)(2,1)} %broadcast_in_dim.10), calls=%async_computation | async-start | bytes 2097152 | tf_op jit(solution)/shard_map/all_to_all | solution.py:412
  40.8 9.5 %all-to-all-start.2 = ((f32[16,2,256]{2,1,0:T(2,128)}), f32[16,2,256]{2,1,0:T(2,128)S(1)}, u32[]{:S(2)}, u32[]{:S(2)}) async-start(f32[16,2,256]{2,1,0:T(2,128)} %broadcast_in_dim.12), calls=%async_computation.2 | async-start | bytes 65536 | tf_op jit(solution)/shard_map/all_to_all | solution.py:412
  51.8 17.8 %all-to-all-start.4 = ((bf16[16,16,2048]{2,1,0:T(8,128)(2,1)}), bf16[16,16,2048]{2,1,0:T(8,128)(2,1)S(1)}, u32[]{:S(2)}, u32[]{:S(2)}) async-start(bf16[16,16,2048]{2,1,0:T(8,128)(2,1)} %bitcast.11), calls=%async_computation.4 | async-start | bytes 2097152 | tf_op jit(solution)/shard_map/all_to_all | solution.py:468
  69.6 1.0 copy-start
  70.6 67.3 %all-to-all-start.6 = ((bf16[128,8,2304]{2,1,0:T(8,128)(2,1)}), bf16[128,8,2304]{2,1,0:T(8,128)(2,1)}, u32[]{:S(2)}, u32[]{:S(2)}) async-start(bf16[128,8,2304]{2,1,0:T(8,128)(2,1)} %bitcast.44), calls=%async_computation.6 | async-start | bytes 9437184 | tf_op jit(solution)/shard_map/all_to_all | solution.py:430
  137.9 62.7 %all-to-all-start.5 = ((bf16[128,8,2304]{2,1,0:T(8,128)(2,1)}), bf16[128,8,2304]{2,1,0:T(8,128)(2,1)}, u32[]{:S(2)}, u32[]{:S(2)}) async-start(bf16[128,8,2304]{2,1,0:T(8,128)(2,1)} %bitcast.47), calls=%async_computation.5 | async-start | bytes 9437184 | tf_op jit(solution)/shard_map/all_to_all | solution.py:430
  200.6 25.1 %all-to-all-start.3 = ((bf16[8,128,256]{2,1,0:T(8,128)(2,1)}), bf16[8,128,256]{2,1,0:T(8,128)(2,1)S(1)}, u32[]{:S(2)}, u32[]{:S(2)}) async-start(bf16[8,128,256]{2,1,0:T(8,128)(2,1)} %bitcast.43), calls=%async_computation.3 | async-start | bytes 1048576 | tf_op jit(solution)/shard_map/all_to_all | solution.py:475
  225.7 9.2 %copy-start.1 = (s32[128,8]{0,1:T(8,128)S(1)}, s32[128,8]{0,1:T(8,128)}, u32[]{:S(2)}) copy-start(s32[128,8]{0,1:T(8,128)} %param.12) | copy-start | bytes 12292
  225.7 64.6 %all-to-all-start.7 = ((bf16[128,8,2304]{2,1,0:T(8,128)(2,1)}), bf16[128,8,2304]{2,1,0:T(8,128)(2,1)}, u32[]{:S(2)}, u32[]{:S(2)}) async-start(bf16[128,8,2304]{2,1,0:T(8,128)(2,1)} %bitcast.48), calls=%async_computation.7 | async-start | bytes 9437184 | tf_op jit(solution)/shard_map/all_to_all | solution.py:430

commit v2 on v1

--- a/solution.py
+++ b/solution.py
@@ -1,4 +1,6 @@
 import functools
+import math
+
 import jax
 import jax.numpy as jnp
 from jax import lax
@@ -95,7 +97,8 @@
     )(ids_t, tokens)
 
 
-def send_grads_kernel(ids_ref, weight_ref, part_ref, out_ref, cot_ref, key_ref, row_ref, rep_ref):
+def send_grads_kernel(ids_ref, weight_ref, *refs):
+    *part_refs, out_ref, cot_ref, key_ref, row_ref, rep_ref = refs
     j = pl.program_id(0)
     tiles = pl.num_programs(0) - 1
     width = out_ref.shape[1]
@@ -116,9 +119,7 @@
         main = jnp.sum(jnp.where(key == slot, weight, 0.0), axis=1, keepdims=True)
         ninth = jnp.sum(jnp.where(key == MAIN, weight, 0.0), axis=1, keepdims=True)
         row_ref[...] = jnp.where(iota(row_ref.shape, 1) == 0, main, ninth)
-        total = part_ref[0].astype(F32)
-        for c in range(1, part_ref.shape[0]):
-            total += part_ref[c].astype(F32)
+        total = sum(part[...].astype(F32) for part in part_refs)
         cot = (total / SEQ_LEN).astype(B16)
         cot_ref[...] = cot
         spread = one_hot(iota((toks, cot.shape[0]), 0) // SEQ_LEN == iota((toks, cot.shape[0]), 1))
@@ -143,12 +144,12 @@
 
 def send_grads(ids_t, weights_t, parts, experts):
     toks = ids_t.shape[1]
-    _, queries, depth = parts.shape
+    queries, depth = parts[0].shape
     width = depth // MAIN
     return pl.pallas_call(
         send_grads_kernel,
         grid=(MAIN + 1,),
-        in_specs=[whole(ids_t.shape), whole(weights_t.shape), whole(parts.shape)],
+        in_specs=[whole(ids_t.shape), whole(weights_t.shape)] + [whole(p.shape) for p in parts],
         out_specs=[
             pl.BlockSpec((experts * MAIN, width), lambda j: (0, j)),
             pl.BlockSpec((queries, depth), lambda j: (0, 0)),
@@ -164,7 +165,7 @@
         ],
         compiler_params=params(),
         name="send_grads",
-    )(ids_t, weights_t, parts)
+    )(ids_t, weights_t, *parts)
 
 
 def unfold(fold, fold_ref, out_ref):
@@ -407,6 +408,135 @@
     )(ids, cot, got, got)
 
 
+def scores_kernel(query_ref, passage_ref, score_ref, stat_ref):
+    pieces, _, width = passage_ref.shape
+    step = query_ref.shape[2]
+    total = jnp.zeros(score_ref.shape, F32)
+    for r in range(pieces):
+        for h in range(width // step):
+            part = passage_ref[r, :, h * step : (h + 1) * step]
+            total += dot(part, query_ref[r * (width // step) + h], ((1,), (1,)))
+    scores = total / SHARPNESS
+    peak = jnp.max(scores, axis=0, keepdims=True)
+    mass = jnp.sum(jnp.exp(scores - peak), axis=0, keepdims=True)
+    score_ref[...] = scores
+    stat_ref[...] = jnp.where(iota(stat_ref.shape, 0) == 0, peak, mass)
+
+
+def local_scores(queries, passages):
+    shape = (passages.shape[1], queries.shape[1])
+    return pl.pallas_call(
+        scores_kernel,
+        out_shape=[
+            jax.ShapeDtypeStruct(shape, F32),
+            jax.ShapeDtypeStruct((8, shape[1]), F32),
+        ],
+        compiler_params=params(),
+        name="local_scores",
+    )(queries, passages)
+
+
+def merged(stats):
+    peak = functools.reduce(jnp.maximum, [s[0:1] for s in stats])
+    mass = sum(s[1:2] * jnp.exp(s[0:1] - peak) for s in stats)
+    return peak, mass
+
+
+def query_part_kernel(at_ref, score_ref, pos_ref, passage_ref, *refs):
+    count = len(refs) - 2
+    side = count // 2
+    stat_refs, out_refs = refs[:side], refs[side:count]
+    dscore_ref, part_ref = refs[count], refs[count + 1]
+    peak, mass = merged([s[...] for s in stat_refs])
+    column = at_ref[1] + iota(score_ref.shape, 0)
+    chosen = jnp.where(pos_ref[...] == column, 1.0, 0.0)
+    soft = jnp.exp(score_ref[...] - peak) / mass
+    dscore = ((soft - chosen) / SHARPNESS).astype(B16)
+    dscore_ref[...] = dscore
+    pieces, _, width = passage_ref.shape
+    for r in range(pieces):
+        part_ref[:, r * width : (r + 1) * width] = dot(
+            dscore, passage_ref[r], ((0,), (0,))
+        ).astype(B16)
+    rows = out_refs[0].shape[0]
+    for k in range(side):
+        start = pl.multiple_of(((at_ref[0] + k) % side) * rows, rows)
+        out_refs[k][...] = part_ref[pl.ds(start, rows), :]
+
+
+def query_part(at, scores, positive, passages, stats):
+    side = len(stats)
+    pieces, _, width = passages.shape
+    queries = scores.shape[1]
+    depth = pieces * width
+    smem = pl.BlockSpec(memory_space=pltpu.SMEM)
+    vmem = pl.BlockSpec(memory_space=pltpu.VMEM)
+    out = pl.pallas_call(
+        query_part_kernel,
+        in_specs=[smem] + [vmem] * (3 + side),
+        out_specs=[vmem] * (side + 1),
+        out_shape=[jax.ShapeDtypeStruct((queries // side, depth), B16)] * side
+        + [jax.ShapeDtypeStruct(scores.shape, B16)],
+        scratch_shapes=[pltpu.VMEM((queries, depth), B16)],
+        compiler_params=params(),
+        name="query_part",
+    )(at, scores, positive, passages, *stats)
+    return out[:side], out[side]
+
+
+def forwarded_kernel(at_ref, *refs):
+    side = (len(refs) - 1) // 2
+    total_ref = refs[-1]
+    total_ref[...] = sum(p[...].astype(F32) for p in refs[:side])
+    rows = refs[side].shape[0]
+    for k in range(side):
+        start = pl.multiple_of(((at_ref[0] + k) % side) * rows, rows)
+        refs[side + k][...] = total_ref[pl.ds(start, rows), :].astype(B16)
+
+
+def forwarded(at, parts):
+    side = len(parts)
+    rows, depth = parts[0].shape
+    vmem = pl.BlockSpec(memory_space=pltpu.VMEM)
+    return pl.pallas_call(
+        forwarded_kernel,
+        in_specs=[pl.BlockSpec(memory_space=pltpu.SMEM)] + [vmem] * side,
+        out_specs=[vmem] * side,
+        out_shape=[jax.ShapeDtypeStruct((rows // side, depth), B16)] * side,
+        scratch_shapes=[pltpu.VMEM((rows, depth), F32)],
+        compiler_params=params(),
+        name="forwarded",
+    )(at, *parts)
+
+
+def passage_part_kernel(at_ref, dscore_ref, query_ref, *refs):
+    peers = len(refs) - 1
+    out_refs, part_ref = refs[:peers], refs[peers]
+    pieces, _, step = query_ref.shape
+    for c in range(pieces):
+        part_ref[:, c * step : (c + 1) * step] = dot(dscore_ref[...], query_ref[c]).astype(B16)
+    width = out_refs[0].shape[1]
+    for k in range(peers):
+        start = pl.multiple_of(((at_ref[0] + k) % peers) * width, width)
+        out_refs[k][...] = part_ref[:, pl.ds(start, width)]
+
+
+def passage_part(at, dscore, queries, peers):
+    pieces, _, step = queries.shape
+    depth = pieces * step
+    rows = dscore.shape[0]
+    vmem = pl.BlockSpec(memory_space=pltpu.VMEM)
+    return pl.pallas_call(
+        passage_part_kernel,
+        in_specs=[pl.BlockSpec(memory_space=pltpu.SMEM), vmem, vmem],
+        out_specs=[vmem] * peers,
+        out_shape=[jax.ShapeDtypeStruct((rows, depth // peers), B16)] * peers,
+        scratch_shapes=[pltpu.VMEM((rows, depth), B16)],
+        compiler_params=params(),
+        name="passage_part",
+    )(at, dscore, queries)
+
+
 def sent_to_all(value, axis):
     peers = lax.axis_size(axis)
     return lax.all_to_all(
@@ -414,15 +544,16 @@
     )
 
 
-def gathered_copies(value, axis):
-    tiles = jnp.moveaxis(sent_to_all(value, axis), 0, 1)
-    return tiles.reshape(tiles.shape[0], -1)
-
-
-def split_up(value, dim, peers):
-    lengths = value.shape
-    tiles = value.reshape(*lengths[:dim], peers, lengths[dim] // peers, *lengths[dim + 1 :])
-    return jnp.moveaxis(tiles, dim, 0)
+def ring_steps(size, side, stride):
+    def moved(i, k):
+        at = i // stride % side
+        return i + ((at + k) % side - at) * stride
+
+    return [[(i, moved(i, k)) for i in range(size)] for k in range(1, side)]
+
+
+def passed(values, axis, steps):
+    return [values[0]] + [lax.ppermute(v, axis, p) for v, p in zip(values[1:], steps)]
 
 
 def exchanged(block, experts):
@@ -452,28 +583,27 @@
     ids_t, weights_t = expert_ids.T, route_weights.T
     tokens_out = send_tokens(ids_t, tokens, experts)
 
-    passages = gathered_copies(document_vectors, "row")
-    queries = gathered_copies(question_vectors, "col")
-    scores = dot(queries, passages, ((1,), (1,))) / SHARPNESS
-    local_peak = jnp.max(scores, axis=1)
-    local_total = jnp.sum(jnp.exp(scores - local_peak[:, None]), axis=1)
-    stats = sent_to_all(jnp.stack([local_peak, local_total]), "col")
-    peak = jnp.max(stats[:, 0], axis=0)
-    total = jnp.sum(stats[:, 1] * jnp.exp(stats[:, 0] - peak[None]), axis=0)
-    count = passages.shape[0]
-    columns = lax.axis_index("col") * count + jnp.arange(count, dtype=jnp.int32)
-    chosen = (positive[:, None] == columns[None, :]).astype(F32)
-    dscore = ((jnp.exp(scores - peak[:, None]) / total[:, None] - chosen) / SHARPNESS).astype(B16)
-    query_part = dot(dscore, passages).astype(B16)
-    query_parts = lax.all_to_all(split_up(query_part, 0, col_size), "col", 0, 0, tiled=True)
-
+    side = math.isqrt(col_size)
+    far, near = ring_steps(col_size, side, side), ring_steps(col_size, side, 1)
+    row, col = lax.axis_index("row"), lax.axis_index("col")
+    passages = lax.all_gather(document_vectors, "row")
+    queries = sent_to_all(question_vectors, "col")
+    tokens_out, passages = lax.optimization_barrier((tokens_out, passages))
+    scores, stat = local_scores(queries, passages)
     slot_inputs = exchanged(tokens_out, experts)
-    grads_out, cot = send_grads(ids_t, weights_t, query_parts, experts)
+    stat = jnp.concatenate(merged(passed([stat] * side, "col", far)))
+    stats = passed([stat] * side, "col", near)
+    parts, dscore = query_part(
+        jnp.stack([col // side, col * scores.shape[0]]), scores, positive[None], passages, stats
+    )
+    parts = forwarded((col % side)[None], passed(parts, "col", far))
+    parts = passed(parts, "col", near)
+    grads_out, cot = send_grads(ids_t, weights_t, parts, experts)
     slot_grads = exchanged(grads_out, experts)
 
-    passage_part = dot(dscore, queries, ((0,), (0,))).astype(B16)
-    passage_parts = lax.all_to_all(split_up(passage_part, 1, row_size), "row", 0, 0, tiled=True)
-    passage_grad = jnp.sum(passage_parts.astype(F32), axis=0)
+    pieces = passage_part(row[None], dscore, queries, row_size)
+    pieces = passed(pieces, "row", ring_steps(row_size, row_size, 1))
+    passage_grad = sum(p.astype(F32) for p in pieces)
 
     hid, cg, cu, inputs9 = forward(slot_inputs, gate_up, hidden)
     back_out, pre_grad, grads9 = backward(slot_grads, down, cg, cu, gate_up)

time: 302 us -> 330 us (1.093)
  starting transfers between devices: 56.7 us -> 76.6 us
  blocking collectives: 0 us -> 15.8 us
  waiting for transfers between devices: 149 us -> 135 us
  Pallas kernels: 81.6 us -> 90.7 us
    ppermute x0 -> x19, waiting for transfers between devices: none -> 92.4 us  [passed(): lax.ppermute(v, axis, p)]
    all_to_all x3, waiting for transfers between devices: 119 us -> 42.6 us  [exchanged(): lax.all_to_all(block.reshape(experts, rows // experts, width), ('row', 'c...]
    ppermute x0 -> x19, starting transfers between devices: none -> 33.8 us  [passed(): lax.ppermute(v, axis, p)]
    all_to_all x3 -> x1, waiting for transfers between devices: 26.5 us -> 0.01 us  [sent_to_all(): lax.all_to_all(jnp.broadcast_to(value[None], (peers, *value.shape)), axis...]
    all_gather x0 -> x1, blocking collectives: none -> 15.8 us  [shards(): passages = lax.all_gather(document_vectors, 'row')]
    all_to_all x3 -> x1, starting transfers between devices: 18.2 us -> 7.28 us  [sent_to_all(): lax.all_to_all(jnp.broadcast_to(value[None], (peers, *value.shape)), axis...]
    all_to_all x2 -> x0, starting transfers between devices: 10.2 us -> none  [the longest x1 6.32 us: shards(): lax.all_to_all(split_up(query_part, 0, col_size), 'col', 0, 0, tiled=True)]
    pallas_call x0 -> x4, Pallas kernels: none -> 9.63 us  [the longest x1 2.63 us: query_part(): pl.pallas_call(query_part_kernel, in_specs=[smem] + [vmem] * (3 + side),...]
  transfers between devices with their start and end apart: 8 -> 23, of which waited for: 7 -> 13; matrix products, arithmetic and copies ran while one was open for 1% -> 1% of each run, Pallas kernels for 25% -> 19%
where the time goes in v2:
time: 330 us; the launch traced here: 327 us
  waiting for transfers between devices  135 us (41%)
  Pallas kernels  90.7 us (27%)
  starting transfers between devices  76.6 us (23%)
  blocking collectives  15.8 us (5%)
  local copies, waits for them, and re-layouts  5.72 us (2%)
    ppermute x19, waiting for transfers between devices, passed(): lax.ppermute(v, axis, p)  92.4 us
    all_to_all x3, waiting for transfers between devices, exchanged(): lax.all_to_all(block.reshape(experts, rows // experts, width), ('row', 'c...  42.6 us
    all_to_all x3, starting transfers between devices, exchanged(): lax.all_to_all(block.reshape(experts, rows // experts, width), ('row', 'c...  35.5 us
    ppermute x19, starting transfers between devices, passed(): lax.ppermute(v, axis, p)  33.8 us
    pallas_call x2, Pallas kernels, weight_grad(): pl.pallas_call(weight_grad_kernel, grid=(columns // tile,), in_specs=[pl....  22.9 us
    pallas_call x1, Pallas kernels, backward(): pl.pallas_call(functools.partial(backward_kernel, first), grid=(first + M...  21.2 us
    all_gather x1, blocking collectives, shards(): passages = lax.all_gather(document_vectors, 'row')  15.8 us
    pallas_call x1, Pallas kernels, forward(): pl.pallas_call(forward_kernel, grid=(tiles,), in_specs=[whole(x.shape), p...  12.8 us
  transfers between devices with their start and end apart: 23, of which 13 were waited for; matrix products, arithmetic and copies ran while one was open for 1% of the time, Pallas kernels for 19%

profile of v2, /device:TPU:37, one launch (start us, length us, event | category | flops | bytes accessed | tf_op | source)
XLA Modules:
  0.0 327.5 jit_solution(3550445881138951757)
XLA Ops:
  2.7 7.3 %all-to-all-start = ((bf16[16,256,128]{2,1,0:T(8,128)(2,1)}), bf16[16,256,128]{2,1,0:T(8,128)(2,1)S(1)}, u32[]{:S(2)}, u32[]{:S(2)}) async-start(bf16[16,256,128]{2,1,0:T(8,128)(2,1)} %broadcast_in_dim.22), calls=%async_computation | async-start | bytes 2097152 | tf_op jit(solution)/shard_map/all_to_all | solution.py:542
  10.0 8.1 %send_tokens.1 = bf16[1024,2304]{1,0:T(8,128)(2,1)} custom-call(s32[8,128]{1,0:T(8,128)} %bitcast.23, bf16[128,2048]{1,0:T(8,128)(2,1)} %tok_ref.1), custom_call_target="tpu_custom_call" | custom-call | tf_op jit(solution)/shard_map/send_tokens/pallas_call | solution.py:88
  18.1 15.8 %all-gather = bf16[1024,256]{1,0:T(8,128)(2,1)} all-gather(bf16[128,256]{1,0:T(8,128)(2,1)S(1)} %copy-done.4), channel_id=2, replica_groups=mesh['row'=8,'col'=16] {'row'}, dimensions={0}, use_global_device_ids=true | all-gather | bytes 589824 | tf_op jit(solution)/shard_map/all_gather | solution.py:589
  34.9 9.1 %all-to-all-start.2 = ((bf16[128,8,2304]{2,1,0:T(8,128)(2,1)}), bf16[128,8,2304]{2,1,0:T(8,128)(2,1)}, u32[]{:S(2)}, u32[]{:S(2)}) async-start(bf16[128,8,2304]{2,1,0:T(8,128)(2,1)} %bitcast.18), calls=%async_computation.2 | async-start | bytes 9437184 | tf_op jit(solution)/shard_map/all_to_all | solution.py:561
  46.6 2.5 collective-permute-start.1
  50.9 8.0 %collective-permute-done.2 = f32[8,256]{1,0:T(8,128)S(1)} collective-permute-done((f32[8,256]{1,0:T(8,128)}, f32[8,256]{1,0:T(8,128)S(1)}, u32[]{:S(2)}, u32[]{:S(2)}) %collective-permute-start.2) | collective-permute-done | bytes 8224 | tf_op jit(solution)/shard_map/ppermute | solution.py:556
  58.9 11.7 %collective-permute-done.1 = f32[8,256]{1,0:T(8,128)S(1)} collective-permute-done((f32[8,256]{1,0:T(8,128)}, f32[8,256]{1,0:T(8,128)S(1)}, u32[]{:S(2)}, u32[]{:S(2)}) %collective-permute-start.1) | collective-permute-done | bytes 8224 | tf_op jit(solution)/shard_map/ppermute | solution.py:556
  71.5 11.6 %collective-permute-start.4 = (f32[2,256]{1,0:T(2,128)S(1)}, f32[2,256]{1,0:T(2,128)S(1)}, u32[]{:S(2)}, u32[]{:S(2)}) collective-permute-start(f32[2,256]{1,0:T(2,128)S(1)} %pad_maximum_fusion.refs_0_), channel_id=1, source_target_pairs={{0,2},{1,3},{2,0},{3,1},{4,6},{5,7},{6,4},{7,5},{8,10},{9,11},{10,... | collective-permute-start | bytes 6152 | tf_op jit(solution)/shard_map/ppermute | solution.py:556
  83.7 11.6 %collective-permute-done.5.refs_3_ = f32[2,256]{1,0:T(2,128)S(1)} collective-permute-done((f32[2,256]{1,0:T(2,128)S(1)}, f32[2,256]{1,0:T(2,128)S(1)}, u32[]{:S(2)}, u32[]{:S(2)}) %collective-permute-start.5) | collective-permute-done | bytes 2080 | tf_op jit(solution)/shard_map/ppermute | solution.py:556
  95.9 2.6 query_part.1
  103.0 2.9 collective-permute-done.13.refs_1_
  105.8 2.7 collective-permute-done.14.refs_2_
  108.5 5.9 %collective-permute-done.15.refs_3_ = bf16[64,2048]{1,0:T(8,128)(2,1)S(1)} collective-permute-done((bf16[64,2048]{1,0:T(8,128)(2,1)}, bf16[64,2048]{1,0:T(8,128)(2,1)S(1)}, u32[]{:S(2)}, u32[]{:S(2)}) %collective-permute-start.15) | collective-permute-done | bytes 262176 | tf_op jit(solution)/shard_map/ppermute | solution.py:556
  124.4 8.2 %send_grads.1 = (bf16[1024,2304]{1,0:T(8,128)(2,1)}, bf16[16,2048]{1,0:T(8,128)(2,1)}) custom-call(s32[8,128]{1,0:T(8,128)} %bitcast.24, f32[8,128]{1,0:T(8,128)} %bitcast.25, bf16[16,2048]{1,0:T(8,128)(2,1)} %get-tuple-element.50.refs_0_, bf16[16,2048]{1,0:T(8,128)(2,1)} %copy-done.5, bf16[16,2048]{1,0:T(8,128)(2,1)} %copy-done.6, bf16[16,2048]{1,0:T(8,128)(2,1)} %copy-done.7), custom_call_target="tpu_custom_call" | custom-call | tf_op jit(solution)/shard_map/send_grads/pallas_call | solution.py:149
  132.6 19.2 %all-to-all-start.1 = ((bf16[128,8,2304]{2,1,0:T(8,128)(2,1)}), bf16[128,8,2304]{2,1,0:T(8,128)(2,1)}, u32[]{:S(2)}, u32[]{:S(2)}) async-start(bf16[128,8,2304]{2,1,0:T(8,128)(2,1)} %bitcast.22), calls=%async_computation.1 | async-start | bytes 9437184 | tf_op jit(solution)/shard_map/all_to_all | solution.py:561
  151.7 12.8 %expert_forward.1 = (bf16[1152,768]{1,0:T(8,128)(2,1)}, bf16[1152,768]{1,0:T(8,128)(2,1)}, bf16[1152,768]{1,0:T(8,128)(2,1)}, bf16[128,2048]{1,0:T(8,128)(2,1)}) custom-call(bf16[1024,2304]{1,0:T(8,128)(2,1)} %bitcast.12.x_ref.a_ref, bf16[2048,1536]{1,0:T(8,128)(2,1)} %bitcast.27, bf16[2048,1536]{1,0:T(8,128)(2,1)} %bitcast.28), custom_call_target="tpu_custom_call" | custom-call | flops 7247757312 | bytes 16318464 | tf_op jit(solution)/shard_map/expert_forward/pallas_call | solution.py:216
  164.5 42.6 %all-to-all-done.1 = bf16[128,8,2304]{2,1,0:T(8,128)(2,1)} async-done(((bf16[128,8,2304]{2,1,0:T(8,128)(2,1)}), bf16[128,8,2304]{2,1,0:T(8,128)(2,1)}, u32[]{:S(2)}, u32[]{:S(2)}) %all-to-all-start.1) | async-done | bytes 4718624 | tf_op jit(solution)/shard_map/all_to_all | solution.py:561
  207.1 21.2 %expert_backward.1 = (bf16[1024,2304]{1,0:T(8,128)(2,1)}, bf16[1152,1536]{1,0:T(8,128)(2,1)}, bf16[128,2048]{1,0:T(8,128)(2,1)}) custom-call(bf16[1024,2304]{1,0:T(8,128)(2,1)} %bitcast.9.g_ref.b_ref, bf16[768,2048]{1,0:T(8,128)(2,1)} %bitcast.30, bf16[1152,768]{1,0:T(8,128)(2,1)} %get-tuple-element.57.cg_ref, bf16[1152,768]{1,0:T(8,128)(2,1)} %get-tuple-element.58.cu_ref, ...), custom_call_target="tpu_custom_call" | custom-call | flops 10871635968 | bytes 18874368 | tf_op jit(solution)/shard_map/expert_backward/pallas_call | solution.py:293
  228.3 7.3 %all-to-all-start.3 = ((bf16[128,8,2304]{2,1,0:T(8,128)(2,1)}), bf16[128,8,2304]{2,1,0:T(8,128)(2,1)}, u32[]{:S(2)}, u32[]{:S(2)}) async-start(bf16[128,8,2304]{2,1,0:T(8,128)(2,1)} %bitcast.21), calls=%async_computation.3 | async-start | bytes 9437184 | tf_op jit(solution)/shard_map/all_to_all | solution.py:561
  235.6 2.5 passage_part.1
  244.8 42.3 %collective-permute-done.6 = bf16[128,256]{1,0:T(8,128)(2,1)S(1)} collective-permute-done((bf16[128,256]{1,0:T(8,128)(2,1)}, bf16[128,256]{1,0:T(8,128)(2,1)S(1)}, u32[]{:S(2)}, u32[]{:S(2)}) %collective-permute-start.6) | collective-permute-done | bytes 65568 | tf_op jit(solution)/shard_map/ppermute | solution.py:556
  296.8 9.6 %down_grad.1 = bf16[768,2048]{1,0:T(8,128)(2,1)} custom-call(bf16[1152,768]{1,0:T(8,128)(2,1)} %get-tuple-element.62.a_ref.a9_ref, bf16[1152,768]{1,0:T(8,128)(2,1)} %get-tuple-element.62.a_ref.a9_ref, bf16[1024,2304]{1,0:T(8,128)(2,1)} %bitcast.9.g_ref.b_ref, bf16[128,2048]{1,0:T(8,128)(2,1)} %get-tuple-element.63.b9_ref), custom_call_target="tpu_custom_call" | custom-call | flops 3623878656 | bytes 9633792 | tf_op jit(solution)/shard_map/down_grad/pallas_call | solution.py:339
  306.5 13.2 %gate_up_grad.1 = bf16[2048,1536]{1,0:T(8,128)(2,1)} custom-call(bf16[1024,2304]{1,0:T(8,128)(2,1)} %bitcast.12.x_ref.a_ref, bf16[128,2048]{1,0:T(8,128)(2,1)} %get-tuple-element.60.a9_ref, bf16[1152,1536]{1,0:T(8,128)(2,1)} %get-tuple-element.61.b_ref.b9_ref, bf16[1152,1536]{1,0:T(8,128)(2,1)} %get-tuple-element.61.b_ref.b9_ref), custom_call_target="tpu_custom_call" | custom-call | flops 7247757312 | bytes 14548992 | tf_op jit(solution)/shard_map/gate_up_grad/pallas_call | solution.py:339
  319.7 7.8 %combine.1 = bf16[128,2048]{1,0:T(8,128)(2,1)} custom-call(s32[128,8]{1,0:T(8,128)} %copy.12.ids_ref, bf16[16,2048]{1,0:T(8,128)(2,1)} %get-tuple-element.54.cot_ref, bf16[1024,2304]{1,0:T(8,128)(2,1)} %bitcast.15.got_ref.fold_ref, bf16[1024,2304]{1,0:T(8,128)(2,1)} %bitcast.15.got_ref.fold_ref), custom_call_target="tpu_custom_call" | custom-call | tf_op jit(solution)/shard_map/combine/pallas_call | solution.py:394
  (66 shorter events, 40.3 us)
Async XLA Ops:
  2.7 31.2 %all-to-all-start = ((bf16[16,256,128]{2,1,0:T(8,128)(2,1)}), bf16[16,256,128]{2,1,0:T(8,128)(2,1)S(1)}, u32[]{:S(2)}, u32[]{:S(2)}) async-start(bf16[16,256,128]{2,1,0:T(8,128)(2,1)} %broadcast_in_dim.22), calls=%async_computation | async-start | bytes 2097152 | tf_op jit(solution)/shard_map/all_to_all | solution.py:542
  34.9 97.6 %all-to-all-start.2 = ((bf16[128,8,2304]{2,1,0:T(8,128)(2,1)}), bf16[128,8,2304]{2,1,0:T(8,128)(2,1)}, u32[]{:S(2)}, u32[]{:S(2)}) async-start(bf16[128,8,2304]{2,1,0:T(8,128)(2,1)} %bitcast.18), calls=%async_computation.2 | async-start | bytes 9437184 | tf_op jit(solution)/shard_map/all_to_all | solution.py:561
  46.5 12.4 %collective-permute-start.2 = (f32[8,256]{1,0:T(8,128)}, f32[8,256]{1,0:T(8,128)S(1)}, u32[]{:S(2)}, u32[]{:S(2)}) collective-permute-start(f32[8,256]{1,0:T(8,128)} %get-tuple-element.36), channel_id=1, source_target_pairs={{0,12},{1,13},{2,14},{3,15},{4,0},{5,1},{6,2},{7,3},{8,4},{9,5},{1... | collective-permute-start | bytes 24584 | tf_op jit(solution)/shard_map/ppermute | solution.py:556
  46.6 24.0 %collective-permute-start.1 = (f32[8,256]{1,0:T(8,128)}, f32[8,256]{1,0:T(8,128)S(1)}, u32[]{:S(2)}, u32[]{:S(2)}) collective-permute-start(f32[8,256]{1,0:T(8,128)} %get-tuple-element.36), channel_id=1, source_target_pairs={{0,8},{1,9},{2,10},{3,11},{4,12},{5,13},{6,14},{7,15},{8,0},{9,1},... | collective-permute-start | bytes 24584 | tf_op jit(solution)/shard_map/ppermute | solution.py:556
  49.1 21.5 %collective-permute-start = (f32[8,256]{1,0:T(8,128)}, f32[8,256]{1,0:T(8,128)S(1)}, u32[]{:S(2)}, u32[]{:S(2)}) collective-permute-start(f32[8,256]{1,0:T(8,128)} %get-tuple-element.36), channel_id=1, source_target_pairs={{0,4},{1,5},{2,6},{3,7},{4,8},{5,9},{6,10},{7,11},{8,12},{9,13},{1... | collective-permute-start | bytes 24584 | tf_op jit(solution)/shard_map/ppermute | solution.py:556
  71.4 23.9 %collective-permute-start.5 = (f32[2,256]{1,0:T(2,128)S(1)}, f32[2,256]{1,0:T(2,128)S(1)}, u32[]{:S(2)}, u32[]{:S(2)}) collective-permute-start(f32[2,256]{1,0:T(2,128)S(1)} %pad_maximum_fusion.refs_0_), channel_id=1, source_target_pairs={{0,3},{1,0},{2,1},{3,2},{4,7},{5,4},{6,5},{7,6},{8,11},{9,8},{10,9... | collective-permute-start | bytes 6152 | tf_op jit(solution)/shard_map/ppermute | solution.py:556
  71.5 23.8 %collective-permute-start.4 = (f32[2,256]{1,0:T(2,128)S(1)}, f32[2,256]{1,0:T(2,128)S(1)}, u32[]{:S(2)}, u32[]{:S(2)}) collective-permute-start(f32[2,256]{1,0:T(2,128)S(1)} %pad_maximum_fusion.refs_0_), channel_id=1, source_target_pairs={{0,2},{1,3},{2,0},{3,1},{4,6},{5,7},{6,4},{7,5},{8,10},{9,11},{10,... | collective-permute-start | bytes 6152 | tf_op jit(solution)/shard_map/ppermute | solution.py:556
  83.1 12.2 %collective-permute-start.3 = (f32[2,256]{1,0:T(2,128)S(1)}, f32[2,256]{1,0:T(2,128)S(1)}, u32[]{:S(2)}, u32[]{:S(2)}) collective-permute-start(f32[2,256]{1,0:T(2,128)S(1)} %pad_maximum_fusion.refs_0_), channel_id=1, source_target_pairs={{0,1},{1,2},{2,3},{3,0},{4,5},{5,6},{6,7},{7,4},{8,9},{9,10},{10,1... | collective-permute-start | bytes 6152 | tf_op jit(solution)/shard_map/ppermute | solution.py:556
  98.6 7.3 %collective-permute-start.13 = (bf16[64,2048]{1,0:T(8,128)(2,1)}, bf16[64,2048]{1,0:T(8,128)(2,1)S(1)}, u32[]{:S(2)}, u32[]{:S(2)}) collective-permute-start(bf16[64,2048]{1,0:T(8,128)(2,1)} %get-tuple-element.47), channel_id=1, source_target_pairs={{0,4},{1,5},{2,6},{3,7},{4,8},{5,9},{6,10},{7,11},{8,12},{9,13},{1... | collective-permute-start | bytes 786440 | tf_op jit(solution)/shard_map/ppermute | solution.py:556
  100.0 8.5 %collective-permute-start.14 = (bf16[64,2048]{1,0:T(8,128)(2,1)}, bf16[64,2048]{1,0:T(8,128)(2,1)S(1)}, u32[]{:S(2)}, u32[]{:S(2)}) collective-permute-start(bf16[64,2048]{1,0:T(8,128)(2,1)} %get-tuple-element.48), channel_id=1, source_target_pairs={{0,8},{1,9},{2,10},{3,11},{4,12},{5,13},{6,14},{7,15},{8,0},{9,1},... | collective-permute-start | bytes 786440 | tf_op jit(solution)/shard_map/ppermute | solution.py:556
  101.0 13.4 %collective-permute-start.15 = (bf16[64,2048]{1,0:T(8,128)(2,1)}, bf16[64,2048]{1,0:T(8,128)(2,1)S(1)}, u32[]{:S(2)}, u32[]{:S(2)}) collective-permute-start(bf16[64,2048]{1,0:T(8,128)(2,1)} %get-tuple-element.49), channel_id=1, source_target_pairs={{0,12},{1,13},{2,14},{3,15},{4,0},{5,1},{6,2},{7,3},{8,4},{9,5},{1... | collective-permute-start | bytes 786440 | tf_op jit(solution)/shard_map/ppermute | solution.py:556
  117.2 4.1 %collective-permute-start.16 = (bf16[16,2048]{1,0:T(8,128)(2,1)}, bf16[16,2048]{1,0:T(8,128)(2,1)S(1)}, u32[]{:S(2)}, u32[]{:S(2)}) collective-permute-start(bf16[16,2048]{1,0:T(8,128)(2,1)} %get-tuple-element.51), channel_id=1, source_target_pairs={{0,1},{1,2},{2,3},{3,0},{4,5},{5,6},{6,7},{7,4},{8,9},{9,10},{10,1... | collective-permute-start | bytes 196616 | tf_op jit(solution)/shard_map/ppermute | solution.py:556
  118.4 5.3 %collective-permute-start.17 = (bf16[16,2048]{1,0:T(8,128)(2,1)}, bf16[16,2048]{1,0:T(8,128)(2,1)S(1)}, u32[]{:S(2)}, u32[]{:S(2)}) collective-permute-start(bf16[16,2048]{1,0:T(8,128)(2,1)} %get-tuple-element.52), channel_id=1, source_target_pairs={{0,2},{1,3},{2,0},{3,1},{4,6},{5,7},{6,4},{7,5},{8,10},{9,11},{10,... | collective-permute-start | bytes 196616 | tf_op jit(solution)/shard_map/ppermute | solution.py:556
  119.6 4.1 %collective-permute-start.18 = (bf16[16,2048]{1,0:T(8,128)(2,1)}, bf16[16,2048]{1,0:T(8,128)(2,1)S(1)}, u32[]{:S(2)}, u32[]{:S(2)}) collective-permute-start(bf16[16,2048]{1,0:T(8,128)(2,1)} %get-tuple-element.53), channel_id=1, source_target_pairs={{0,3},{1,0},{2,1},{3,2},{4,7},{5,4},{6,5},{7,6},{8,11},{9,8},{10,9... | collective-permute-start | bytes 196616 | tf_op jit(solution)/shard_map/ppermute | solution.py:556
  132.6 74.6 %all-to-all-start.1 = ((bf16[128,8,2304]{2,1,0:T(8,128)(2,1)}), bf16[128,8,2304]{2,1,0:T(8,128)(2,1)}, u32[]{:S(2)}, u32[]{:S(2)}) async-start(bf16[128,8,2304]{2,1,0:T(8,128)(2,1)} %bitcast.22), calls=%async_computation.1 | async-start | bytes 9437184 | tf_op jit(solution)/shard_map/all_to_all | solution.py:561
  228.3 63.3 %copy-start.8 = (s32[128,8]{0,1:T(8,128)S(1)}, s32[128,8]{0,1:T(8,128)}, u32[]{:S(2)}) copy-start(s32[128,8]{0,1:T(8,128)} %param.12) | copy-start | bytes 12292
  228.3 91.4 %all-to-all-start.3 = ((bf16[128,8,2304]{2,1,0:T(8,128)(2,1)}), bf16[128,8,2304]{2,1,0:T(8,128)(2,1)}, u32[]{:S(2)}, u32[]{:S(2)}) async-start(bf16[128,8,2304]{2,1,0:T(8,128)(2,1)} %bitcast.21), calls=%async_computation.3 | async-start | bytes 9437184 | tf_op jit(solution)/shard_map/all_to_all | solution.py:561
  238.1 49.0 %collective-permute-start.6 = (bf16[128,256]{1,0:T(8,128)(2,1)}, bf16[128,256]{1,0:T(8,128)(2,1)S(1)}, u32[]{:S(2)}, u32[]{:S(2)}) collective-permute-start(bf16[128,256]{1,0:T(8,128)(2,1)} %get-tuple-element.39), channel_id=1, source_target_pairs={{0,16},{16,32},{32,48},{48,64},{64,80},{80,96},{96,112},{112,0},{1... | collective-permute-start | bytes 196616 | tf_op jit(solution)/shard_map/ppermute | solution.py:556
  239.6 51.7 %collective-permute-start.7 = (bf16[128,256]{1,0:T(8,128)(2,1)}, bf16[128,256]{1,0:T(8,128)(2,1)S(1)}, u32[]{:S(2)}, u32[]{:S(2)}) collective-permute-start(bf16[128,256]{1,0:T(8,128)(2,1)} %get-tuple-element.40), channel_id=1, source_target_pairs={{0,32},{16,48},{32,64},{48,80},{64,96},{80,112},{96,0},{112,16},{1... | collective-permute-start | bytes 196616 | tf_op jit(solution)/shard_map/ppermute | solution.py:556
  240.9 51.5 %collective-permute-start.8 = (bf16[128,256]{1,0:T(8,128)(2,1)}, bf16[128,256]{1,0:T(8,128)(2,1)S(1)}, u32[]{:S(2)}, u32[]{:S(2)}) collective-permute-start(bf16[128,256]{1,0:T(8,128)(2,1)} %get-tuple-element.41), channel_id=1, source_target_pairs={{0,48},{16,64},{32,80},{48,96},{64,112},{80,0},{96,16},{112,32},{1... | collective-permute-start | bytes 196616 | tf_op jit(solution)/shard_map/ppermute | solution.py:556
  242.6 52.0 %collective-permute-start.9 = (bf16[128,256]{1,0:T(8,128)(2,1)}, bf16[128,256]{1,0:T(8,128)(2,1)S(1)}, u32[]{:S(2)}, u32[]{:S(2)}) collective-permute-start(bf16[128,256]{1,0:T(8,128)(2,1)} %get-tuple-element.42), channel_id=1, source_target_pairs={{0,64},{16,80},{32,96},{48,112},{64,0},{80,16},{96,32},{112,48},{1... | collective-permute-start | bytes 196616 | tf_op jit(solution)/shard_map/ppermute | solution.py:556
  243.0 52.0 %collective-permute-start.10 = (bf16[128,256]{1,0:T(8,128)(2,1)}, bf16[128,256]{1,0:T(8,128)(2,1)S(1)}, u32[]{:S(2)}, u32[]{:S(2)}) collective-permute-start(bf16[128,256]{1,0:T(8,128)(2,1)} %get-tuple-element.43), channel_id=1, source_target_pairs={{0,80},{16,96},{32,112},{48,0},{64,16},{80,32},{96,48},{112,64},{1... | collective-permute-start | bytes 196616 | tf_op jit(solution)/shard_map/ppermute | solution.py:556
  287.1 7.9 %collective-permute-start.11 = (bf16[128,256]{1,0:T(8,128)(2,1)}, bf16[128,256]{1,0:T(8,128)(2,1)S(1)}, u32[]{:S(2)}, u32[]{:S(2)}) collective-permute-start(bf16[128,256]{1,0:T(8,128)(2,1)} %get-tuple-element.44), channel_id=1, source_target_pairs={{0,96},{16,112},{32,0},{48,16},{64,32},{80,48},{96,64},{112,80},{1... | collective-permute-start | bytes 196616 | tf_op jit(solution)/shard_map/ppermute | solution.py:556
  291.3 3.9 %collective-permute-start.12 = (bf16[128,256]{1,0:T(8,128)(2,1)}, bf16[128,256]{1,0:T(8,128)(2,1)S(1)}, u32[]{:S(2)}, u32[]{:S(2)}) collective-permute-start(bf16[128,256]{1,0:T(8,128)(2,1)} %get-tuple-element.45), channel_id=1, source_target_pairs={{0,112},{16,0},{32,16},{48,32},{64,48},{80,64},{96,80},{112,96},{1... | collective-permute-start | bytes 196616 | tf_op jit(solution)/shard_map/ppermute | solution.py:556
  (12 other events, 63.0 us)

commit v3 on v1

--- a/solution.py
+++ b/solution.py
@@ -1,4 +1,5 @@
 import functools
+
 import jax
 import jax.numpy as jnp
 from jax import lax
@@ -54,7 +55,21 @@
     )
 
 
-def send_tokens_kernel(ids_ref, tok_ref, out_ref, key_ref):
+def fold_up(ninth, fold_ref):
+    experts, depth = ninth.shape
+    width = depth // MAIN
+    for half in range(width // LANES):
+        for i in range(MAIN):
+            start = i * width + half * LANES
+            fold_ref[half, pl.ds(i, experts, stride=MAIN), :] = ninth[:, start : start + LANES]
+
+
+def write_fold(fold_ref, out_ref):
+    for half in range(fold_ref.shape[0]):
+        out_ref[:, half * LANES : (half + 1) * LANES] = fold_ref[half].astype(B16)
+
+
+def send_tokens_kernel(ids_ref, tok_ref, out_ref, mask_ref, fold_ref):
     j = pl.program_id(0)
     tiles = pl.num_programs(0) - 1
     width = out_ref.shape[1]
@@ -62,60 +77,60 @@
 
     @pl.when(j == 0)
     def _():
-        key_ref[...] = per_slot(slot_keys(ids_ref[...], experts))
-
-    slot = iota(key_ref.shape, 0) % MAIN
+        key = slot_keys(ids_ref[...], experts)
+        slot = iota(mask_ref.shape, 0) % MAIN
+        mask_ref[...] = one_hot(per_slot(key) == slot)
+        fold_up(dot(one_hot(key == MAIN), tok_ref[...]), fold_ref)
 
     @pl.when(j < tiles)
     def _():
         cols = pl.ds(pl.multiple_of(j * width, width), width)
-        out_ref[...] = dot(one_hot(key_ref[...] == slot), tok_ref[:, cols]).astype(B16)
+        out_ref[...] = dot(mask_ref[...], tok_ref[:, cols]).astype(B16)
 
     @pl.when(j == tiles)
     def _():
-        ninth = key_ref[...] == MAIN
-        total = jnp.zeros(out_ref.shape, F32)
-        for i in range(MAIN):
-            total += dot(one_hot(ninth & (slot == i)), tok_ref[:, i * width : (i + 1) * width])
-        out_ref[...] = total.astype(B16)
+        write_fold(fold_ref, out_ref)
 
 
 def send_tokens(ids_t, tokens, experts):
     toks, depth = tokens.shape
     width = depth // MAIN
+    rows = experts * MAIN
     return pl.pallas_call(
         send_tokens_kernel,
         grid=(MAIN + 1,),
         in_specs=[whole(ids_t.shape), whole(tokens.shape)],
-        out_specs=pl.BlockSpec((experts * MAIN, width), lambda j: (0, j)),
-        out_shape=jax.ShapeDtypeStruct((experts * MAIN, depth + width), B16),
-        scratch_shapes=[pltpu.VMEM((experts * MAIN, toks), jnp.int32)],
+        out_specs=pl.BlockSpec((rows, width), lambda j: (0, j)),
+        out_shape=jax.ShapeDtypeStruct((rows, depth + width), B16),
+        scratch_shapes=[
+            pltpu.VMEM((rows, toks), B16),
+            pltpu.VMEM((width // LANES, rows, LANES), F32),
+        ],
         compiler_params=params(),
         name="send_tokens",
     )(ids_t, tokens)
 
 
-def send_grads_kernel(ids_ref, weight_ref, part_ref, out_ref, cot_ref, key_ref, row_ref, rep_ref):
+def send_grads_kernel(
+    ids_ref, weight_ref, part_ref, out_ref, cot_ref, mask_ref, row_ref, rep_ref, fold_ref
+):
     j = pl.program_id(0)
     tiles = pl.num_programs(0) - 1
     width = out_ref.shape[1]
     experts = out_ref.shape[0] // MAIN
-    slots, toks = key_ref.shape
+    slots, toks = mask_ref.shape
 
     @pl.when(j == 0)
     def _():
         ids = ids_ref[...]
-        key = per_slot(slot_keys(ids, experts))
-        key_ref[...] = key
+        key = slot_keys(ids, experts)
         expert = iota((experts, toks), 0)
         weight = jnp.zeros((experts, toks), F32)
         for k in range(ids.shape[0]):
             weight += jnp.where(ids[k : k + 1, :] == expert, weight_ref[k : k + 1, :], 0.0)
-        weight = per_slot(weight)
-        slot = iota((slots, toks), 0) % MAIN
-        main = jnp.sum(jnp.where(key == slot, weight, 0.0), axis=1, keepdims=True)
-        ninth = jnp.sum(jnp.where(key == MAIN, weight, 0.0), axis=1, keepdims=True)
-        row_ref[...] = jnp.where(iota(row_ref.shape, 1) == 0, main, ninth)
+        mine = per_slot(key) == iota((slots, toks), 0) % MAIN
+        mask_ref[...] = one_hot(mine)
+        row_ref[...] = jnp.sum(jnp.where(mine, per_slot(weight), 0.0), axis=1, keepdims=True)
         total = part_ref[0].astype(F32)
         for c in range(1, part_ref.shape[0]):
             total += part_ref[c].astype(F32)
@@ -123,44 +138,42 @@
         cot_ref[...] = cot
         spread = one_hot(iota((toks, cot.shape[0]), 0) // SEQ_LEN == iota((toks, cot.shape[0]), 1))
         rep_ref[...] = dot(spread, cot).astype(B16)
-
-    slot = iota((slots, toks), 0) % MAIN
+        last = key == MAIN
+        ninth = jnp.sum(jnp.where(last, weight, 0.0), axis=1, keepdims=True)
+        fold_up(dot(one_hot(last), rep_ref[...]) * ninth, fold_ref)
 
     @pl.when(j < tiles)
     def _():
         cols = pl.ds(pl.multiple_of(j * width, width), width)
-        rows = dot(one_hot(key_ref[...] == slot), rep_ref[:, cols])
-        out_ref[...] = (rows * row_ref[:, 0:1]).astype(B16)
+        out_ref[...] = (dot(mask_ref[...], rep_ref[:, cols]) * row_ref[...]).astype(B16)
 
     @pl.when(j == tiles)
     def _():
-        ninth = key_ref[...] == MAIN
-        total = jnp.zeros(out_ref.shape, F32)
-        for i in range(MAIN):
-            total += dot(one_hot(ninth & (slot == i)), rep_ref[:, i * width : (i + 1) * width])
-        out_ref[...] = (total * row_ref[:, 1:2]).astype(B16)
+        write_fold(fold_ref, out_ref)
 
 
 def send_grads(ids_t, weights_t, parts, experts):
     toks = ids_t.shape[1]
     _, queries, depth = parts.shape
     width = depth // MAIN
+    rows = experts * MAIN
     return pl.pallas_call(
         send_grads_kernel,
         grid=(MAIN + 1,),
         in_specs=[whole(ids_t.shape), whole(weights_t.shape), whole(parts.shape)],
         out_specs=[
-            pl.BlockSpec((experts * MAIN, width), lambda j: (0, j)),
+            pl.BlockSpec((rows, width), lambda j: (0, j)),
             pl.BlockSpec((queries, depth), lambda j: (0, 0)),
         ],
         out_shape=[
-            jax.ShapeDtypeStruct((experts * MAIN, depth + width), B16),
+            jax.ShapeDtypeStruct((rows, depth + width), B16),
             jax.ShapeDtypeStruct((queries, depth), B16),
         ],
         scratch_shapes=[
-            pltpu.VMEM((experts * MAIN, toks), jnp.int32),
-            pltpu.VMEM((experts * MAIN, 128), F32),
+            pltpu.VMEM((rows, toks), B16),
+            pltpu.VMEM((rows, 1), F32),
             pltpu.VMEM((toks, depth), B16),
+            pltpu.VMEM((width // LANES, rows, LANES), F32),
         ],
         compiler_params=params(),
         name="send_grads",
@@ -358,10 +371,11 @@
     )(a, a9, b, b9)
 
 
-def combine_kernel(ids_ref, cot_ref, got_ref, fold_ref, out_ref, key_ref):
+def combine_kernel(ids_ref, cot_ref, got_ref, fold_ref, out_ref, mask_ref, last_ref, ninth_ref, buf_ref):
     j = pl.program_id(0)
-    toks, slots = key_ref.shape
+    toks, slots = mask_ref.shape
     experts = slots // MAIN
+    width = out_ref.shape[1]
 
     @pl.when(j == 0)
     def _():
@@ -372,16 +386,17 @@
             hit += jnp.where(ids[:, k : k + 1] == expert, 1.0, 0.0)
         earlier = one_hot(iota((toks, toks), 1) < iota((toks, toks), 0))
         rank = dot(earlier, hit.astype(B16))
-        key = jnp.where(hit > 0.0, rank, -1.0).astype(B16)
+        key = jnp.where(hit > 0.0, rank, -1.0)
+        last_ref[...] = one_hot(key == float(MAIN))
         spread = one_hot(iota((experts, slots), 0) == iota((experts, slots), 1) // MAIN)
-        key_ref[...] = dot(key, spread).astype(jnp.int32)
-
-    key = key_ref[...]
-    slot = iota(key.shape, 1) % MAIN
+        slot = (iota((toks, slots), 1) % MAIN).astype(F32)
+        mask_ref[...] = one_hot(dot(key.astype(B16), spread) == slot)
+        unfold(fold_ref[...], buf_ref, ninth_ref)
+
     queries = cot_ref.shape[0]
     spread = one_hot(iota((toks, queries), 0) // SEQ_LEN == iota((toks, queries), 1))
-    total = dot(one_hot(key == slot), got_ref[...])
-    total += dot(one_hot((key == MAIN) & (slot == j)), fold_ref[...])
+    cols = pl.ds(pl.multiple_of(j * width, width), width)
+    total = dot(mask_ref[...], got_ref[...]) + dot(last_ref[...], ninth_ref[:, cols])
     out_ref[...] = (dot(spread, cot_ref[...]) + total).astype(B16)
 
 
@@ -389,22 +404,113 @@
     toks = ids.shape[0]
     queries, depth = cot.shape
     rows = got.shape[0]
-    width = depth // MAIN
+    experts = rows // MAIN
+    fold = depth // MAIN
+    width = 2 * fold
     return pl.pallas_call(
         combine_kernel,
-        grid=(MAIN,),
+        grid=(depth // width,),
         in_specs=[
             whole(ids.shape),
             pl.BlockSpec((queries, width), lambda j: (0, j)),
             pl.BlockSpec((rows, width), lambda j: (0, j)),
-            pl.BlockSpec((rows, width), lambda j: (0, MAIN), pipeline_mode=pl.Buffered(1)),
+            pl.BlockSpec((rows, fold), lambda j: (0, MAIN), pipeline_mode=pl.Buffered(1)),
         ],
         out_specs=pl.BlockSpec((toks, width), lambda j: (0, j)),
         out_shape=jax.ShapeDtypeStruct((toks, depth), B16),
-        scratch_shapes=[pltpu.VMEM((toks, rows), jnp.int32)],
+        scratch_shapes=[
+            pltpu.VMEM((toks, rows), B16),
+            pltpu.VMEM((toks, experts), B16),
+            pltpu.VMEM((experts, depth), B16),
+            pltpu.VMEM((fold // LANES, rows, LANES), F32),
+        ],
         compiler_params=params(),
         name="combine",
     )(ids, cot, got, got)
+
+
+def scores_kernel(query_ref, passage_ref, score_ref, stat_ref):
+    pieces, _, width = passage_ref.shape
+    step = query_ref.shape[2]
+    total = jnp.zeros(score_ref.shape, F32)
+    for r in range(pieces):
+        for h in range(width // step):
+            part = passage_ref[r, :, h * step : (h + 1) * step]
+            total += dot(part, query_ref[r * (width // step) + h], ((1,), (1,)))
+    scores = total / SHARPNESS
+    peak = jnp.max(scores, axis=0, keepdims=True)
+    mass = jnp.sum(jnp.exp(scores - peak), axis=0, keepdims=True)
+    score_ref[...] = scores
+    stat_ref[...] = jnp.where(iota(stat_ref.shape, 0) == 0, peak, mass)
+
+
+def local_scores(queries, passages):
+    shape = (passages.shape[1], queries.shape[1])
+    return pl.pallas_call(
+        scores_kernel,
+        out_shape=[
+            jax.ShapeDtypeStruct(shape, F32),
+            jax.ShapeDtypeStruct((8, shape[1]), F32),
+        ],
+        compiler_params=params(),
+        name="local_scores",
+    )(queries, passages)
+
+
+def query_part_kernel(at_ref, score_ref, stat_ref, pos_ref, passage_ref, out_ref, dscore_ref):
+    parts = [stat_ref[c] for c in range(stat_ref.shape[0])]
+    peak = functools.reduce(jnp.maximum, [p[0:1] for p in parts])
+    mass = sum(p[1:2] * jnp.exp(p[0:1] - peak) for p in parts)
+    column = at_ref[0] + iota(score_ref.shape, 0)
+    chosen = jnp.where(pos_ref[...] == column, 1.0, 0.0)
+    soft = jnp.exp(score_ref[...] - peak) / mass
+    dscore = ((soft - chosen) / SHARPNESS).astype(B16)
+    dscore_ref[...] = dscore
+    pieces, _, width = passage_ref.shape
+    for r in range(pieces):
+        out_ref[:, r * width : (r + 1) * width] = dot(
+            dscore, passage_ref[r], ((0,), (0,))
+        ).astype(B16)
+
+
+def query_part(at, scores, stats, positive, passages):
+    pieces, _, width = passages.shape
+    smem = pl.BlockSpec(memory_space=pltpu.SMEM)
+    vmem = pl.BlockSpec(memory_space=pltpu.VMEM)
+    return pl.pallas_call(
+        query_part_kernel,
+        in_specs=[smem] + [vmem] * 4,
+        out_specs=[vmem] * 2,
+        out_shape=[
+            jax.ShapeDtypeStruct((scores.shape[1], pieces * width), B16),
+            jax.ShapeDtypeStruct(scores.shape, B16),
+        ],
+        compiler_params=params(),
+        name="query_part",
+    )(at, scores, stats, positive, passages)
+
+
+def passage_part_kernel(dscore_ref, query_ref, out_ref):
+    peers, _, width = out_ref.shape
+    pieces, _, step = query_ref.shape
+    for c in range(pieces):
+        at = c * step
+        out_ref[at // width, :, at % width : at % width + step] = dot(
+            dscore_ref[...], query_ref[c]
+        ).astype(B16)
+
+
+def passage_part(dscore, queries, peers):
+    pieces, _, step = queries.shape
+    vmem = pl.BlockSpec(memory_space=pltpu.VMEM)
+    return pl.pallas_call(
+        passage_part_kernel,
+        in_specs=[vmem, vmem],
+        out_specs=vmem,
+        out_shape=jax.ShapeDtypeStruct((peers, dscore.shape[0], pieces * step // peers), B16),
+        compiler_params=params(),
+        name="passage_part",
+    )(dscore, queries)
 
 
 def sent_to_all(value, axis):
@@ -412,17 +518,6 @@
     return lax.all_to_all(
         jnp.broadcast_to(value[None], (peers, *value.shape)), axis, 0, 0, tiled=True
     )
-
-
-def gathered_copies(value, axis):
-    tiles = jnp.moveaxis(sent_to_all(value, axis), 0, 1)
-    return tiles.reshape(tiles.shape[0], -1)
-
-
-def split_up(value, dim, peers):
-    lengths = value.shape
-    tiles = value.reshape(*lengths[:dim], peers, lengths[dim] // peers, *lengths[dim + 1 :])
-    return jnp.moveaxis(tiles, dim, 0)
 
 
 def exchanged(block, experts):
@@ -452,30 +547,25 @@
     ids_t, weights_t = expert_ids.T, route_weights.T
     tokens_out = send_tokens(ids_t, tokens, experts)
 
-    passages = gathered_copies(document_vectors, "row")
-    queries = gathered_copies(question_vectors, "col")
-    scores = dot(queries, passages, ((1,), (1,))) / SHARPNESS
-    local_peak = jnp.max(scores, axis=1)
-    local_total = jnp.sum(jnp.exp(scores - local_peak[:, None]), axis=1)
-    stats = sent_to_all(jnp.stack([local_peak, local_total]), "col")
-    peak = jnp.max(stats[:, 0], axis=0)
-    total = jnp.sum(stats[:, 1] * jnp.exp(stats[:, 0] - peak[None]), axis=0)
-    count = passages.shape[0]
-    columns = lax.axis_index("col") * count + jnp.arange(count, dtype=jnp.int32)
-    chosen = (positive[:, None] == columns[None, :]).astype(F32)
-    dscore = ((jnp.exp(scores - peak[:, None]) / total[:, None] - chosen) / SHARPNESS).astype(B16)
-    query_part = dot(dscore, passages).astype(B16)
-    query_parts = lax.all_to_all(split_up(query_part, 0, col_size), "col", 0, 0, tiled=True)
-
+    passages = lax.all_gather(document_vectors, "row")
+    queries = sent_to_all(question_vectors, "col")
+    scores, stat = local_scores(queries, passages)
+    stats = sent_to_all(stat, "col")
+    at = lax.axis_index("col") * scores.shape[0]
+    part, dscore = query_part(at[None], scores, stats, positive[None], passages)
+    parts = lax.all_to_all(
+        part.reshape(col_size, -1, part.shape[1]), "col", 0, 0, tiled=True
+    )
     slot_inputs = exchanged(tokens_out, experts)
-    grads_out, cot = send_grads(ids_t, weights_t, query_parts, experts)
+    grads_out, cot = send_grads(ids_t, weights_t, parts, experts)
+    pieces = passage_part(dscore, queries, row_size)
+    grads_out, pieces = lax.optimization_barrier((grads_out, pieces))
+    passage_sum = lax.psum_scatter(pieces, "row")
     slot_grads = exchanged(grads_out, experts)
 
-    passage_part = dot(dscore, queries, ((0,), (0,))).astype(B16)
-    passage_parts = lax.all_to_all(split_up(passage_part, 1, row_size), "row", 0, 0, tiled=True)
-    passage_grad = jnp.sum(passage_parts.astype(F32), axis=0)
-
     hid, cg, cu, inputs9 = forward(slot_inputs, gate_up, hidden)
+    cg, passage_sum = lax.optimization_barrier((cg, passage_sum))
+    passage_grad = passage_sum.astype(F32)
     back_out, pre_grad, grads9 = backward(slot_grads, down, cg, cu, gate_up)
     returned = exchanged(back_out, experts)
     down_grad = weight_grad(hid, hid, slot_grads, grads9, down.shape[1], MAIN, 0, "down_grad")

time: 302 us -> 308 us (1.020)
  blocking collectives: 0 us -> 16 us
  between operations: 0.73 us -> 14.1 us
  waiting for transfers between devices: 149 us -> 137 us
  starting transfers between devices: 56.7 us -> 45.3 us
    reduce_scatter x0 -> x1, waiting for transfers between devices: none -> 48.4 us  [shards(): passage_sum = lax.psum_scatter(pieces, 'row')]
    all_to_all x3, waiting for transfers between devices: 119 us -> 76.7 us  [exchanged(): lax.all_to_all(block.reshape(experts, rows // experts, width), ('row', 'c...]
    all_to_all x3 -> x2, waiting for transfers between devices: 26.5 us -> 4.29 us  [sent_to_all(): lax.all_to_all(jnp.broadcast_to(value[None], (peers, *value.shape)), axis...]
    all_gather x0 -> x1, blocking collectives: none -> 16 us  [shards(): passages = lax.all_gather(document_vectors, 'row')]
    pallas_call x1 -> x4, Pallas kernels: 7.78 us -> 13.2 us  [the longest x1 5.57 us: combine(): pl.pallas_call(combine_kernel, grid=(depth // width,), in_specs=[whole(id...]
    all_to_all x3 -> x2, starting transfers between devices: 18.2 us -> 13.9 us  [sent_to_all(): lax.all_to_all(jnp.broadcast_to(value[None], (peers, *value.shape)), axis...]
    all_to_all x2 -> x1, starting transfers between devices: 10.2 us -> 6.14 us  [shards(): lax.all_to_all(part.reshape(col_size, -1, part.shape[1]), 'col', 0, 0, ti...]
    all_to_all x2 -> x1, waiting for transfers between devices: 3.27 us -> 7.18 us  [shards(): lax.all_to_all(part.reshape(col_size, -1, part.shape[1]), 'col', 0, 0, ti...]
  transfers between devices with their start and end apart: 8 -> 7, of which waited for: 7 -> 5; matrix products, arithmetic and copies ran while one was open for 1% -> 0% of each run, Pallas kernels for 25% -> 17%
where the time goes in v3:
time: 308 us; the launch traced here: 305 us
  waiting for transfers between devices  137 us (44%)
  Pallas kernels  84.5 us (27%)
  starting transfers between devices  45.3 us (15%)
  blocking collectives  16 us (5%)
  between operations  14.1 us (5%)
  local copies, waits for them, and re-layouts  6.72 us (2%)
    all_to_all x3, waiting for transfers between devices, exchanged(): lax.all_to_all(block.reshape(experts, rows // experts, width), ('row', 'c...  76.7 us
    reduce_scatter x1, waiting for transfers between devices, shards(): passage_sum = lax.psum_scatter(pieces, 'row')  48.4 us
    all_to_all x3, starting transfers between devices, exchanged(): lax.all_to_all(block.reshape(experts, rows // experts, width), ('row', 'c...  25.2 us
    pallas_call x2, Pallas kernels, weight_grad(): pl.pallas_call(weight_grad_kernel, grid=(columns // tile,), in_specs=[pl....  22.9 us
    pallas_call x1, Pallas kernels, backward(): pl.pallas_call(functools.partial(backward_kernel, first), grid=(first + M...  21.2 us
    all_gather x1, blocking collectives, shards(): passages = lax.all_gather(document_vectors, 'row')  16 us
    all_to_all x2, starting transfers between devices, sent_to_all(): lax.all_to_all(jnp.broadcast_to(value[None], (peers, *value.shape)), axis...  13.9 us
    pallas_call x1, Pallas kernels, forward(): pl.pallas_call(forward_kernel, grid=(tiles,), in_specs=[whole(x.shape), p...  12.8 us
  transfers between devices with their start and end apart: 7, of which 5 were waited for; matrix products, arithmetic and copies ran while one was open for 0% of the time, Pallas kernels for 17%

profile of v3, /device:TPU:37, one launch (start us, length us, event | category | flops | bytes accessed | tf_op | source)
XLA Modules:
  0.0 304.5 jit_solution(9206427548892484756)
XLA Ops:
  7.2 2.0 broadcast_in_dim.25
  9.2 7.3 %all-to-all-start.1 = ((bf16[16,256,128]{2,1,0:T(8,128)(2,1)}), bf16[16,256,128]{2,1,0:T(8,128)(2,1)S(1)}, u32[]{:S(2)}, u32[]{:S(2)}) async-start(bf16[16,256,128]{2,1,0:T(8,128)(2,1)} %broadcast_in_dim.25), calls=%async_computation.1 | async-start | bytes 2097152 | tf_op jit(solution)/shard_map/all_to_all | solution.py:518
  16.5 16.0 %all-gather = bf16[1024,256]{1,0:T(8,128)(2,1)} all-gather(bf16[128,256]{1,0:T(8,128)(2,1)} %param.9), channel_id=2, replica_groups=mesh['row'=8,'col'=16] {'row'}, dimensions={0}, use_global_device_ids=true | all-gather | bytes 589824 | tf_op jit(solution)/shard_map/all_gather | solution.py:550
  33.4 2.5 local_scores.1
  35.9 1.4 broadcast_in_dim.26
  37.2 6.7 %all-to-all-start.2 = ((f32[16,8,256]{2,1,0:T(8,128)}), f32[16,8,256]{2,1,0:T(8,128)S(1)}, u32[]{:S(2)}, u32[]{:S(2)}) async-start(f32[16,8,256]{2,1,0:T(8,128)} %broadcast_in_dim.26), calls=%async_computation.2 | async-start | bytes 262144 | tf_op jit(solution)/shard_map/all_to_all | solution.py:518
  43.9 4.3 %all-to-all-done.2.stat_ref = f32[16,8,256]{2,1,0:T(8,128)S(1)} async-done(((f32[16,8,256]{2,1,0:T(8,128)}), f32[16,8,256]{2,1,0:T(8,128)S(1)}, u32[]{:S(2)}, u32[]{:S(2)}) %all-to-all-start.2) | async-done | bytes 131104 | tf_op jit(solution)/shard_map/all_to_all | solution.py:518
  48.8 2.7 query_part.1
  51.5 6.1 %all-to-all-start.3 = ((bf16[16,16,2048]{2,1,0:T(8,128)(2,1)}), bf16[16,16,2048]{2,1,0:T(8,128)(2,1)S(1)}, u32[]{:S(2)}, u32[]{:S(2)}) async-start(bf16[16,16,2048]{2,1,0:T(8,128)(2,1)} %bitcast.22), calls=%async_computation.3 | async-start | bytes 2097152 | tf_op jit(solution)/shard_map/all_to_all | solution.py:556
  57.6 7.2 %send_tokens.1 = bf16[1024,2304]{1,0:T(8,128)(2,1)} custom-call(s32[8,128]{1,0:T(8,128)} %bitcast.24, bf16[128,2048]{1,0:T(8,128)(2,1)} %tok_ref.1), custom_call_target="tpu_custom_call" | custom-call | tf_op jit(solution)/shard_map/send_tokens/pallas_call | solution.py:99
  64.8 7.2 %all-to-all-done.3.part_ref = bf16[16,16,2048]{2,1,0:T(8,128)(2,1)S(1)} async-done(((bf16[16,16,2048]{2,1,0:T(8,128)(2,1)}), bf16[16,16,2048]{2,1,0:T(8,128)(2,1)S(1)}, u32[]{:S(2)}, u32[]{:S(2)}) %all-to-all-start.3) | async-done | bytes 1048608 | tf_op jit(solution)/shard_map/all_to_all | solution.py:556
  73.0 8.9 %all-to-all-start = ((bf16[128,8,2304]{2,1,0:T(8,128)(2,1)}), bf16[128,8,2304]{2,1,0:T(8,128)(2,1)}, u32[]{:S(2)}, u32[]{:S(2)}) async-start(bf16[128,8,2304]{2,1,0:T(8,128)(2,1)} %bitcast.17), calls=%async_computation | async-start | bytes 9437184 | tf_op jit(solution)/shard_map/all_to_all | solution.py:525
  81.9 2.5 passage_part.1
  84.4 7.3 %send_grads.1 = (bf16[1024,2304]{1,0:T(8,128)(2,1)}, bf16[16,2048]{1,0:T(8,128)(2,1)}) custom-call(s32[8,128]{1,0:T(8,128)} %bitcast.25, f32[8,128]{1,0:T(8,128)} %bitcast.26, bf16[16,16,2048]{2,1,0:T(8,128)(2,1)} %copy-done.1), custom_call_target="tpu_custom_call" | custom-call | tf_op jit(solution)/shard_map/send_grads/pallas_call | solution.py:160
  91.7 45.6 %all-to-all-done = bf16[128,8,2304]{2,1,0:T(8,128)(2,1)} async-done(((bf16[128,8,2304]{2,1,0:T(8,128)(2,1)}), bf16[128,8,2304]{2,1,0:T(8,128)(2,1)}, u32[]{:S(2)}, u32[]{:S(2)}) %all-to-all-start) | async-done | bytes 4718624 | tf_op jit(solution)/shard_map/all_to_all | solution.py:525
  137.3 7.3 %all-to-all-start.4 = ((bf16[128,8,2304]{2,1,0:T(8,128)(2,1)}), bf16[128,8,2304]{2,1,0:T(8,128)(2,1)}, u32[]{:S(2)}, u32[]{:S(2)}) async-start(bf16[128,8,2304]{2,1,0:T(8,128)(2,1)} %bitcast.20), calls=%async_computation.5 | async-start | bytes 9437184 | tf_op jit(solution)/shard_map/all_to_all | solution.py:525
  145.3 12.8 %expert_forward.1 = (bf16[1152,768]{1,0:T(8,128)(2,1)}, bf16[1152,768]{1,0:T(8,128)(2,1)}, bf16[1152,768]{1,0:T(8,128)(2,1)}, bf16[128,2048]{1,0:T(8,128)(2,1)}) custom-call(bf16[1024,2304]{1,0:T(8,128)(2,1)} %bitcast.2.x_ref.a_ref, bf16[2048,1536]{1,0:T(8,128)(2,1)} %bitcast.28, bf16[2048,1536]{1,0:T(8,128)(2,1)} %bitcast.29), custom_call_target="tpu_custom_call" | custom-call | flops 7247757312 | bytes 16318464 | tf_op jit(solution)/shard_map/expert_forward/pallas_call | solution.py:228
  158.1 48.4 %reduce-scatter.2.cloned.1.call-done = bf16[1,128,256]{2,1,0:T(8,128)(2,1)} async-done(((bf16[8,128,256]{2,1,0:T(8,128)(2,1)}), bf16[1,128,256]{2,1,0:T(8,128)(2,1)}) %reduce-scatter.2.cloned.1.call-update) | async-done | bytes 65552 | tf_op jit(solution)/shard_map/reduce_scatter | solution.py:563
  206.5 21.2 %expert_backward.1 = (bf16[1024,2304]{1,0:T(8,128)(2,1)}, bf16[1152,1536]{1,0:T(8,128)(2,1)}, bf16[128,2048]{1,0:T(8,128)(2,1)}) custom-call(bf16[1024,2304]{1,0:T(8,128)(2,1)} %bitcast.11.g_ref.b_ref, bf16[768,2048]{1,0:T(8,128)(2,1)} %bitcast.31, bf16[1152,768]{1,0:T(8,128)(2,1)} %get-tuple-element.31.cg_ref, bf16[1152,768]{1,0:T(8,128)(2,1)} %get-tuple-element.32.cu_ref, ...), custom_call_target="tpu_custom_call" | custom-call | flops 10871635968 | bytes 18874368 | tf_op jit(solution)/shard_map/expert_backward/pallas_call | solution.py:305
  227.7 9.0 %all-to-all-start.5 = ((bf16[128,8,2304]{2,1,0:T(8,128)(2,1)}), bf16[128,8,2304]{2,1,0:T(8,128)(2,1)}, u32[]{:S(2)}, u32[]{:S(2)}) async-start(bf16[128,8,2304]{2,1,0:T(8,128)(2,1)} %bitcast.21), calls=%async_computation.6 | async-start | bytes 9437184 | tf_op jit(solution)/shard_map/all_to_all | solution.py:525
  238.2 9.6 %down_grad.1 = bf16[768,2048]{1,0:T(8,128)(2,1)} custom-call(bf16[1152,768]{1,0:T(8,128)(2,1)} %get-tuple-element.36.a_ref.a9_ref, bf16[1152,768]{1,0:T(8,128)(2,1)} %get-tuple-element.36.a_ref.a9_ref, bf16[1024,2304]{1,0:T(8,128)(2,1)} %bitcast.11.g_ref.b_ref, bf16[128,2048]{1,0:T(8,128)(2,1)} %get-tuple-element.37.b9_ref), custom_call_target="tpu_custom_call" | custom-call | flops 3623878656 | bytes 9633792 | tf_op jit(solution)/shard_map/down_grad/pallas_call | solution.py:351
  247.8 13.2 %gate_up_grad.1 = bf16[2048,1536]{1,0:T(8,128)(2,1)} custom-call(bf16[1024,2304]{1,0:T(8,128)(2,1)} %bitcast.2.x_ref.a_ref, bf16[128,2048]{1,0:T(8,128)(2,1)} %get-tuple-element.34.a9_ref, bf16[1152,1536]{1,0:T(8,128)(2,1)} %get-tuple-element.35.b_ref.b9_ref, bf16[1152,1536]{1,0:T(8,128)(2,1)} %get-tuple-element.35.b_ref.b9_ref), custom_call_target="tpu_custom_call" | custom-call | flops 7247757312 | bytes 14548992 | tf_op jit(solution)/shard_map/gate_up_grad/pallas_call | solution.py:351
  261.0 31.1 %all-to-all-done.5 = bf16[128,8,2304]{2,1,0:T(8,128)(2,1)} async-done(((bf16[128,8,2304]{2,1,0:T(8,128)(2,1)}), bf16[128,8,2304]{2,1,0:T(8,128)(2,1)}, u32[]{:S(2)}, u32[]{:S(2)}) %all-to-all-start.5) | async-done | bytes 4718624 | tf_op jit(solution)/shard_map/all_to_all | solution.py:525
  292.1 5.6 %combine.1 = bf16[128,2048]{1,0:T(8,128)(2,1)} custom-call(s32[128,8]{1,0:T(8,128)} %copy.12.ids_ref, bf16[16,2048]{1,0:T(8,128)(2,1)} %get-tuple-element.29.cot_ref, bf16[1024,2304]{1,0:T(8,128)(2,1)} %bitcast.14.got_ref.fold_ref, bf16[1024,2304]{1,0:T(8,128)(2,1)} %bitcast.14.got_ref.fold_ref), custom_call_target="tpu_custom_call" | custom-call | tf_op jit(solution)/shard_map/combine/pallas_call | solution.py:410
  (16 shorter events, 4.7 us)
Async XLA Ops:
  9.2 23.3 %all-to-all-start.1 = ((bf16[16,256,128]{2,1,0:T(8,128)(2,1)}), bf16[16,256,128]{2,1,0:T(8,128)(2,1)S(1)}, u32[]{:S(2)}, u32[]{:S(2)}) async-start(bf16[16,256,128]{2,1,0:T(8,128)(2,1)} %broadcast_in_dim.25), calls=%async_computation.1 | async-start | bytes 2097152 | tf_op jit(solution)/shard_map/all_to_all | solution.py:518
  32.4 1.0 copy-start
  37.2 10.9 %all-to-all-start.2 = ((f32[16,8,256]{2,1,0:T(8,128)}), f32[16,8,256]{2,1,0:T(8,128)S(1)}, u32[]{:S(2)}, u32[]{:S(2)}) async-start(f32[16,8,256]{2,1,0:T(8,128)} %broadcast_in_dim.26), calls=%async_computation.2 | async-start | bytes 262144 | tf_op jit(solution)/shard_map/all_to_all | solution.py:518
  48.2 0.7 copy-start.2
  51.5 20.5 %all-to-all-start.3 = ((bf16[16,16,2048]{2,1,0:T(8,128)(2,1)}), bf16[16,16,2048]{2,1,0:T(8,128)(2,1)S(1)}, u32[]{:S(2)}, u32[]{:S(2)}) async-start(bf16[16,16,2048]{2,1,0:T(8,128)(2,1)} %bitcast.22), calls=%async_computation.3 | async-start | bytes 2097152 | tf_op jit(solution)/shard_map/all_to_all | solution.py:556
  72.0 1.0 copy-start.1
  73.0 64.3 %all-to-all-start = ((bf16[128,8,2304]{2,1,0:T(8,128)(2,1)}), bf16[128,8,2304]{2,1,0:T(8,128)(2,1)}, u32[]{:S(2)}, u32[]{:S(2)}) async-start(bf16[128,8,2304]{2,1,0:T(8,128)(2,1)} %bitcast.17), calls=%async_computation | async-start | bytes 9437184 | tf_op jit(solution)/shard_map/all_to_all | solution.py:525
  137.3 69.2 %all-to-all-start.4 = ((bf16[128,8,2304]{2,1,0:T(8,128)(2,1)}), bf16[128,8,2304]{2,1,0:T(8,128)(2,1)}, u32[]{:S(2)}, u32[]{:S(2)}) async-start(bf16[128,8,2304]{2,1,0:T(8,128)(2,1)} %bitcast.20), calls=%async_computation.5 | async-start | bytes 9437184 | tf_op jit(solution)/shard_map/all_to_all | solution.py:525
  144.6 61.9 %reduce-scatter.2.cloned.1.call-start = ((), (), s32[]{:S(2)}) async-start(), calls=%async_computation.7 | async-start | bytes 589824 | tf_op jit(solution)/shard_map/reduce_scatter | solution.py:563
  227.7 9.1 %copy-start.4 = (s32[128,8]{0,1:T(8,128)S(1)}, s32[128,8]{0,1:T(8,128)}, u32[]{:S(2)}) copy-start(s32[128,8]{0,1:T(8,128)} %param.12) | copy-start | bytes 12292
  227.7 9.8 %copy-start.3 = (bf16[1,128,256]{2,1,0:T(8,128)(2,1)S(1)}, bf16[1,128,256]{2,1,0:T(8,128)(2,1)}, u32[]{:S(2)}) copy-start(bf16[1,128,256]{2,1,0:T(8,128)(2,1)} %reduce-scatter.2.cloned.1.call-done) | copy-start | bytes 196612
  227.7 64.4 %all-to-all-start.5 = ((bf16[128,8,2304]{2,1,0:T(8,128)(2,1)}), bf16[128,8,2304]{2,1,0:T(8,128)(2,1)}, u32[]{:S(2)}, u32[]{:S(2)}) async-start(bf16[128,8,2304]{2,1,0:T(8,128)(2,1)} %bitcast.21), calls=%async_computation.6 | async-start | bytes 9437184 | tf_op jit(solution)/shard_map/all_to_all | solution.py:525
Sparse Core Ops, SparseCore 0:
  148.3 58.0 reduce-scatter.1

commit v4 on v3

--- a/solution.py
+++ b/solution.py
@@ -13,15 +13,14 @@
 LANES = 128
 B16 = jnp.bfloat16
 F32 = jnp.float32
-VMEM_LIMIT = 56 * 1024 * 1024
 
 
 def iota(shape, dim):
     return lax.broadcasted_iota(jnp.int32, shape, dim)
 
 
-def params():
-    return pltpu.CompilerParams(vmem_limit_bytes=VMEM_LIMIT)
+def params(mib=56):
+    return pltpu.CompilerParams(vmem_limit_bytes=mib * 1024 * 1024)
 
 
 def whole(shape):
@@ -106,13 +105,13 @@
             pltpu.VMEM((rows, toks), B16),
             pltpu.VMEM((width // LANES, rows, LANES), F32),
         ],
-        compiler_params=params(),
+        compiler_params=params(24),
         name="send_tokens",
     )(ids_t, tokens)
 
 
 def send_grads_kernel(
-    ids_ref, weight_ref, part_ref, out_ref, cot_ref, mask_ref, row_ref, rep_ref, fold_ref
+    ids_ref, weight_ref, part_hbm, out_ref, cot_ref, mask_ref, row_ref, rep_ref, fold_ref, part_ref
 ):
     j = pl.program_id(0)
     tiles = pl.num_programs(0) - 1
@@ -122,6 +121,7 @@
 
     @pl.when(j == 0)
     def _():
+        pltpu.sync_copy(part_hbm, part_ref)
         ids = ids_ref[...]
         key = slot_keys(ids, experts)
         expert = iota((experts, toks), 0)
@@ -160,7 +160,11 @@
     return pl.pallas_call(
         send_grads_kernel,
         grid=(MAIN + 1,),
-        in_specs=[whole(ids_t.shape), whole(weights_t.shape), whole(parts.shape)],
+        in_specs=[
+            whole(ids_t.shape),
+            whole(weights_t.shape),
+            pl.BlockSpec(memory_space=pl.ANY),
+        ],
         out_specs=[
             pl.BlockSpec((rows, width), lambda j: (0, j)),
             pl.BlockSpec((queries, depth), lambda j: (0, 0)),
@@ -174,8 +178,9 @@
             pltpu.VMEM((rows, 1), F32),
             pltpu.VMEM((toks, depth), B16),
             pltpu.VMEM((width // LANES, rows, LANES), F32),
-        ],
-        compiler_params=params(),
+            pltpu.VMEM(parts.shape, B16),
+        ],
+        compiler_params=params(24),
         name="send_grads",
     )(ids_t, weights_t, parts)
 
@@ -247,7 +252,7 @@
 
 
 def backward_kernel(
-    first, g_ref, down_ref, cg_ref, cu_ref, w_ref, out_ref, pg_ref, g9_ref, fold_ref
+    first, g_ref, down_ref, cg_ref, cu_ref, w_ref, out_ref, pair_ref, g9_ref, pg_ref, fold_ref
 ):
     j = pl.program_id(0)
     rows = g_ref.shape[0]
@@ -257,6 +262,7 @@
     tile = down_ref.shape[0]
     hidden = pg_ref.shape[1] // 2
 
+
     @pl.when(j == 0)
     def _():
         unfold(g_ref[:, depth:], fold_ref, g9_ref)
@@ -266,8 +272,12 @@
         def finish(at, grad):
             gate_cols = pl.ds(pl.multiple_of(j * tile, tile), tile)
             up_cols = pl.ds(pl.multiple_of(hidden + j * tile, tile), tile)
-            pg_ref[at, gate_cols] = (grad * cg_ref[at, :].astype(F32)).astype(B16)
-            pg_ref[at, up_cols] = (grad * cu_ref[at, :].astype(F32)).astype(B16)
+            gate = (grad * cg_ref[at, :].astype(F32)).astype(B16)
+            up = (grad * cu_ref[at, :].astype(F32)).astype(B16)
+            pg_ref[at, gate_cols] = gate
+            pg_ref[at, up_cols] = up
+            pair_ref[at, :tile] = gate
+            pair_ref[at, tile:] = up
 
         step = rows // 4
         for m in range(4):
@@ -277,11 +287,9 @@
 
     @pl.when((j >= first) & (j < first + MAIN))
     def _():
-        step = rows // 4
-        for m in range(4):
-            at = slice(m * step, (m + 1) * step)
-            out_ref[at, :] = dot(pg_ref[at, :], w_ref[...], ((1,), (1,))).astype(B16)
-        ninth = dot(pg_ref[rows:total, :], w_ref[...], ((1,), (1,)))
+        grads = dot(pg_ref[...], w_ref[...], ((1,), (1,)))
+        out_ref[...] = grads[:rows].astype(B16)
+        ninth = grads[rows:]
         for half in range(width // LANES):
             fold_ref[half, pl.ds(j - first, sources, stride=MAIN), :] = ninth[
                 :, half * LANES : (half + 1) * LANES
@@ -316,7 +324,7 @@
         ],
         out_specs=[
             pl.BlockSpec((rows, width), lambda j: (0, jnp.maximum(j - first, 0))),
-            pl.BlockSpec((rows + sources, 2 * hidden), lambda j: (0, 0)),
+            pl.BlockSpec((rows + sources, 2 * tile), head),
             pl.BlockSpec((sources, depth), lambda j: (0, 0)),
         ],
         out_shape=[
@@ -324,7 +332,10 @@
             jax.ShapeDtypeStruct((rows + sources, 2 * hidden), B16),
             jax.ShapeDtypeStruct((sources, depth), B16),
         ],
-        scratch_shapes=[pltpu.VMEM((width // LANES, rows, LANES), F32)],
+        scratch_shapes=[
+            pltpu.VMEM((rows + sources, 2 * hidden), B16),
+            pltpu.VMEM((width // LANES, rows, LANES), F32),
+        ],
         compiler_params=params(),
         cost_estimate=pl.CostEstimate(
             flops=6 * (rows + sources) * depth * hidden,
@@ -343,11 +354,13 @@
     ).astype(B16)
 
 
-def weight_grad(a, a9, b, b9, columns, a9_block, b9_block, name):
+def weight_grad(a, a9, b, b9, columns, a9_block, b9_block, name, pairs=False):
     sources = a9.shape[0] if a9_block == 0 else a.shape[0] - 8 * (a.shape[0] // 9)
     rows = sources * MAIN
     width = a9.shape[1]
     tile = 256
+    half = columns // tile // 2
+    place = (lambda j: (0, j // 2 + (j % 2) * half)) if pairs else (lambda j: (0, j))
     return pl.pallas_call(
         weight_grad_kernel,
         grid=(columns // tile,),
@@ -359,7 +372,7 @@
             pl.BlockSpec((rows, tile), lambda j: (0, j)),
             pl.BlockSpec((sources, tile), lambda j: (b9_block, j)),
         ],
-        out_specs=pl.BlockSpec((width, tile), lambda j: (0, j)),
+        out_specs=pl.BlockSpec((width, tile), place),
         out_shape=jax.ShapeDtypeStruct((width, columns), B16),
         compiler_params=params(),
         cost_estimate=pl.CostEstimate(
@@ -371,26 +384,43 @@
     )(a, a9, b, b9)
 
 
-def combine_kernel(ids_ref, cot_ref, got_ref, fold_ref, out_ref, mask_ref, last_ref, ninth_ref, buf_ref):
-    j = pl.program_id(0)
+def plan_kernel(ids_ref, mask_ref, last_ref):
     toks, slots = mask_ref.shape
     experts = slots // MAIN
+    ids = ids_ref[...]
+    expert = iota((toks, experts), 1)
+    hit = jnp.zeros((toks, experts), F32)
+    for k in range(ids.shape[1]):
+        hit += jnp.where(ids[:, k : k + 1] == expert, 1.0, 0.0)
+    earlier = one_hot(iota((toks, toks), 1) < iota((toks, toks), 0))
+    rank = dot(earlier, hit.astype(B16))
+    key = jnp.where(hit > 0.0, rank, -1.0)
+    last_ref[...] = one_hot(key == float(MAIN))
+    spread = one_hot(iota((experts, slots), 0) == iota((experts, slots), 1) // MAIN)
+    slot = (iota((toks, slots), 1) % MAIN).astype(F32)
+    mask_ref[...] = one_hot(dot(key.astype(B16), spread) == slot)
+
+
+def combine_plan(ids, experts):
+    toks = ids.shape[0]
+    return pl.pallas_call(
+        plan_kernel,
+        out_shape=[
+            jax.ShapeDtypeStruct((toks, experts * MAIN), B16),
+            jax.ShapeDtypeStruct((toks, experts), B16),
+        ],
+        compiler_params=params(16),
+        name="combine_plan",
+    )(ids)
+
+
+def combine_kernel(mask_ref, last_ref, cot_ref, got_ref, fold_ref, out_ref, ninth_ref, buf_ref):
+    j = pl.program_id(0)
+    toks = mask_ref.shape[0]
     width = out_ref.shape[1]
 
     @pl.when(j == 0)
     def _():
-        ids = ids_ref[...]
-        expert = iota((toks, experts), 1)
-        hit = jnp.zeros((toks, experts), F32)
-        for k in range(ids.shape[1]):
-            hit += jnp.where(ids[:, k : k + 1] == expert, 1.0, 0.0)
-        earlier = one_hot(iota((toks, toks), 1) < iota((toks, toks), 0))
-        rank = dot(earlier, hit.astype(B16))
-        key = jnp.where(hit > 0.0, rank, -1.0)
-        last_ref[...] = one_hot(key == float(MAIN))
-        spread = one_hot(iota((experts, slots), 0) == iota((experts, slots), 1) // MAIN)
-        slot = (iota((toks, slots), 1) % MAIN).astype(F32)
-        mask_ref[...] = one_hot(dot(key.astype(B16), spread) == slot)
         unfold(fold_ref[...], buf_ref, ninth_ref)
 
     queries = cot_ref.shape[0]
@@ -400,18 +430,19 @@
     out_ref[...] = (dot(spread, cot_ref[...]) + total).astype(B16)
 
 
-def combine(ids, cot, got):
-    toks = ids.shape[0]
+def combine(plan, cot, got):
+    mask, last = plan
+    toks, experts = last.shape
     queries, depth = cot.shape
     rows = got.shape[0]
-    experts = rows // MAIN
     fold = depth // MAIN
     width = 2 * fold
     return pl.pallas_call(
         combine_kernel,
         grid=(depth // width,),
         in_specs=[
-            whole(ids.shape),
+            whole(mask.shape),
+            whole(last.shape),
             pl.BlockSpec((queries, width), lambda j: (0, j)),
             pl.BlockSpec((rows, width), lambda j: (0, j)),
             pl.BlockSpec((rows, fold), lambda j: (0, MAIN), pipeline_mode=pl.Buffered(1)),
@@ -419,17 +450,16 @@
         out_specs=pl.BlockSpec((toks, width), lambda j: (0, j)),
         out_shape=jax.ShapeDtypeStruct((toks, depth), B16),
         scratch_shapes=[
-            pltpu.VMEM((toks, rows), B16),
-            pltpu.VMEM((toks, experts), B16),
             pltpu.VMEM((experts, depth), B16),
             pltpu.VMEM((fold // LANES, rows, LANES), F32),
         ],
-        compiler_params=params(),
+        compiler_params=params(32),
         name="combine",
-    )(ids, cot, got, got)
-
-
-def scores_kernel(query_ref, passage_ref, score_ref, stat_ref):
+    )(mask, last, cot, got, got)
+
+
+def scores_kernel(query_hbm, passage_ref, score_ref, stat_ref, query_ref):
+    pltpu.sync_copy(query_hbm, query_ref)
     pieces, _, width = passage_ref.shape
     step = query_ref.shape[2]
     total = jnp.zeros(score_ref.shape, F32)
@@ -448,16 +478,21 @@
     shape = (passages.shape[1], queries.shape[1])
     return pl.pallas_call(
         scores_kernel,
+        in_specs=[pl.BlockSpec(memory_space=pl.ANY), pl.BlockSpec(memory_space=pltpu.VMEM)],
+        scratch_shapes=[pltpu.VMEM(queries.shape, B16)],
         out_shape=[
             jax.ShapeDtypeStruct(shape, F32),
-            jax.ShapeDtypeStruct((8, shape[1]), F32),
-        ],
-        compiler_params=params(),
+            jax.ShapeDtypeStruct((2, shape[1]), F32),
+        ],
+        compiler_params=params(16),
         name="local_scores",
     )(queries, passages)
 
 
-def query_part_kernel(at_ref, score_ref, stat_ref, pos_ref, passage_ref, out_ref, dscore_ref):
+def query_part_kernel(
+    at_ref, score_ref, stat_hbm, pos_ref, passage_ref, out_ref, dscore_ref, stat_ref
+):
+    pltpu.sync_copy(stat_hbm, stat_ref)
     parts = [stat_ref[c] for c in range(stat_ref.shape[0])]
     peak = functools.reduce(jnp.maximum, [p[0:1] for p in parts])
     mass = sum(p[1:2] * jnp.exp(p[0:1] - peak) for p in parts)
@@ -479,18 +514,20 @@
     vmem = pl.BlockSpec(memory_space=pltpu.VMEM)
     return pl.pallas_call(
         query_part_kernel,
-        in_specs=[smem] + [vmem] * 4,
+        in_specs=[smem, vmem, pl.BlockSpec(memory_space=pl.ANY), vmem, vmem],
         out_specs=[vmem] * 2,
+        scratch_shapes=[pltpu.VMEM(stats.shape, F32)],
         out_shape=[
             jax.ShapeDtypeStruct((scores.shape[1], pieces * width), B16),
             jax.ShapeDtypeStruct(scores.shape, B16),
         ],
-        compiler_params=params(),
+        compiler_params=params(16),
         name="query_part",
     )(at, scores, stats, positive, passages)
 
 
-def passage_part_kernel(dscore_ref, query_ref, out_ref):
+def passage_part_kernel(dscore_ref, query_hbm, out_ref, query_ref):
+    pltpu.sync_copy(query_hbm, query_ref)
     peers, _, width = out_ref.shape
     pieces, _, step = query_ref.shape
     for c in range(pieces):
@@ -505,10 +542,11 @@
     vmem = pl.BlockSpec(memory_space=pltpu.VMEM)
     return pl.pallas_call(
         passage_part_kernel,
-        in_specs=[vmem, vmem],
+        in_specs=[vmem, pl.BlockSpec(memory_space=pl.ANY)],
         out_specs=vmem,
+        scratch_shapes=[pltpu.VMEM(queries.shape, B16)],
         out_shape=jax.ShapeDtypeStruct((peers, dscore.shape[0], pieces * step // peers), B16),
-        compiler_params=params(),
+        compiler_params=params(16),
         name="passage_part",
     )(dscore, queries)
 
@@ -559,20 +597,20 @@
     slot_inputs = exchanged(tokens_out, experts)
     grads_out, cot = send_grads(ids_t, weights_t, parts, experts)
     pieces = passage_part(dscore, queries, row_size)
-    grads_out, pieces = lax.optimization_barrier((grads_out, pieces))
-    passage_sum = lax.psum_scatter(pieces, "row")
     slot_grads = exchanged(grads_out, experts)
 
+    plan = combine_plan(expert_ids, experts)
     hid, cg, cu, inputs9 = forward(slot_inputs, gate_up, hidden)
-    cg, passage_sum = lax.optimization_barrier((cg, passage_sum))
-    passage_grad = passage_sum.astype(F32)
+    pieces, cg, plan = lax.optimization_barrier((pieces, cg, plan))
+    passage_parts = lax.all_to_all(pieces, "row", 0, 0, tiled=True)
+    passage_grad = jnp.sum(passage_parts.astype(F32), axis=0)
     back_out, pre_grad, grads9 = backward(slot_grads, down, cg, cu, gate_up)
     returned = exchanged(back_out, experts)
     down_grad = weight_grad(hid, hid, slot_grads, grads9, down.shape[1], MAIN, 0, "down_grad")
     gate_up_grad = weight_grad(
-        slot_inputs, inputs9, pre_grad, pre_grad, 2 * hidden, 0, MAIN, "gate_up_grad"
+        slot_inputs, inputs9, pre_grad, pre_grad, 2 * hidden, 0, MAIN, "gate_up_grad", True
     )
-    token_grad = combine(expert_ids, cot, returned)
+    token_grad = combine(plan, cot, returned)
     return (passage_grad, token_grad, gate_up_grad[None], down_grad[None])
 
 

time: 308 us -> 284 us (0.922)
  between operations: 14.1 us -> 0.76 us
  Pallas kernels: 84.5 us -> 72.5 us
  starting transfers between devices: 45.3 us -> 49.6 us
    reduce_scatter x1 -> x0, waiting for transfers between devices: 48.4 us -> none  [shards(): passage_sum = lax.psum_scatter(pieces, 'row')]
    all_to_all x3, waiting for transfers between devices: 76.7 us -> 122 us  [exchanged(): lax.all_to_all(block.reshape(experts, rows // experts, width), ('row', 'c...]
    pallas_call x4 -> x5, Pallas kernels: 13.2 us -> 8.96 us  [the longest x1 5 us: combine(): pl.pallas_call(combine_kernel, grid=(depth // width,), in_specs=[whole(ma...]
    all_to_all x0 -> x1, starting transfers between devices: none -> 3.86 us  [shards(): passage_parts = lax.all_to_all(pieces, 'row', 0, 0, tiled=True)]
    pallas_call x1, Pallas kernels: 7.18 us -> 3.37 us  [send_tokens(): pl.pallas_call(send_tokens_kernel, grid=(MAIN + 1,), in_specs=[whole(ids_...]
    pallas_call x1, Pallas kernels: 7.29 us -> 3.83 us  [send_grads(): pl.pallas_call(send_grads_kernel, grid=(MAIN + 1,), in_specs=[whole(ids_t...]
  transfers between devices with their start and end apart: 7 -> 7, of which waited for: 5 -> 5; matrix products, arithmetic and copies ran while one was open for 0% -> 0% of each run, Pallas kernels for 17% -> 23%
where the time goes in v4:
time: 284 us; the launch traced here: 280 us
  waiting for transfers between devices  135 us (48%)
  Pallas kernels  72.5 us (26%)
  starting transfers between devices  49.6 us (17%)
  blocking collectives  14.9 us (5%)
  local copies, waits for them, and re-layouts  7.17 us (3%)
    all_to_all x3, waiting for transfers between devices, exchanged(): lax.all_to_all(block.reshape(experts, rows // experts, width), ('row', 'c...  122 us
    all_to_all x3, starting transfers between devices, exchanged(): lax.all_to_all(block.reshape(experts, rows // experts, width), ('row', 'c...  25.7 us
    pallas_call x2, Pallas kernels, weight_grad(): pl.pallas_call(weight_grad_kernel, grid=(columns // tile,), in_specs=[pl....  22.9 us
    pallas_call x1, Pallas kernels, backward(): pl.pallas_call(functools.partial(backward_kernel, first), grid=(first + M...  20.6 us
    all_gather x1, blocking collectives, shards(): passages = lax.all_gather(document_vectors, 'row')  14.9 us
    all_to_all x2, starting transfers between devices, sent_to_all(): lax.all_to_all(jnp.broadcast_to(value[None], (peers, *value.shape)), axis...  13.9 us
    pallas_call x1, Pallas kernels, forward(): pl.pallas_call(forward_kernel, grid=(tiles,), in_specs=[whole(x.shape), p...  12.8 us
    all_to_all x1, waiting for transfers between devices, shards(): lax.all_to_all(part.reshape(col_size, -1, part.shape[1]), 'col', 0, 0, ti...  8.83 us
  transfers between devices with their start and end apart: 7, of which 5 were waited for; matrix products, arithmetic and copies ran while one was open for 0% of the time, Pallas kernels for 23%

profile of v4, /device:TPU:37, one launch (start us, length us, event | category | flops | bytes accessed | tf_op | source)
XLA Modules:
  0.0 280.1 jit_solution(5784154414399788288)
XLA Ops:
  0.7 2.1 broadcast_in_dim.25
  2.7 7.3 %all-to-all-start = ((bf16[16,256,128]{2,1,0:T(8,128)(2,1)}), bf16[16,256,128]{2,1,0:T(8,128)(2,1)S(1)}, u32[]{:S(2)}, u32[]{:S(2)}) async-start(bf16[16,256,128]{2,1,0:T(8,128)(2,1)} %broadcast_in_dim.25), calls=%async_computation | async-start | bytes 2097152 | tf_op jit(solution)/shard_map/all_to_all | solution.py:556
  10.0 14.9 %all-gather = bf16[1024,256]{1,0:T(8,128)(2,1)S(1)} all-gather(bf16[128,256]{1,0:T(8,128)(2,1)} %param.9), channel_id=2, replica_groups=mesh['row'=8,'col'=16] {'row'}, dimensions={0}, use_global_device_ids=true | all-gather | bytes 589824 | tf_op jit(solution)/shard_map/all_gather | solution.py:588
  26.1 6.7 %all-to-all-start.1 = ((f32[16,2,256]{2,1,0:T(2,128)}), f32[16,2,256]{2,1,0:T(2,128)S(1)}, u32[]{:S(2)}, u32[]{:S(2)}) async-start(f32[16,2,256]{2,1,0:T(2,128)} %broadcast_in_dim.26), calls=%async_computation.1 | async-start | bytes 65536 | tf_op jit(solution)/shard_map/all_to_all | solution.py:556
  32.8 4.0 %all-to-all-done.1.stat_hbm = f32[16,2,256]{2,1,0:T(2,128)S(1)} async-done(((f32[16,2,256]{2,1,0:T(2,128)}), f32[16,2,256]{2,1,0:T(2,128)S(1)}, u32[]{:S(2)}, u32[]{:S(2)}) %all-to-all-start.1) | async-done | bytes 32800 | tf_op jit(solution)/shard_map/all_to_all | solution.py:556
  36.7 1.5 query_part.1
  38.2 6.1 %all-to-all-start.4 = ((bf16[16,16,2048]{2,1,0:T(8,128)(2,1)}), bf16[16,16,2048]{2,1,0:T(8,128)(2,1)S(1)}, u32[]{:S(2)}, u32[]{:S(2)}) async-start(bf16[16,16,2048]{2,1,0:T(8,128)(2,1)} %bitcast.8), calls=%async_computation.4 | async-start | bytes 2097152 | tf_op jit(solution)/shard_map/all_to_all | solution.py:594
  44.3 3.4 %send_tokens.1 = bf16[1024,2304]{1,0:T(8,128)(2,1)S(1)} custom-call(s32[8,128]{1,0:T(8,128)S(1)} %bitcast.20, bf16[128,2048]{1,0:T(8,128)(2,1)S(1)} %copy-done.2), custom_call_target="tpu_custom_call" | custom-call | tf_op jit(solution)/shard_map/send_tokens/pallas_call | solution.py:98
  47.7 2.2 copy-done
  49.9 8.8 %all-to-all-done.4.part_hbm = bf16[16,16,2048]{2,1,0:T(8,128)(2,1)S(1)} async-done(((bf16[16,16,2048]{2,1,0:T(8,128)(2,1)}), bf16[16,16,2048]{2,1,0:T(8,128)(2,1)S(1)}, u32[]{:S(2)}, u32[]{:S(2)}) %all-to-all-start.4) | async-done | bytes 1048608 | tf_op jit(solution)/shard_map/all_to_all | solution.py:594
  58.7 9.2 %all-to-all-start.2 = ((bf16[128,8,2304]{2,1,0:T(8,128)(2,1)}), bf16[128,8,2304]{2,1,0:T(8,128)(2,1)}, u32[]{:S(2)}, u32[]{:S(2)}) async-start(bf16[128,8,2304]{2,1,0:T(8,128)(2,1)} %bitcast.16), calls=%async_computation.2 | async-start | bytes 9437184 | tf_op jit(solution)/shard_map/all_to_all | solution.py:563
  68.0 3.8 %send_grads.1 = (bf16[1024,2304]{1,0:T(8,128)(2,1)S(1)}, bf16[16,2048]{1,0:T(8,128)(2,1)S(1)}) custom-call(s32[8,128]{1,0:T(8,128)S(1)} %bitcast.21, f32[8,128]{1,0:T(8,128)S(1)} %bitcast.22, bf16[16,16,2048]{2,1,0:T(8,128)(2,1)S(1)} %all-to-all-done.4.part_hbm), custom_call_target="tpu_custom_call" | custom-call | tf_op jit(solution)/shard_map/send_grads/pallas_call | solution.py:160
  71.8 2.2 copy-done.1
  74.0 49.4 %all-to-all-done.2 = bf16[128,8,2304]{2,1,0:T(8,128)(2,1)} async-done(((bf16[128,8,2304]{2,1,0:T(8,128)(2,1)}), bf16[128,8,2304]{2,1,0:T(8,128)(2,1)}, u32[]{:S(2)}, u32[]{:S(2)}) %all-to-all-start.2) | async-done | bytes 4718624 | tf_op jit(solution)/shard_map/all_to_all | solution.py:563
  123.3 7.3 %all-to-all-start.5 = ((bf16[128,8,2304]{2,1,0:T(8,128)(2,1)}), bf16[128,8,2304]{2,1,0:T(8,128)(2,1)}, u32[]{:S(2)}, u32[]{:S(2)}) async-start(bf16[128,8,2304]{2,1,0:T(8,128)(2,1)} %bitcast.19), calls=%async_computation.5 | async-start | bytes 9437184 | tf_op jit(solution)/shard_map/all_to_all | solution.py:563
  132.6 12.8 %expert_forward.1 = (bf16[1152,768]{1,0:T(8,128)(2,1)}, bf16[1152,768]{1,0:T(8,128)(2,1)}, bf16[1152,768]{1,0:T(8,128)(2,1)}, bf16[128,2048]{1,0:T(8,128)(2,1)}) custom-call(bf16[1024,2304]{1,0:T(8,128)(2,1)} %bitcast.5.x_ref.a_ref, bf16[2048,1536]{1,0:T(8,128)(2,1)} %bitcast.25, bf16[2048,1536]{1,0:T(8,128)(2,1)} %bitcast.26), custom_call_target="tpu_custom_call" | custom-call | flops 7247757312 | bytes 16318464 | tf_op jit(solution)/shard_map/expert_forward/pallas_call | solution.py:233
  145.4 40.6 %all-to-all-done.5 = bf16[128,8,2304]{2,1,0:T(8,128)(2,1)} async-done(((bf16[128,8,2304]{2,1,0:T(8,128)(2,1)}), bf16[128,8,2304]{2,1,0:T(8,128)(2,1)}, u32[]{:S(2)}, u32[]{:S(2)}) %all-to-all-start.5) | async-done | bytes 4718624 | tf_op jit(solution)/shard_map/all_to_all | solution.py:563
  186.0 3.9 %all-to-all-start.3 = ((bf16[8,128,256]{2,1,0:T(8,128)(2,1)}), bf16[8,128,256]{2,1,0:T(8,128)(2,1)S(1)}, u32[]{:S(2)}, u32[]{:S(2)}) async-start(bf16[8,128,256]{2,1,0:T(8,128)(2,1)} %passage_part.1), calls=%async_computation.3 | async-start | bytes 1048576 | tf_op jit(solution)/shard_map/all_to_all | solution.py:605
  189.9 20.6 %expert_backward.1 = (bf16[1024,2304]{1,0:T(8,128)(2,1)}, bf16[1152,1536]{1,0:T(8,128)(2,1)}, bf16[128,2048]{1,0:T(8,128)(2,1)}) custom-call(bf16[1024,2304]{1,0:T(8,128)(2,1)} %bitcast.10.g_ref.b_ref, bf16[768,2048]{1,0:T(8,128)(2,1)} %bitcast.28, bf16[1152,768]{1,0:T(8,128)(2,1)} %get-tuple-element.35.cg_ref, bf16[1152,768]{1,0:T(8,128)(2,1)} %get-tuple-element.36.cu_ref, ...), custom_call_target="tpu_custom_call" | custom-call | flops 10871635968 | bytes 18874368 | tf_op jit(solution)/shard_map/expert_backward/pallas_call | solution.py:313
  210.5 9.2 %all-to-all-start.6 = ((bf16[128,8,2304]{2,1,0:T(8,128)(2,1)}), bf16[128,8,2304]{2,1,0:T(8,128)(2,1)}, u32[]{:S(2)}, u32[]{:S(2)}) async-start(bf16[128,8,2304]{2,1,0:T(8,128)(2,1)} %bitcast.24), calls=%async_computation.6 | async-start | bytes 9437184 | tf_op jit(solution)/shard_map/all_to_all | solution.py:563
  220.4 9.6 %down_grad.1 = bf16[768,2048]{1,0:T(8,128)(2,1)} custom-call(bf16[1152,768]{1,0:T(8,128)(2,1)} %get-tuple-element.40.a_ref.a9_ref, bf16[1152,768]{1,0:T(8,128)(2,1)} %get-tuple-element.40.a_ref.a9_ref, bf16[1024,2304]{1,0:T(8,128)(2,1)} %bitcast.10.g_ref.b_ref, bf16[128,2048]{1,0:T(8,128)(2,1)} %get-tuple-element.41.b9_ref), custom_call_target="tpu_custom_call" | custom-call | flops 3623878656 | bytes 9633792 | tf_op jit(solution)/shard_map/down_grad/pallas_call | solution.py:364
  230.1 13.3 %gate_up_grad.1 = bf16[2048,1536]{1,0:T(8,128)(2,1)} custom-call(bf16[1024,2304]{1,0:T(8,128)(2,1)} %bitcast.5.x_ref.a_ref, bf16[128,2048]{1,0:T(8,128)(2,1)} %get-tuple-element.38.a9_ref, bf16[1152,1536]{1,0:T(8,128)(2,1)} %get-tuple-element.39.b_ref.b9_ref, bf16[1152,1536]{1,0:T(8,128)(2,1)} %get-tuple-element.39.b_ref.b9_ref), custom_call_target="tpu_custom_call" | custom-call | flops 7247757312 | bytes 14548992 | tf_op jit(solution)/shard_map/gate_up_grad/pallas_call | solution.py:364
  243.3 31.8 %all-to-all-done.6 = bf16[128,8,2304]{2,1,0:T(8,128)(2,1)} async-done(((bf16[128,8,2304]{2,1,0:T(8,128)(2,1)}), bf16[128,8,2304]{2,1,0:T(8,128)(2,1)}, u32[]{:S(2)}, u32[]{:S(2)}) %all-to-all-start.6) | async-done | bytes 4718624 | tf_op jit(solution)/shard_map/all_to_all | solution.py:563
  275.1 5.0 %combine.1 = bf16[128,2048]{1,0:T(8,128)(2,1)} custom-call(bf16[128,1024]{1,0:T(8,128)(2,1)S(1)} %get-tuple-element.30.mask_ref, bf16[128,128]{1,0:T(8,128)(2,1)S(1)} %get-tuple-element.31.last_ref, bf16[16,2048]{1,0:T(8,128)(2,1)S(1)} %get-tuple-element.33.cot_ref, bf16[1024,2304]{1,0:T(8,128)(2,1)} %bitcast.13.got_ref.fold_ref, ...), custom_call_target="tpu_custom_call" | custom-call | tf_op jit(solution)/shard_map/combine/pallas_call | solution.py:440
  (18 shorter events, 3.9 us)
Async XLA Ops:
  0.6 36.1 %copy-start.5 = (s32[256]{0:T(256)S(1)}, s32[256]{0:T(256)}, u32[]{:S(2)}) copy-start(s32[256]{0:T(256)} %param.10) | copy-start | bytes 3076
  0.6 43.7 %copy-start.3 = (s32[128,8]{0,1:T(8,128)S(1)}, s32[128,8]{0,1:T(8,128)}, u32[]{:S(2)}) copy-start(s32[128,8]{0,1:T(8,128)} %param.12) | copy-start | bytes 12292
  0.7 43.7 %copy-start.2 = (bf16[128,2048]{1,0:T(8,128)(2,1)S(1)}, bf16[128,2048]{1,0:T(8,128)(2,1)}, u32[]{:S(2)}) copy-start(bf16[128,2048]{1,0:T(8,128)(2,1)} %tok_ref.1) | copy-start | bytes 1572868
  2.7 22.2 %all-to-all-start = ((bf16[16,256,128]{2,1,0:T(8,128)(2,1)}), bf16[16,256,128]{2,1,0:T(8,128)(2,1)S(1)}, u32[]{:S(2)}, u32[]{:S(2)}) async-start(bf16[16,256,128]{2,1,0:T(8,128)(2,1)} %broadcast_in_dim.25), calls=%async_computation | async-start | bytes 2097152 | tf_op jit(solution)/shard_map/all_to_all | solution.py:556
  26.1 10.6 %all-to-all-start.1 = ((f32[16,2,256]{2,1,0:T(2,128)}), f32[16,2,256]{2,1,0:T(2,128)S(1)}, u32[]{:S(2)}, u32[]{:S(2)}) async-start(f32[16,2,256]{2,1,0:T(2,128)} %broadcast_in_dim.26), calls=%async_computation.1 | async-start | bytes 65536 | tf_op jit(solution)/shard_map/all_to_all | solution.py:556
  38.2 20.5 %all-to-all-start.4 = ((bf16[16,16,2048]{2,1,0:T(8,128)(2,1)}), bf16[16,16,2048]{2,1,0:T(8,128)(2,1)S(1)}, u32[]{:S(2)}, u32[]{:S(2)}) async-start(bf16[16,16,2048]{2,1,0:T(8,128)(2,1)} %bitcast.8), calls=%async_computation.4 | async-start | bytes 2097152 | tf_op jit(solution)/shard_map/all_to_all | solution.py:594
  47.7 2.2 copy-start
  58.7 9.2 %copy-start.4 = (f32[128,8]{0,1:T(8,128)S(1)}, f32[128,8]{0,1:T(8,128)}, u32[]{:S(2)}) copy-start(f32[128,8]{0,1:T(8,128)} %param.13) | copy-start | bytes 12292
  58.7 64.6 %all-to-all-start.2 = ((bf16[128,8,2304]{2,1,0:T(8,128)(2,1)}), bf16[128,8,2304]{2,1,0:T(8,128)(2,1)}, u32[]{:S(2)}, u32[]{:S(2)}) async-start(bf16[128,8,2304]{2,1,0:T(8,128)(2,1)} %bitcast.16), calls=%async_computation.2 | async-start | bytes 9437184 | tf_op jit(solution)/shard_map/all_to_all | solution.py:563
  71.8 2.2 copy-start.1
  123.3 62.7 %all-to-all-start.5 = ((bf16[128,8,2304]{2,1,0:T(8,128)(2,1)}), bf16[128,8,2304]{2,1,0:T(8,128)(2,1)}, u32[]{:S(2)}, u32[]{:S(2)}) async-start(bf16[128,8,2304]{2,1,0:T(8,128)(2,1)} %bitcast.19), calls=%async_computation.5 | async-start | bytes 9437184 | tf_op jit(solution)/shard_map/all_to_all | solution.py:563
  186.0 24.5 %all-to-all-start.3 = ((bf16[8,128,256]{2,1,0:T(8,128)(2,1)}), bf16[8,128,256]{2,1,0:T(8,128)(2,1)S(1)}, u32[]{:S(2)}, u32[]{:S(2)}) async-start(bf16[8,128,256]{2,1,0:T(8,128)(2,1)} %passage_part.1), calls=%async_computation.3 | async-start | bytes 1048576 | tf_op jit(solution)/shard_map/all_to_all | solution.py:605
  210.5 64.6 %all-to-all-start.6 = ((bf16[128,8,2304]{2,1,0:T(8,128)(2,1)}), bf16[128,8,2304]{2,1,0:T(8,128)(2,1)}, u32[]{:S(2)}, u32[]{:S(2)}) async-start(bf16[128,8,2304]{2,1,0:T(8,128)(2,1)} %bitcast.24), calls=%async_computation.6 | async-start | bytes 9437184 | tf_op jit(solution)/shard_map/all_to_all | solution.py:563

commit v5 on v4

--- a/solution.py
+++ b/solution.py
@@ -526,29 +526,69 @@
     )(at, scores, stats, positive, passages)
 
 
-def passage_part_kernel(dscore_ref, query_hbm, out_ref, query_ref):
+CORES = 2
+
+
+def passage_part_kernel(at_ref, dscore_ref, query_hbm, own_ref, other_ref, query_ref, part_ref):
     pltpu.sync_copy(query_hbm, query_ref)
-    peers, _, width = out_ref.shape
+    chips, _, width = own_ref.shape
     pieces, _, step = query_ref.shape
     for c in range(pieces):
         at = c * step
-        out_ref[at // width, :, at % width : at % width + step] = dot(
+        part_ref[at // width, :, at % width : at % width + step] = dot(
             dscore_ref[...], query_ref[c]
         ).astype(B16)
-
-
-def passage_part(dscore, queries, peers):
+    core = at_ref[0] % CORES
+    for y in range(chips):
+        own_ref[y] = part_ref[y * CORES + core]
+        other_ref[y] = part_ref[y * CORES + 1 - core]
+
+
+def passage_part(at, dscore, queries, peers):
     pieces, _, step = queries.shape
+    width = pieces * step // peers
+    smem = pl.BlockSpec(memory_space=pltpu.SMEM)
     vmem = pl.BlockSpec(memory_space=pltpu.VMEM)
+    half = jax.ShapeDtypeStruct((peers // CORES, dscore.shape[0], width), B16)
     return pl.pallas_call(
         passage_part_kernel,
-        in_specs=[vmem, pl.BlockSpec(memory_space=pl.ANY)],
-        out_specs=vmem,
-        scratch_shapes=[pltpu.VMEM(queries.shape, B16)],
-        out_shape=jax.ShapeDtypeStruct((peers, dscore.shape[0], pieces * step // peers), B16),
+        in_specs=[smem, vmem, pl.BlockSpec(memory_space=pl.ANY)],
+        out_specs=[vmem, vmem],
+        out_shape=[half, half],
+        scratch_shapes=[
+            pltpu.VMEM(queries.shape, B16),
+            pltpu.VMEM((peers, dscore.shape[0], width), B16),
+        ],
         compiler_params=params(16),
         name="passage_part",
-    )(dscore, queries)
+    )(at, dscore, queries)
+
+
+def pair_sum_kernel(at_ref, own_ref, got_ref, mine_ref, *out_refs):
+    chips = own_ref.shape[0]
+    chip = at_ref[0] // CORES
+
+    def pair(k):
+        y = (chip + k) % chips
+        return own_ref[y].astype(F32) + got_ref[y].astype(F32)
+
+    mine_ref[...] = pair(0)
+    for k in range(1, chips):
+        out_refs[k - 1][...] = pair(k).astype(B16)
+
+
+def pair_sum(at, own, got):
+    chips, rows, width = own.shape
+    vmem = pl.BlockSpec(memory_space=pltpu.VMEM)
+    return pl.pallas_call(
+        pair_sum_kernel,
+        in_specs=[pl.BlockSpec(memory_space=pltpu.SMEM), vmem, vmem],
+        out_specs=[vmem] * chips,
+        out_shape=[jax.ShapeDtypeStruct((rows, width), F32)]
+        + [jax.ShapeDtypeStruct((rows, width), B16)] * (chips - 1),
+        compiler_params=params(16),
+        name="pair_sum",
+    )(at, own, got)
 
 
 def sent_to_all(value, axis):
@@ -590,20 +630,30 @@
     scores, stat = local_scores(queries, passages)
     stats = sent_to_all(stat, "col")
     at = lax.axis_index("col") * scores.shape[0]
+    stats, tokens_out = lax.optimization_barrier((stats, tokens_out))
     part, dscore = query_part(at[None], scores, stats, positive[None], passages)
     parts = lax.all_to_all(
         part.reshape(col_size, -1, part.shape[1]), "col", 0, 0, tiled=True
     )
+    row = lax.axis_index("row")[None]
+    own, other = passage_part(row, dscore, queries, row_size)
+    got = lax.ppermute(other, "row", [(i, i ^ 1) for i in range(row_size)])
+    mine, *further = pair_sum(row, own, got)
+    further = [
+        lax.ppermute(
+            value, "row", [(i, (i + k * CORES) % row_size) for i in range(row_size)]
+        )
+        for k, value in enumerate(further, 1)
+    ]
+    tokens_out, *further = lax.optimization_barrier((tokens_out, *further))
+    passage_grad = mine + sum(value.astype(F32) for value in further)
     slot_inputs = exchanged(tokens_out, experts)
     grads_out, cot = send_grads(ids_t, weights_t, parts, experts)
-    pieces = passage_part(dscore, queries, row_size)
     slot_grads = exchanged(grads_out, experts)
 
     plan = combine_plan(expert_ids, experts)
     hid, cg, cu, inputs9 = forward(slot_inputs, gate_up, hidden)
-    pieces, cg, plan = lax.optimization_barrier((pieces, cg, plan))
-    passage_parts = lax.all_to_all(pieces, "row", 0, 0, tiled=True)
-    passage_grad = jnp.sum(passage_parts.astype(F32), axis=0)
+    passage_grad, cg, plan = lax.optimization_barrier((passage_grad, cg, plan))
     back_out, pre_grad, grads9 = backward(slot_grads, down, cg, cu, gate_up)
     returned = exchanged(back_out, experts)
     down_grad = weight_grad(hid, hid, slot_grads, grads9, down.shape[1], MAIN, 0, "down_grad")

time: 284 us -> 280 us (0.986)
  waiting for transfers between devices: 135 us -> 130 us
    ppermute x0 -> x4, starting transfers between devices: none -> 6.45 us  [the longest x3 5.07 us: shards(): lax.ppermute(value, 'row', [(i, (i + k * CORES) % row_size) for i in rang...]
    all_to_all x1, waiting for transfers between devices: 8.83 us -> 3.7 us  [shards(): lax.all_to_all(part.reshape(col_size, -1, part.shape[1]), 'col', 0, 0, ti...]
    all_to_all x2, waiting for transfers between devices: 3.96 us -> 0.01 us  [sent_to_all(): lax.all_to_all(jnp.broadcast_to(value[None], (peers, *value.shape)), axis...]
    all_to_all x1 -> x0, starting transfers between devices: 3.86 us -> none  [shards(): passage_parts = lax.all_to_all(pieces, 'row', 0, 0, tiled=True)]
    ppermute x0 -> x4, waiting for transfers between devices: none -> 3.5 us  [the longest x3 2.34 us: shards(): lax.ppermute(value, 'row', [(i, (i + k * CORES) % row_size) for i in rang...]
  transfers between devices with their start and end apart: 7 -> 10, of which waited for: 5 -> 7; matrix products, arithmetic and copies ran while one was open for 0% -> 0% of each run, Pallas kernels for 23% -> 16%
where the time goes in v5:
time: 280 us; the launch traced here: 277 us
  waiting for transfers between devices  130 us (46%)
  Pallas kernels  71.9 us (26%)
  starting transfers between devices  51 us (18%)
  blocking collectives  14.9 us (5%)
  local copies, waits for them, and re-layouts  7.17 us (3%)
    all_to_all x3, waiting for transfers between devices, exchanged(): lax.all_to_all(block.reshape(experts, rows // experts, width), ('row', 'c...  123 us
    all_to_all x3, starting transfers between devices, exchanged(): lax.all_to_all(block.reshape(experts, rows // experts, width), ('row', 'c...  23.8 us
    pallas_call x2, Pallas kernels, weight_grad(): pl.pallas_call(weight_grad_kernel, grid=(columns // tile,), in_specs=[pl....  22.9 us
    pallas_call x1, Pallas kernels, backward(): pl.pallas_call(functools.partial(backward_kernel, first), grid=(first + M...  20.6 us
    all_gather x1, blocking collectives, shards(): passages = lax.all_gather(document_vectors, 'row')  14.9 us
    all_to_all x2, starting transfers between devices, sent_to_all(): lax.all_to_all(jnp.broadcast_to(value[None], (peers, *value.shape)), axis...  14.1 us
    pallas_call x1, Pallas kernels, forward(): pl.pallas_call(forward_kernel, grid=(tiles,), in_specs=[whole(x.shape), p...  12.8 us
    all_to_all x1, starting transfers between devices, shards(): lax.all_to_all(part.reshape(col_size, -1, part.shape[1]), 'col', 0, 0, ti...  6.68 us
  transfers between devices with their start and end apart: 10, of which 7 were waited for; matrix products, arithmetic and copies ran while one was open for 0% of the time, Pallas kernels for 16%

profile of v5, /device:TPU:37, one launch (start us, length us, event | category | flops | bytes accessed | tf_op | source)
XLA Modules:
  0.0 276.6 jit_solution(788094594337803359)
XLA Ops:
  0.7 2.1 broadcast_in_dim.29
  2.7 7.4 %all-to-all-start = ((bf16[16,256,128]{2,1,0:T(8,128)(2,1)}), bf16[16,256,128]{2,1,0:T(8,128)(2,1)S(1)}, u32[]{:S(2)}, u32[]{:S(2)}) async-start(bf16[16,256,128]{2,1,0:T(8,128)(2,1)} %broadcast_in_dim.29), calls=%async_computation | async-start | bytes 2097152 | tf_op jit(solution)/shard_map/all_to_all | solution.py:596
  10.1 14.9 %all-gather = bf16[1024,256]{1,0:T(8,128)(2,1)S(1)} all-gather(bf16[128,256]{1,0:T(8,128)(2,1)} %param.9), channel_id=2, replica_groups=mesh['row'=8,'col'=16] {'row'}, dimensions={0}, use_global_device_ids=true | all-gather | bytes 589824 | tf_op jit(solution)/shard_map/all_gather | solution.py:628
  26.2 6.7 %all-to-all-start.1 = ((f32[16,2,256]{2,1,0:T(2,128)}), f32[16,2,256]{2,1,0:T(2,128)S(1)}, u32[]{:S(2)}, u32[]{:S(2)}) async-start(f32[16,2,256]{2,1,0:T(2,128)} %broadcast_in_dim.30), calls=%async_computation.1 | async-start | bytes 65536 | tf_op jit(solution)/shard_map/all_to_all | solution.py:596
  32.9 3.4 %send_tokens.1 = bf16[1024,2304]{1,0:T(8,128)(2,1)S(1)} custom-call(s32[8,128]{1,0:T(8,128)S(1)} %bitcast.21, bf16[128,2048]{1,0:T(8,128)(2,1)S(1)} %copy-done.2), custom_call_target="tpu_custom_call" | custom-call | tf_op jit(solution)/shard_map/send_tokens/pallas_call | solution.py:98
  36.3 2.2 copy-done
  38.5 1.5 query_part.1
  40.0 6.7 %all-to-all-start.3 = ((bf16[16,16,2048]{2,1,0:T(8,128)(2,1)}), bf16[16,16,2048]{2,1,0:T(8,128)(2,1)S(1)}, u32[]{:S(2)}, u32[]{:S(2)}) async-start(bf16[16,16,2048]{2,1,0:T(8,128)(2,1)} %bitcast.9), calls=%async_computation.3 | async-start | bytes 2097152 | tf_op jit(solution)/shard_map/all_to_all | solution.py:635
  51.3 2.6 collective-permute-start.2
  55.0 1.9 collective-permute-done.2
  57.3 3.7 %all-to-all-done.3.part_hbm = bf16[16,16,2048]{2,1,0:T(8,128)(2,1)S(1)} async-done(((bf16[16,16,2048]{2,1,0:T(8,128)(2,1)}), bf16[16,16,2048]{2,1,0:T(8,128)(2,1)S(1)}, u32[]{:S(2)}, u32[]{:S(2)}) %all-to-all-start.3) | async-done | bytes 1048608 | tf_op jit(solution)/shard_map/all_to_all | solution.py:635
  61.0 9.2 %all-to-all-start.2 = ((bf16[128,8,2304]{2,1,0:T(8,128)(2,1)}), bf16[128,8,2304]{2,1,0:T(8,128)(2,1)}, u32[]{:S(2)}, u32[]{:S(2)}) async-start(bf16[128,8,2304]{2,1,0:T(8,128)(2,1)} %bitcast.17), calls=%async_computation.2 | async-start | bytes 9437184 | tf_op jit(solution)/shard_map/all_to_all | solution.py:603
  70.2 3.8 %send_grads.1 = (bf16[1024,2304]{1,0:T(8,128)(2,1)S(1)}, bf16[16,2048]{1,0:T(8,128)(2,1)S(1)}) custom-call(s32[8,128]{1,0:T(8,128)S(1)} %bitcast.22, f32[8,128]{1,0:T(8,128)S(1)} %bitcast.23, bf16[16,16,2048]{2,1,0:T(8,128)(2,1)S(1)} %all-to-all-done.3.part_hbm), custom_call_target="tpu_custom_call" | custom-call | tf_op jit(solution)/shard_map/send_grads/pallas_call | solution.py:160
  74.1 2.2 copy-done.1
  76.2 49.4 %all-to-all-done.2 = bf16[128,8,2304]{2,1,0:T(8,128)(2,1)} async-done(((bf16[128,8,2304]{2,1,0:T(8,128)(2,1)}), bf16[128,8,2304]{2,1,0:T(8,128)(2,1)}, u32[]{:S(2)}, u32[]{:S(2)}) %all-to-all-start.2) | async-done | bytes 4718624 | tf_op jit(solution)/shard_map/all_to_all | solution.py:603
  125.6 7.3 %all-to-all-start.4 = ((bf16[128,8,2304]{2,1,0:T(8,128)(2,1)}), bf16[128,8,2304]{2,1,0:T(8,128)(2,1)}, u32[]{:S(2)}, u32[]{:S(2)}) async-start(bf16[128,8,2304]{2,1,0:T(8,128)(2,1)} %bitcast.20), calls=%async_computation.4 | async-start | bytes 9437184 | tf_op jit(solution)/shard_map/all_to_all | solution.py:603
  134.3 12.8 %expert_forward.1 = (bf16[1152,768]{1,0:T(8,128)(2,1)}, bf16[1152,768]{1,0:T(8,128)(2,1)}, bf16[1152,768]{1,0:T(8,128)(2,1)}, bf16[128,2048]{1,0:T(8,128)(2,1)}) custom-call(bf16[1024,2304]{1,0:T(8,128)(2,1)} %bitcast.6.x_ref.a_ref, bf16[2048,1536]{1,0:T(8,128)(2,1)} %bitcast.26, bf16[2048,1536]{1,0:T(8,128)(2,1)} %bitcast.27), custom_call_target="tpu_custom_call" | custom-call | flops 7247757312 | bytes 16318464 | tf_op jit(solution)/shard_map/expert_forward/pallas_call | solution.py:233
  147.1 41.2 %all-to-all-done.4 = bf16[128,8,2304]{2,1,0:T(8,128)(2,1)} async-done(((bf16[128,8,2304]{2,1,0:T(8,128)(2,1)}), bf16[128,8,2304]{2,1,0:T(8,128)(2,1)}, u32[]{:S(2)}, u32[]{:S(2)}) %all-to-all-start.4) | async-done | bytes 4718624 | tf_op jit(solution)/shard_map/all_to_all | solution.py:603
  188.3 20.6 %expert_backward.1 = (bf16[1024,2304]{1,0:T(8,128)(2,1)}, bf16[1152,1536]{1,0:T(8,128)(2,1)}, bf16[128,2048]{1,0:T(8,128)(2,1)}) custom-call(bf16[1024,2304]{1,0:T(8,128)(2,1)} %bitcast.11.g_ref.b_ref, bf16[768,2048]{1,0:T(8,128)(2,1)} %bitcast.29, bf16[1152,768]{1,0:T(8,128)(2,1)} %get-tuple-element.59.cg_ref, bf16[1152,768]{1,0:T(8,128)(2,1)} %get-tuple-element.60.cu_ref, ...), custom_call_target="tpu_custom_call" | custom-call | flops 10871635968 | bytes 18874368 | tf_op jit(solution)/shard_map/expert_backward/pallas_call | solution.py:313
  208.9 7.3 %all-to-all-start.5 = ((bf16[128,8,2304]{2,1,0:T(8,128)(2,1)}), bf16[128,8,2304]{2,1,0:T(8,128)(2,1)}, u32[]{:S(2)}, u32[]{:S(2)}) async-start(bf16[128,8,2304]{2,1,0:T(8,128)(2,1)} %bitcast.25), calls=%async_computation.5 | async-start | bytes 9437184 | tf_op jit(solution)/shard_map/all_to_all | solution.py:603
  216.2 9.7 %down_grad.1 = bf16[768,2048]{1,0:T(8,128)(2,1)} custom-call(bf16[1152,768]{1,0:T(8,128)(2,1)} %get-tuple-element.64.a_ref.a9_ref, bf16[1152,768]{1,0:T(8,128)(2,1)} %get-tuple-element.64.a_ref.a9_ref, bf16[1024,2304]{1,0:T(8,128)(2,1)} %bitcast.11.g_ref.b_ref, bf16[128,2048]{1,0:T(8,128)(2,1)} %get-tuple-element.65.b9_ref), custom_call_target="tpu_custom_call" | custom-call | flops 3623878656 | bytes 9633792 | tf_op jit(solution)/shard_map/down_grad/pallas_call | solution.py:364
  225.9 13.3 %gate_up_grad.1 = bf16[2048,1536]{1,0:T(8,128)(2,1)} custom-call(bf16[1024,2304]{1,0:T(8,128)(2,1)} %bitcast.6.x_ref.a_ref, bf16[128,2048]{1,0:T(8,128)(2,1)} %get-tuple-element.62.a9_ref, bf16[1152,1536]{1,0:T(8,128)(2,1)} %get-tuple-element.63.b_ref.b9_ref, bf16[1152,1536]{1,0:T(8,128)(2,1)} %get-tuple-element.63.b_ref.b9_ref), custom_call_target="tpu_custom_call" | custom-call | flops 7247757312 | bytes 14548992 | tf_op jit(solution)/shard_map/gate_up_grad/pallas_call | solution.py:364
  239.2 32.5 %all-to-all-done.5 = bf16[128,8,2304]{2,1,0:T(8,128)(2,1)} async-done(((bf16[128,8,2304]{2,1,0:T(8,128)(2,1)}), bf16[128,8,2304]{2,1,0:T(8,128)(2,1)}, u32[]{:S(2)}, u32[]{:S(2)}) %all-to-all-start.5) | async-done | bytes 4718624 | tf_op jit(solution)/shard_map/all_to_all | solution.py:603
  271.6 5.0 %combine.1 = bf16[128,2048]{1,0:T(8,128)(2,1)} custom-call(bf16[128,1024]{1,0:T(8,128)(2,1)S(1)} %get-tuple-element.54.mask_ref, bf16[128,128]{1,0:T(8,128)(2,1)S(1)} %get-tuple-element.55.last_ref, bf16[16,2048]{1,0:T(8,128)(2,1)S(1)} %get-tuple-element.57.cot_ref, bf16[1024,2304]{1,0:T(8,128)(2,1)} %bitcast.14.got_ref.fold_ref, ...), custom_call_target="tpu_custom_call" | custom-call | tf_op jit(solution)/shard_map/combine/pallas_call | solution.py:440
  (25 shorter events, 8.7 us)
Async XLA Ops:
  0.6 32.3 %copy-start.3 = (s32[128,8]{0,1:T(8,128)S(1)}, s32[128,8]{0,1:T(8,128)}, u32[]{:S(2)}) copy-start(s32[128,8]{0,1:T(8,128)} %param.12) | copy-start | bytes 12292
  0.6 32.3 %copy-start.2 = (bf16[128,2048]{1,0:T(8,128)(2,1)S(1)}, bf16[128,2048]{1,0:T(8,128)(2,1)}, u32[]{:S(2)}) copy-start(bf16[128,2048]{1,0:T(8,128)(2,1)} %tok_ref.1) | copy-start | bytes 1572868
  2.7 35.7 %copy-start.5 = (s32[256]{0:T(256)S(1)}, s32[256]{0:T(256)}, u32[]{:S(2)}) copy-start(s32[256]{0:T(256)} %param.10) | copy-start | bytes 3076
  2.7 22.3 %all-to-all-start = ((bf16[16,256,128]{2,1,0:T(8,128)(2,1)}), bf16[16,256,128]{2,1,0:T(8,128)(2,1)S(1)}, u32[]{:S(2)}, u32[]{:S(2)}) async-start(bf16[16,256,128]{2,1,0:T(8,128)(2,1)} %broadcast_in_dim.29), calls=%async_computation | async-start | bytes 2097152 | tf_op jit(solution)/shard_map/all_to_all | solution.py:596
  26.2 12.2 %all-to-all-start.1 = ((f32[16,2,256]{2,1,0:T(2,128)}), f32[16,2,256]{2,1,0:T(2,128)S(1)}, u32[]{:S(2)}, u32[]{:S(2)}) async-start(f32[16,2,256]{2,1,0:T(2,128)} %broadcast_in_dim.30), calls=%async_computation.1 | async-start | bytes 65536 | tf_op jit(solution)/shard_map/all_to_all | solution.py:596
  36.3 2.2 copy-start
  40.0 21.0 %all-to-all-start.3 = ((bf16[16,16,2048]{2,1,0:T(8,128)(2,1)}), bf16[16,16,2048]{2,1,0:T(8,128)(2,1)S(1)}, u32[]{:S(2)}, u32[]{:S(2)}) async-start(bf16[16,16,2048]{2,1,0:T(8,128)(2,1)} %bitcast.9), calls=%async_computation.3 | async-start | bytes 2097152 | tf_op jit(solution)/shard_map/all_to_all | solution.py:635
  47.3 2.5 collective-permute-start
  49.9 5.1 %collective-permute-start.1 = (bf16[128,256]{1,0:T(8,128)(2,1)S(1)}, bf16[128,256]{1,0:T(8,128)(2,1)S(1)}, u32[]{:S(2)}, u32[]{:S(2)}) collective-permute-start(bf16[128,256]{1,0:T(8,128)(2,1)S(1)} %get-tuple-element.43), channel_id=1, source_target_pairs={{0,32},{16,48},{32,64},{48,80},{64,96},{80,112},{96,0},{112,16},{1... | collective-permute-start | bytes 196616 | tf_op jit(solution)/shard_map/ppermute | solution.py:643
  51.3 5.6 %collective-permute-start.2 = (bf16[128,256]{1,0:T(8,128)(2,1)S(1)}, bf16[128,256]{1,0:T(8,128)(2,1)S(1)}, u32[]{:S(2)}, u32[]{:S(2)}) collective-permute-start(bf16[128,256]{1,0:T(8,128)(2,1)S(1)} %get-tuple-element.44), channel_id=1, source_target_pairs={{0,64},{16,80},{32,96},{48,112},{64,0},{80,16},{96,32},{112,48},{1... | collective-permute-start | bytes 196616 | tf_op jit(solution)/shard_map/ppermute | solution.py:643
  53.9 3.4 %collective-permute-start.3 = (bf16[128,256]{1,0:T(8,128)(2,1)S(1)}, bf16[128,256]{1,0:T(8,128)(2,1)S(1)}, u32[]{:S(2)}, u32[]{:S(2)}) collective-permute-start(bf16[128,256]{1,0:T(8,128)(2,1)S(1)} %get-tuple-element.45), channel_id=1, source_target_pairs={{0,96},{16,112},{32,0},{48,16},{64,32},{80,48},{96,64},{112,80},{1... | collective-permute-start | bytes 196616 | tf_op jit(solution)/shard_map/ppermute | solution.py:643
  61.0 9.2 %copy-start.4 = (f32[128,8]{0,1:T(8,128)S(1)}, f32[128,8]{0,1:T(8,128)}, u32[]{:S(2)}) copy-start(f32[128,8]{0,1:T(8,128)} %param.13) | copy-start | bytes 12292
  61.0 64.6 %all-to-all-start.2 = ((bf16[128,8,2304]{2,1,0:T(8,128)(2,1)}), bf16[128,8,2304]{2,1,0:T(8,128)(2,1)}, u32[]{:S(2)}, u32[]{:S(2)}) async-start(bf16[128,8,2304]{2,1,0:T(8,128)(2,1)} %bitcast.17), calls=%async_computation.2 | async-start | bytes 9437184 | tf_op jit(solution)/shard_map/all_to_all | solution.py:603
  74.1 2.2 copy-start.1
  125.6 62.7 %all-to-all-start.4 = ((bf16[128,8,2304]{2,1,0:T(8,128)(2,1)}), bf16[128,8,2304]{2,1,0:T(8,128)(2,1)}, u32[]{:S(2)}, u32[]{:S(2)}) async-start(bf16[128,8,2304]{2,1,0:T(8,128)(2,1)} %bitcast.20), calls=%async_computation.4 | async-start | bytes 9437184 | tf_op jit(solution)/shard_map/all_to_all | solution.py:603
  208.9 62.7 %all-to-all-start.5 = ((bf16[128,8,2304]{2,1,0:T(8,128)(2,1)}), bf16[128,8,2304]{2,1,0:T(8,128)(2,1)}, u32[]{:S(2)}, u32[]{:S(2)}) async-start(bf16[128,8,2304]{2,1,0:T(8,128)(2,1)} %bitcast.25), calls=%async_computation.5 | async-start | bytes 9437184 | tf_op jit(solution)/shard_map/all_to_all | solution.py:603

commit v6 on v5

--- a/solution.py
+++ b/solution.py
@@ -251,11 +251,17 @@
     )(x, gate_up, gate_up)
 
 
+CHUNKS = 4
+
+
 def backward_kernel(
-    first, g_ref, down_ref, cg_ref, cu_ref, w_ref, out_ref, pair_ref, g9_ref, pg_ref, fold_ref
+    first, *refs
 ):
+    g_refs, refs = refs[:CHUNKS], refs[CHUNKS:]
+    down_ref, cg_ref, cu_ref, w_ref, out_ref, pair_ref, g9_ref, pg_ref, fold_ref = refs
     j = pl.program_id(0)
-    rows = g_ref.shape[0]
+    step = g_refs[0].shape[0]
+    rows = step * CHUNKS
     sources, depth = g9_ref.shape
     width = out_ref.shape[1]
     total = rows + sources
@@ -265,7 +271,7 @@
 
     @pl.when(j == 0)
     def _():
-        unfold(g_ref[:, depth:], fold_ref, g9_ref)
+        unfold(jnp.concatenate([g[:, depth:] for g in g_refs]), fold_ref, g9_ref)
 
     @pl.when(j < first)
     def _():
@@ -279,10 +285,9 @@
             pair_ref[at, :tile] = gate
             pair_ref[at, tile:] = up
 
-        step = rows // 4
-        for m in range(4):
+        for m in range(CHUNKS):
             at = slice(m * step, (m + 1) * step)
-            finish(at, dot(g_ref[at, :depth], down_ref[...], ((1,), (1,))))
+            finish(at, dot(g_refs[m][:, :depth], down_ref[...], ((1,), (1,))))
         finish(slice(rows, total), dot(g9_ref[...], down_ref[...], ((1,), (1,))))
 
     @pl.when((j >= first) & (j < first + MAIN))
@@ -314,7 +319,14 @@
         functools.partial(backward_kernel, first),
         grid=(first + MAIN + 1,),
         in_specs=[
-            whole(g.shape),
+            *[
+                pl.BlockSpec(
+                    (rows // CHUNKS, g.shape[1]),
+                    lambda j, m=m: (m, 0),
+                    pipeline_mode=pl.Buffered(1),
+                )
+                for m in range(CHUNKS)
+            ],
             pl.BlockSpec((tile, depth), lambda j: (jnp.minimum(j, first - 1), 0)),
             part,
             part,
@@ -343,7 +355,7 @@
             transcendentals=0,
         ),
         name="expert_backward",
-    )(g, down, cg, cu, gate_up)
+    )(*[g] * CHUNKS, down, cg, cu, gate_up)
 
 
 def weight_grad_kernel(a_ref, a9_ref, b_ref, b9_ref, out_ref):
@@ -436,7 +448,7 @@
     queries, depth = cot.shape
     rows = got.shape[0]
     fold = depth // MAIN
-    width = 2 * fold
+    width = 4 * fold
     return pl.pallas_call(
         combine_kernel,
         grid=(depth // width,),

time: 280 us -> 279 us (level)
  no operation moved by 1% of the time
where the time goes in v6:
time: 279 us; the launch traced here: 275 us
  waiting for transfers between devices  130 us (47%)
  Pallas kernels  70.5 us (25%)
  starting transfers between devices  51 us (18%)
  blocking collectives  14.9 us (5%)
  local copies, waits for them, and re-layouts  7.17 us (3%)
    all_to_all x3, waiting for transfers between devices, exchanged(): lax.all_to_all(block.reshape(experts, rows // experts, width), ('row', 'c...  123 us
    all_to_all x3, starting transfers between devices, exchanged(): lax.all_to_all(block.reshape(experts, rows // experts, width), ('row', 'c...  23.8 us
    pallas_call x2, Pallas kernels, weight_grad(): pl.pallas_call(weight_grad_kernel, grid=(columns // tile,), in_specs=[pl....  22.9 us
    pallas_call x1, Pallas kernels, backward(): pl.pallas_call(functools.partial(backward_kernel, first), grid=(first + M...  20.3 us
    all_gather x1, blocking collectives, shards(): passages = lax.all_gather(document_vectors, 'row')  14.9 us
    all_to_all x2, starting transfers between devices, sent_to_all(): lax.all_to_all(jnp.broadcast_to(value[None], (peers, *value.shape)), axis...  14.1 us
    pallas_call x1, Pallas kernels, forward(): pl.pallas_call(forward_kernel, grid=(tiles,), in_specs=[whole(x.shape), p...  12.8 us
    all_to_all x1, starting transfers between devices, shards(): lax.all_to_all(part.reshape(col_size, -1, part.shape[1]), 'col', 0, 0, ti...  6.68 us
  transfers between devices with their start and end apart: 10, of which 7 were waited for; matrix products, arithmetic and copies ran while one was open for 0% of the time, Pallas kernels for 16%

profile of v6, /device:TPU:37, one launch (start us, length us, event | category | flops | bytes accessed | tf_op | source)
XLA Modules:
  0.0 275.2 jit_solution(12260907723004408125)
XLA Ops:
  0.7 2.1 broadcast_in_dim.29
  2.7 7.4 %all-to-all-start = ((bf16[16,256,128]{2,1,0:T(8,128)(2,1)}), bf16[16,256,128]{2,1,0:T(8,128)(2,1)S(1)}, u32[]{:S(2)}, u32[]{:S(2)}) async-start(bf16[16,256,128]{2,1,0:T(8,128)(2,1)} %broadcast_in_dim.29), calls=%async_computation | async-start | bytes 2097152 | tf_op jit(solution)/shard_map/all_to_all | solution.py:608
  10.1 14.9 %all-gather = bf16[1024,256]{1,0:T(8,128)(2,1)S(1)} all-gather(bf16[128,256]{1,0:T(8,128)(2,1)} %param.9), channel_id=2, replica_groups=mesh['row'=8,'col'=16] {'row'}, dimensions={0}, use_global_device_ids=true | all-gather | bytes 589824 | tf_op jit(solution)/shard_map/all_gather | solution.py:640
  26.2 6.7 %all-to-all-start.1 = ((f32[16,2,256]{2,1,0:T(2,128)}), f32[16,2,256]{2,1,0:T(2,128)S(1)}, u32[]{:S(2)}, u32[]{:S(2)}) async-start(f32[16,2,256]{2,1,0:T(2,128)} %broadcast_in_dim.30), calls=%async_computation.1 | async-start | bytes 65536 | tf_op jit(solution)/shard_map/all_to_all | solution.py:608
  32.9 3.4 %send_tokens.1 = bf16[1024,2304]{1,0:T(8,128)(2,1)S(1)} custom-call(s32[8,128]{1,0:T(8,128)S(1)} %bitcast.21, bf16[128,2048]{1,0:T(8,128)(2,1)S(1)} %copy-done.2), custom_call_target="tpu_custom_call" | custom-call | tf_op jit(solution)/shard_map/send_tokens/pallas_call | solution.py:98
  36.3 2.2 copy-done
  38.5 1.5 query_part.1
  40.0 6.7 %all-to-all-start.3 = ((bf16[16,16,2048]{2,1,0:T(8,128)(2,1)}), bf16[16,16,2048]{2,1,0:T(8,128)(2,1)S(1)}, u32[]{:S(2)}, u32[]{:S(2)}) async-start(bf16[16,16,2048]{2,1,0:T(8,128)(2,1)} %bitcast.9), calls=%async_computation.3 | async-start | bytes 2097152 | tf_op jit(solution)/shard_map/all_to_all | solution.py:647
  51.3 2.6 collective-permute-start.2
  55.0 1.9 collective-permute-done.2
  57.3 3.7 %all-to-all-done.3.part_hbm = bf16[16,16,2048]{2,1,0:T(8,128)(2,1)S(1)} async-done(((bf16[16,16,2048]{2,1,0:T(8,128)(2,1)}), bf16[16,16,2048]{2,1,0:T(8,128)(2,1)S(1)}, u32[]{:S(2)}, u32[]{:S(2)}) %all-to-all-start.3) | async-done | bytes 1048608 | tf_op jit(solution)/shard_map/all_to_all | solution.py:647
  61.0 9.2 %all-to-all-start.2 = ((bf16[128,8,2304]{2,1,0:T(8,128)(2,1)}), bf16[128,8,2304]{2,1,0:T(8,128)(2,1)}, u32[]{:S(2)}, u32[]{:S(2)}) async-start(bf16[128,8,2304]{2,1,0:T(8,128)(2,1)} %bitcast.17), calls=%async_computation.2 | async-start | bytes 9437184 | tf_op jit(solution)/shard_map/all_to_all | solution.py:615
  70.2 3.8 %send_grads.1 = (bf16[1024,2304]{1,0:T(8,128)(2,1)S(1)}, bf16[16,2048]{1,0:T(8,128)(2,1)S(1)}) custom-call(s32[8,128]{1,0:T(8,128)S(1)} %bitcast.22, f32[8,128]{1,0:T(8,128)S(1)} %bitcast.23, bf16[16,16,2048]{2,1,0:T(8,128)(2,1)S(1)} %all-to-all-done.3.part_hbm), custom_call_target="tpu_custom_call" | custom-call | tf_op jit(solution)/shard_map/send_grads/pallas_call | solution.py:160
  74.1 2.2 copy-done.1
  76.2 49.4 %all-to-all-done.2 = bf16[128,8,2304]{2,1,0:T(8,128)(2,1)} async-done(((bf16[128,8,2304]{2,1,0:T(8,128)(2,1)}), bf16[128,8,2304]{2,1,0:T(8,128)(2,1)}, u32[]{:S(2)}, u32[]{:S(2)}) %all-to-all-start.2) | async-done | bytes 4718624 | tf_op jit(solution)/shard_map/all_to_all | solution.py:615
  125.6 7.3 %all-to-all-start.4 = ((bf16[128,8,2304]{2,1,0:T(8,128)(2,1)}), bf16[128,8,2304]{2,1,0:T(8,128)(2,1)}, u32[]{:S(2)}, u32[]{:S(2)}) async-start(bf16[128,8,2304]{2,1,0:T(8,128)(2,1)} %bitcast.20), calls=%async_computation.4 | async-start | bytes 9437184 | tf_op jit(solution)/shard_map/all_to_all | solution.py:615
  134.3 12.8 %expert_forward.1 = (bf16[1152,768]{1,0:T(8,128)(2,1)}, bf16[1152,768]{1,0:T(8,128)(2,1)}, bf16[1152,768]{1,0:T(8,128)(2,1)}, bf16[128,2048]{1,0:T(8,128)(2,1)}) custom-call(bf16[1024,2304]{1,0:T(8,128)(2,1)} %bitcast.6.x_ref.a_ref, bf16[2048,1536]{1,0:T(8,128)(2,1)} %bitcast.26, bf16[2048,1536]{1,0:T(8,128)(2,1)} %bitcast.27), custom_call_target="tpu_custom_call" | custom-call | flops 7247757312 | bytes 16318464 | tf_op jit(solution)/shard_map/expert_forward/pallas_call | solution.py:233
  147.1 41.2 %all-to-all-done.4 = bf16[128,8,2304]{2,1,0:T(8,128)(2,1)} async-done(((bf16[128,8,2304]{2,1,0:T(8,128)(2,1)}), bf16[128,8,2304]{2,1,0:T(8,128)(2,1)}, u32[]{:S(2)}, u32[]{:S(2)}) %all-to-all-start.4) | async-done | bytes 4718624 | tf_op jit(solution)/shard_map/all_to_all | solution.py:615
  188.3 20.3 %expert_backward.1 = (bf16[1024,2304]{1,0:T(8,128)(2,1)}, bf16[1152,1536]{1,0:T(8,128)(2,1)}, bf16[128,2048]{1,0:T(8,128)(2,1)}) custom-call(bf16[1024,2304]{1,0:T(8,128)(2,1)} %bitcast.11.refs_0_.refs_1_.refs_2_.refs_3_.b_ref, bf16[1024,2304]{1,0:T(8,128)(2,1)} %bitcast.11.refs_0_.refs_1_.refs_2_.refs_3_.b_ref, ...), custom_call_target="tpu_custom_call" | custom-call | flops 10871635968 | bytes 18874368 | tf_op jit(solution)/shard_map/expert_backward/pallas_call | solution.py:318
  208.6 7.3 %all-to-all-start.5 = ((bf16[128,8,2304]{2,1,0:T(8,128)(2,1)}), bf16[128,8,2304]{2,1,0:T(8,128)(2,1)}, u32[]{:S(2)}, u32[]{:S(2)}) async-start(bf16[128,8,2304]{2,1,0:T(8,128)(2,1)} %bitcast.25), calls=%async_computation.5 | async-start | bytes 9437184 | tf_op jit(solution)/shard_map/all_to_all | solution.py:615
  215.9 9.7 %down_grad.1 = bf16[768,2048]{1,0:T(8,128)(2,1)} custom-call(bf16[1152,768]{1,0:T(8,128)(2,1)} %get-tuple-element.64.a_ref.a9_ref, bf16[1152,768]{1,0:T(8,128)(2,1)} %get-tuple-element.64.a_ref.a9_ref, bf16[1024,2304]{1,0:T(8,128)(2,1)} %bitcast.11.refs_0_.refs_1_.refs_2_.refs_3_.b_ref, bf16[128,2048]{1,0:T(8,128)(2,1)} %get-tuple-element.65.b9_ref), custom_call_target="tpu_custom_call" | custom-call | flops 3623878656 | bytes 9633792 | tf_op jit(solution)/shard_map/down_grad/pallas_call | solution.py:376
  225.6 13.3 %gate_up_grad.1 = bf16[2048,1536]{1,0:T(8,128)(2,1)} custom-call(bf16[1024,2304]{1,0:T(8,128)(2,1)} %bitcast.6.x_ref.a_ref, bf16[128,2048]{1,0:T(8,128)(2,1)} %get-tuple-element.62.a9_ref, bf16[1152,1536]{1,0:T(8,128)(2,1)} %get-tuple-element.63.b_ref.b9_ref, bf16[1152,1536]{1,0:T(8,128)(2,1)} %get-tuple-element.63.b_ref.b9_ref), custom_call_target="tpu_custom_call" | custom-call | flops 7247757312 | bytes 14548992 | tf_op jit(solution)/shard_map/gate_up_grad/pallas_call | solution.py:376
  238.9 32.5 %all-to-all-done.5 = bf16[128,8,2304]{2,1,0:T(8,128)(2,1)} async-done(((bf16[128,8,2304]{2,1,0:T(8,128)(2,1)}), bf16[128,8,2304]{2,1,0:T(8,128)(2,1)}, u32[]{:S(2)}, u32[]{:S(2)}) %all-to-all-start.5) | async-done | bytes 4718624 | tf_op jit(solution)/shard_map/all_to_all | solution.py:615
  271.3 3.9 %combine.1 = bf16[128,2048]{1,0:T(8,128)(2,1)} custom-call(bf16[128,1024]{1,0:T(8,128)(2,1)S(1)} %get-tuple-element.54.mask_ref, bf16[128,128]{1,0:T(8,128)(2,1)S(1)} %get-tuple-element.55.last_ref, bf16[16,2048]{1,0:T(8,128)(2,1)S(1)} %get-tuple-element.57.cot_ref, bf16[1024,2304]{1,0:T(8,128)(2,1)} %bitcast.14.got_ref.fold_ref, ...), custom_call_target="tpu_custom_call" | custom-call | tf_op jit(solution)/shard_map/combine/pallas_call | solution.py:452
  (25 shorter events, 8.7 us)
Async XLA Ops:
  0.6 32.3 %copy-start.3 = (s32[128,8]{0,1:T(8,128)S(1)}, s32[128,8]{0,1:T(8,128)}, u32[]{:S(2)}) copy-start(s32[128,8]{0,1:T(8,128)} %param.12) | copy-start | bytes 12292
  0.6 32.3 %copy-start.2 = (bf16[128,2048]{1,0:T(8,128)(2,1)S(1)}, bf16[128,2048]{1,0:T(8,128)(2,1)}, u32[]{:S(2)}) copy-start(bf16[128,2048]{1,0:T(8,128)(2,1)} %tok_ref.1) | copy-start | bytes 1572868
  2.7 35.7 %copy-start.5 = (s32[256]{0:T(256)S(1)}, s32[256]{0:T(256)}, u32[]{:S(2)}) copy-start(s32[256]{0:T(256)} %param.10) | copy-start | bytes 3076
  2.7 22.3 %all-to-all-start = ((bf16[16,256,128]{2,1,0:T(8,128)(2,1)}), bf16[16,256,128]{2,1,0:T(8,128)(2,1)S(1)}, u32[]{:S(2)}, u32[]{:S(2)}) async-start(bf16[16,256,128]{2,1,0:T(8,128)(2,1)} %broadcast_in_dim.29), calls=%async_computation | async-start | bytes 2097152 | tf_op jit(solution)/shard_map/all_to_all | solution.py:608
  26.2 12.2 %all-to-all-start.1 = ((f32[16,2,256]{2,1,0:T(2,128)}), f32[16,2,256]{2,1,0:T(2,128)S(1)}, u32[]{:S(2)}, u32[]{:S(2)}) async-start(f32[16,2,256]{2,1,0:T(2,128)} %broadcast_in_dim.30), calls=%async_computation.1 | async-start | bytes 65536 | tf_op jit(solution)/shard_map/all_to_all | solution.py:608
  36.3 2.2 copy-start
  40.0 21.0 %all-to-all-start.3 = ((bf16[16,16,2048]{2,1,0:T(8,128)(2,1)}), bf16[16,16,2048]{2,1,0:T(8,128)(2,1)S(1)}, u32[]{:S(2)}, u32[]{:S(2)}) async-start(bf16[16,16,2048]{2,1,0:T(8,128)(2,1)} %bitcast.9), calls=%async_computation.3 | async-start | bytes 2097152 | tf_op jit(solution)/shard_map/all_to_all | solution.py:647
  47.3 2.5 collective-permute-start
  49.9 5.1 %collective-permute-start.1 = (bf16[128,256]{1,0:T(8,128)(2,1)S(1)}, bf16[128,256]{1,0:T(8,128)(2,1)S(1)}, u32[]{:S(2)}, u32[]{:S(2)}) collective-permute-start(bf16[128,256]{1,0:T(8,128)(2,1)S(1)} %get-tuple-element.43), channel_id=1, source_target_pairs={{0,32},{16,48},{32,64},{48,80},{64,96},{80,112},{96,0},{112,16},{1... | collective-permute-start | bytes 196616 | tf_op jit(solution)/shard_map/ppermute | solution.py:655
  51.3 5.6 %collective-permute-start.2 = (bf16[128,256]{1,0:T(8,128)(2,1)S(1)}, bf16[128,256]{1,0:T(8,128)(2,1)S(1)}, u32[]{:S(2)}, u32[]{:S(2)}) collective-permute-start(bf16[128,256]{1,0:T(8,128)(2,1)S(1)} %get-tuple-element.44), channel_id=1, source_target_pairs={{0,64},{16,80},{32,96},{48,112},{64,0},{80,16},{96,32},{112,48},{1... | collective-permute-start | bytes 196616 | tf_op jit(solution)/shard_map/ppermute | solution.py:655
  53.9 3.4 %collective-permute-start.3 = (bf16[128,256]{1,0:T(8,128)(2,1)S(1)}, bf16[128,256]{1,0:T(8,128)(2,1)S(1)}, u32[]{:S(2)}, u32[]{:S(2)}) collective-permute-start(bf16[128,256]{1,0:T(8,128)(2,1)S(1)} %get-tuple-element.45), channel_id=1, source_target_pairs={{0,96},{16,112},{32,0},{48,16},{64,32},{80,48},{96,64},{112,80},{1... | collective-permute-start | bytes 196616 | tf_op jit(solution)/shard_map/ppermute | solution.py:655
  61.0 9.2 %copy-start.4 = (f32[128,8]{0,1:T(8,128)S(1)}, f32[128,8]{0,1:T(8,128)}, u32[]{:S(2)}) copy-start(f32[128,8]{0,1:T(8,128)} %param.13) | copy-start | bytes 12292
  61.0 64.6 %all-to-all-start.2 = ((bf16[128,8,2304]{2,1,0:T(8,128)(2,1)}), bf16[128,8,2304]{2,1,0:T(8,128)(2,1)}, u32[]{:S(2)}, u32[]{:S(2)}) async-start(bf16[128,8,2304]{2,1,0:T(8,128)(2,1)} %bitcast.17), calls=%async_computation.2 | async-start | bytes 9437184 | tf_op jit(solution)/shard_map/all_to_all | solution.py:615
  74.1 2.2 copy-start.1
  125.6 62.7 %all-to-all-start.4 = ((bf16[128,8,2304]{2,1,0:T(8,128)(2,1)}), bf16[128,8,2304]{2,1,0:T(8,128)(2,1)}, u32[]{:S(2)}, u32[]{:S(2)}) async-start(bf16[128,8,2304]{2,1,0:T(8,128)(2,1)} %bitcast.20), calls=%async_computation.4 | async-start | bytes 9437184 | tf_op jit(solution)/shard_map/all_to_all | solution.py:615
  208.6 62.7 %all-to-all-start.5 = ((bf16[128,8,2304]{2,1,0:T(8,128)(2,1)}), bf16[128,8,2304]{2,1,0:T(8,128)(2,1)}, u32[]{:S(2)}, u32[]{:S(2)}) async-start(bf16[128,8,2304]{2,1,0:T(8,128)(2,1)} %bitcast.25), calls=%async_computation.5 | async-start | bytes 9437184 | tf_op jit(solution)/shard_map/all_to_all | solution.py:615

commit v7 on v6

--- a/solution.py
+++ b/solution.py
@@ -651,16 +651,18 @@
     own, other = passage_part(row, dscore, queries, row_size)
     got = lax.ppermute(other, "row", [(i, i ^ 1) for i in range(row_size)])
     mine, *further = pair_sum(row, own, got)
+    tokens_out, mine, *further = lax.optimization_barrier((tokens_out, mine, *further))
+    slot_inputs = exchanged(tokens_out, experts)
+    grads_out, cot = send_grads(ids_t, weights_t, parts, experts)
+    grads_out, *further = lax.optimization_barrier((grads_out, *further))
     further = [
         lax.ppermute(
             value, "row", [(i, (i + k * CORES) % row_size) for i in range(row_size)]
         )
         for k, value in enumerate(further, 1)
     ]
-    tokens_out, *further = lax.optimization_barrier((tokens_out, *further))
+    grads_out, *further = lax.optimization_barrier((grads_out, *further))
     passage_grad = mine + sum(value.astype(F32) for value in further)
-    slot_inputs = exchanged(tokens_out, experts)
-    grads_out, cot = send_grads(ids_t, weights_t, parts, experts)
     slot_grads = exchanged(grads_out, experts)
 
     plan = combine_plan(expert_ids, experts)

time: 279 us -> 281 us (level)
    all_to_all x3, waiting for transfers between devices: 123 us -> 73.7 us  [exchanged(): lax.all_to_all(block.reshape(experts, rows // experts, width), ('row', 'c...]
    ppermute x3, waiting for transfers between devices: 2.34 us -> 45.5 us  [shards(): lax.ppermute(value, 'row', [(i, (i + k * CORES) % row_size) for i in rang...]
    all_to_all x1, waiting for transfers between devices: 3.7 us -> 11.1 us  [shards(): lax.all_to_all(part.reshape(col_size, -1, part.shape[1]), 'col', 0, 0, ti...]
  transfers between devices with their start and end apart: 10 -> 10, of which waited for: 7 -> 6; matrix products, arithmetic and copies ran while one was open for 0% -> 0% of each run, Pallas kernels for 16% -> 16%
where the time goes in v7:
time: 281 us; the launch traced here: 278 us
  waiting for transfers between devices  131 us (47%)
  Pallas kernels  70.4 us (25%)
  starting transfers between devices  52.4 us (19%)
  blocking collectives  14.9 us (5%)
  local copies, waits for them, and re-layouts  7.17 us (3%)
    all_to_all x3, waiting for transfers between devices, exchanged(): lax.all_to_all(block.reshape(experts, rows // experts, width), ('row', 'c...  73.7 us
    ppermute x3, waiting for transfers between devices, shards(): lax.ppermute(value, 'row', [(i, (i + k * CORES) % row_size) for i in rang...  45.5 us
    all_to_all x3, starting transfers between devices, exchanged(): lax.all_to_all(block.reshape(experts, rows // experts, width), ('row', 'c...  25.3 us
    pallas_call x2, Pallas kernels, weight_grad(): pl.pallas_call(weight_grad_kernel, grid=(columns // tile,), in_specs=[pl....  22.9 us
    pallas_call x1, Pallas kernels, backward(): pl.pallas_call(functools.partial(backward_kernel, first), grid=(first + M...  20.3 us
    all_gather x1, blocking collectives, shards(): passages = lax.all_gather(document_vectors, 'row')  14.9 us
    all_to_all x2, starting transfers between devices, sent_to_all(): lax.all_to_all(jnp.broadcast_to(value[None], (peers, *value.shape)), axis...  14.1 us
    pallas_call x1, Pallas kernels, forward(): pl.pallas_call(forward_kernel, grid=(tiles,), in_specs=[whole(x.shape), p...  12.8 us
  transfers between devices with their start and end apart: 10, of which 6 were waited for; matrix products, arithmetic and copies ran while one was open for 0% of the time, Pallas kernels for 16%

profile of v7, /device:TPU:37, one launch (start us, length us, event | category | flops | bytes accessed | tf_op | source)
XLA Modules:
  0.0 277.7 jit_solution(6280373380088240433)
XLA Ops:
  0.7 2.1 broadcast_in_dim.27
  2.7 7.4 %all-to-all-start = ((bf16[16,256,128]{2,1,0:T(8,128)(2,1)}), bf16[16,256,128]{2,1,0:T(8,128)(2,1)S(1)}, u32[]{:S(2)}, u32[]{:S(2)}) async-start(bf16[16,256,128]{2,1,0:T(8,128)(2,1)} %broadcast_in_dim.27), calls=%async_computation | async-start | bytes 2097152 | tf_op jit(solution)/shard_map/all_to_all | solution.py:608
  10.1 14.9 %all-gather = bf16[1024,256]{1,0:T(8,128)(2,1)S(1)} all-gather(bf16[128,256]{1,0:T(8,128)(2,1)} %param.9), channel_id=2, replica_groups=mesh['row'=8,'col'=16] {'row'}, dimensions={0}, use_global_device_ids=true | all-gather | bytes 589824 | tf_op jit(solution)/shard_map/all_gather | solution.py:640
  26.2 6.7 %all-to-all-start.1 = ((f32[16,2,256]{2,1,0:T(2,128)}), f32[16,2,256]{2,1,0:T(2,128)S(1)}, u32[]{:S(2)}, u32[]{:S(2)}) async-start(f32[16,2,256]{2,1,0:T(2,128)} %broadcast_in_dim.28), calls=%async_computation.1 | async-start | bytes 65536 | tf_op jit(solution)/shard_map/all_to_all | solution.py:608
  32.9 3.4 %send_tokens.1 = bf16[1024,2304]{1,0:T(8,128)(2,1)S(1)} custom-call(s32[8,128]{1,0:T(8,128)S(1)} %bitcast.21, bf16[128,2048]{1,0:T(8,128)(2,1)S(1)} %copy-done.2), custom_call_target="tpu_custom_call" | custom-call | tf_op jit(solution)/shard_map/send_tokens/pallas_call | solution.py:98
  36.3 2.2 copy-done
  38.5 1.5 query_part.1
  40.0 6.7 %all-to-all-start.2 = ((bf16[16,16,2048]{2,1,0:T(8,128)(2,1)}), bf16[16,16,2048]{2,1,0:T(8,128)(2,1)S(1)}, u32[]{:S(2)}, u32[]{:S(2)}) async-start(bf16[16,16,2048]{2,1,0:T(8,128)(2,1)} %bitcast.6), calls=%async_computation.2 | async-start | bytes 2097152 | tf_op jit(solution)/shard_map/all_to_all | solution.py:647
  49.9 11.1 %all-to-all-done.2.part_hbm = bf16[16,16,2048]{2,1,0:T(8,128)(2,1)S(1)} async-done(((bf16[16,16,2048]{2,1,0:T(8,128)(2,1)}), bf16[16,16,2048]{2,1,0:T(8,128)(2,1)S(1)}, u32[]{:S(2)}, u32[]{:S(2)}) %all-to-all-start.2) | async-done | bytes 1048608 | tf_op jit(solution)/shard_map/all_to_all | solution.py:647
  61.0 9.2 %all-to-all-start.3 = ((bf16[128,8,2304]{2,1,0:T(8,128)(2,1)}), bf16[128,8,2304]{2,1,0:T(8,128)(2,1)}, u32[]{:S(2)}, u32[]{:S(2)}) async-start(bf16[128,8,2304]{2,1,0:T(8,128)(2,1)} %bitcast.17), calls=%async_computation.3 | async-start | bytes 9437184 | tf_op jit(solution)/shard_map/all_to_all | solution.py:615
  70.2 3.8 %send_grads.1 = (bf16[1024,2304]{1,0:T(8,128)(2,1)S(1)}, bf16[16,2048]{1,0:T(8,128)(2,1)S(1)}) custom-call(s32[8,128]{1,0:T(8,128)S(1)} %bitcast.22, f32[8,128]{1,0:T(8,128)S(1)} %bitcast.23, bf16[16,16,2048]{2,1,0:T(8,128)(2,1)S(1)} %all-to-all-done.2.part_hbm), custom_call_target="tpu_custom_call" | custom-call | tf_op jit(solution)/shard_map/send_grads/pallas_call | solution.py:160
  74.1 2.2 copy-done.1
  77.5 2.5 collective-permute-start.2
  81.1 43.8 %collective-permute-done.1 = bf16[128,256]{1,0:T(8,128)(2,1)S(1)} collective-permute-done((bf16[128,256]{1,0:T(8,128)(2,1)S(1)}, bf16[128,256]{1,0:T(8,128)(2,1)S(1)}, u32[]{:S(2)}, u32[]{:S(2)}) %collective-permute-start.1) | collective-permute-done | bytes 65568 | tf_op jit(solution)/shard_map/ppermute | solution.py:659
  124.9 1.7 collective-permute-done.2
  126.6 8.8 %all-to-all-start.4 = ((bf16[128,8,2304]{2,1,0:T(8,128)(2,1)}), bf16[128,8,2304]{2,1,0:T(8,128)(2,1)}, u32[]{:S(2)}, u32[]{:S(2)}) async-start(bf16[128,8,2304]{2,1,0:T(8,128)(2,1)} %bitcast.20), calls=%async_computation.4 | async-start | bytes 9437184 | tf_op jit(solution)/shard_map/all_to_all | solution.py:615
  136.8 12.8 %expert_forward.1 = (bf16[1152,768]{1,0:T(8,128)(2,1)}, bf16[1152,768]{1,0:T(8,128)(2,1)}, bf16[1152,768]{1,0:T(8,128)(2,1)}, bf16[128,2048]{1,0:T(8,128)(2,1)}) custom-call(bf16[1024,2304]{1,0:T(8,128)(2,1)} %bitcast.8.x_ref.a_ref, bf16[2048,1536]{1,0:T(8,128)(2,1)} %bitcast.26, bf16[2048,1536]{1,0:T(8,128)(2,1)} %bitcast.27), custom_call_target="tpu_custom_call" | custom-call | flops 7247757312 | bytes 16318464 | tf_op jit(solution)/shard_map/expert_forward/pallas_call | solution.py:233
  149.6 41.2 %all-to-all-done.4 = bf16[128,8,2304]{2,1,0:T(8,128)(2,1)} async-done(((bf16[128,8,2304]{2,1,0:T(8,128)(2,1)}), bf16[128,8,2304]{2,1,0:T(8,128)(2,1)}, u32[]{:S(2)}, u32[]{:S(2)}) %all-to-all-start.4) | async-done | bytes 4718624 | tf_op jit(solution)/shard_map/all_to_all | solution.py:615
  190.8 20.3 %expert_backward.1 = (bf16[1024,2304]{1,0:T(8,128)(2,1)}, bf16[1152,1536]{1,0:T(8,128)(2,1)}, bf16[128,2048]{1,0:T(8,128)(2,1)}) custom-call(bf16[1024,2304]{1,0:T(8,128)(2,1)} %bitcast.11.refs_0_.refs_1_.refs_2_.refs_3_.b_ref, bf16[1024,2304]{1,0:T(8,128)(2,1)} %bitcast.11.refs_0_.refs_1_.refs_2_.refs_3_.b_ref, ...), custom_call_target="tpu_custom_call" | custom-call | flops 10871635968 | bytes 18874368 | tf_op jit(solution)/shard_map/expert_backward/pallas_call | solution.py:318
  211.1 7.4 %all-to-all-start.5 = ((bf16[128,8,2304]{2,1,0:T(8,128)(2,1)}), bf16[128,8,2304]{2,1,0:T(8,128)(2,1)}, u32[]{:S(2)}, u32[]{:S(2)}) async-start(bf16[128,8,2304]{2,1,0:T(8,128)(2,1)} %bitcast.25), calls=%async_computation.5 | async-start | bytes 9437184 | tf_op jit(solution)/shard_map/all_to_all | solution.py:615
  218.5 9.7 %down_grad.1 = bf16[768,2048]{1,0:T(8,128)(2,1)} custom-call(bf16[1152,768]{1,0:T(8,128)(2,1)} %get-tuple-element.82.a_ref.a9_ref, bf16[1152,768]{1,0:T(8,128)(2,1)} %get-tuple-element.82.a_ref.a9_ref, bf16[1024,2304]{1,0:T(8,128)(2,1)} %bitcast.11.refs_0_.refs_1_.refs_2_.refs_3_.b_ref, bf16[128,2048]{1,0:T(8,128)(2,1)} %get-tuple-element.83.b9_ref), custom_call_target="tpu_custom_call" | custom-call | flops 3623878656 | bytes 9633792 | tf_op jit(solution)/shard_map/down_grad/pallas_call | solution.py:376
  228.2 13.3 %gate_up_grad.1 = bf16[2048,1536]{1,0:T(8,128)(2,1)} custom-call(bf16[1024,2304]{1,0:T(8,128)(2,1)} %bitcast.8.x_ref.a_ref, bf16[128,2048]{1,0:T(8,128)(2,1)} %get-tuple-element.80.a9_ref, bf16[1152,1536]{1,0:T(8,128)(2,1)} %get-tuple-element.81.b_ref.b9_ref, bf16[1152,1536]{1,0:T(8,128)(2,1)} %get-tuple-element.81.b_ref.b9_ref), custom_call_target="tpu_custom_call" | custom-call | flops 7247757312 | bytes 14548992 | tf_op jit(solution)/shard_map/gate_up_grad/pallas_call | solution.py:376
  241.4 32.5 %all-to-all-done.5 = bf16[128,8,2304]{2,1,0:T(8,128)(2,1)} async-done(((bf16[128,8,2304]{2,1,0:T(8,128)(2,1)}), bf16[128,8,2304]{2,1,0:T(8,128)(2,1)}, u32[]{:S(2)}, u32[]{:S(2)}) %all-to-all-start.5) | async-done | bytes 4718624 | tf_op jit(solution)/shard_map/all_to_all | solution.py:615
  273.9 3.8 %combine.1 = bf16[128,2048]{1,0:T(8,128)(2,1)} custom-call(bf16[128,1024]{1,0:T(8,128)(2,1)S(1)} %get-tuple-element.73.mask_ref, bf16[128,128]{1,0:T(8,128)(2,1)S(1)} %get-tuple-element.74.last_ref, bf16[16,2048]{1,0:T(8,128)(2,1)S(1)} %get-tuple-element.75.cot_ref, bf16[1024,2304]{1,0:T(8,128)(2,1)} %bitcast.14.got_ref.fold_ref, ...), custom_call_target="tpu_custom_call" | custom-call | tf_op jit(solution)/shard_map/combine/pallas_call | solution.py:452
  (25 shorter events, 8.2 us)
Async XLA Ops:
  0.6 32.3 %copy-start.3 = (s32[128,8]{0,1:T(8,128)S(1)}, s32[128,8]{0,1:T(8,128)}, u32[]{:S(2)}) copy-start(s32[128,8]{0,1:T(8,128)} %param.12) | copy-start | bytes 12292
  0.6 32.3 %copy-start.2 = (bf16[128,2048]{1,0:T(8,128)(2,1)S(1)}, bf16[128,2048]{1,0:T(8,128)(2,1)}, u32[]{:S(2)}) copy-start(bf16[128,2048]{1,0:T(8,128)(2,1)} %tok_ref.1) | copy-start | bytes 1572868
  2.7 35.7 %copy-start.5 = (s32[256]{0:T(256)S(1)}, s32[256]{0:T(256)}, u32[]{:S(2)}) copy-start(s32[256]{0:T(256)} %param.10) | copy-start | bytes 3076
  2.7 22.3 %all-to-all-start = ((bf16[16,256,128]{2,1,0:T(8,128)(2,1)}), bf16[16,256,128]{2,1,0:T(8,128)(2,1)S(1)}, u32[]{:S(2)}, u32[]{:S(2)}) async-start(bf16[16,256,128]{2,1,0:T(8,128)(2,1)} %broadcast_in_dim.27), calls=%async_computation | async-start | bytes 2097152 | tf_op jit(solution)/shard_map/all_to_all | solution.py:608
  26.2 12.2 %all-to-all-start.1 = ((f32[16,2,256]{2,1,0:T(2,128)}), f32[16,2,256]{2,1,0:T(2,128)S(1)}, u32[]{:S(2)}, u32[]{:S(2)}) async-start(f32[16,2,256]{2,1,0:T(2,128)} %broadcast_in_dim.28), calls=%async_computation.1 | async-start | bytes 65536 | tf_op jit(solution)/shard_map/all_to_all | solution.py:608
  36.3 2.2 copy-start
  40.0 21.0 %all-to-all-start.2 = ((bf16[16,16,2048]{2,1,0:T(8,128)(2,1)}), bf16[16,16,2048]{2,1,0:T(8,128)(2,1)S(1)}, u32[]{:S(2)}, u32[]{:S(2)}) async-start(bf16[16,16,2048]{2,1,0:T(8,128)(2,1)} %bitcast.6), calls=%async_computation.2 | async-start | bytes 2097152 | tf_op jit(solution)/shard_map/all_to_all | solution.py:647
  47.3 2.5 collective-permute-start
  61.0 9.2 %copy-start.4 = (f32[128,8]{0,1:T(8,128)S(1)}, f32[128,8]{0,1:T(8,128)}, u32[]{:S(2)}) copy-start(f32[128,8]{0,1:T(8,128)} %param.13) | copy-start | bytes 12292
  61.0 65.6 %all-to-all-start.3 = ((bf16[128,8,2304]{2,1,0:T(8,128)(2,1)}), bf16[128,8,2304]{2,1,0:T(8,128)(2,1)}, u32[]{:S(2)}, u32[]{:S(2)}) async-start(bf16[128,8,2304]{2,1,0:T(8,128)(2,1)} %bitcast.17), calls=%async_computation.3 | async-start | bytes 9437184 | tf_op jit(solution)/shard_map/all_to_all | solution.py:615
  74.1 2.2 copy-start.1
  76.2 48.7 %collective-permute-start.1 = (bf16[128,256]{1,0:T(8,128)(2,1)S(1)}, bf16[128,256]{1,0:T(8,128)(2,1)S(1)}, u32[]{:S(2)}, u32[]{:S(2)}) collective-permute-start(bf16[128,256]{1,0:T(8,128)(2,1)S(1)} %get-tuple-element.62), channel_id=1, source_target_pairs={{0,32},{16,48},{32,64},{48,80},{64,96},{80,112},{96,0},{112,16},{1... | collective-permute-start | bytes 196616 | tf_op jit(solution)/shard_map/ppermute | solution.py:659
  77.5 49.1 %collective-permute-start.2 = (bf16[128,256]{1,0:T(8,128)(2,1)S(1)}, bf16[128,256]{1,0:T(8,128)(2,1)S(1)}, u32[]{:S(2)}, u32[]{:S(2)}) collective-permute-start(bf16[128,256]{1,0:T(8,128)(2,1)S(1)} %get-tuple-element.63), channel_id=1, source_target_pairs={{0,64},{16,80},{32,96},{48,112},{64,0},{80,16},{96,32},{112,48},{1... | collective-permute-start | bytes 196616 | tf_op jit(solution)/shard_map/ppermute | solution.py:659
  80.0 46.6 %collective-permute-start.3 = (bf16[128,256]{1,0:T(8,128)(2,1)S(1)}, bf16[128,256]{1,0:T(8,128)(2,1)S(1)}, u32[]{:S(2)}, u32[]{:S(2)}) collective-permute-start(bf16[128,256]{1,0:T(8,128)(2,1)S(1)} %get-tuple-element.64), channel_id=1, source_target_pairs={{0,96},{16,112},{32,0},{48,16},{64,32},{80,48},{96,64},{112,80},{1... | collective-permute-start | bytes 196616 | tf_op jit(solution)/shard_map/ppermute | solution.py:659
  126.6 64.2 %all-to-all-start.4 = ((bf16[128,8,2304]{2,1,0:T(8,128)(2,1)}), bf16[128,8,2304]{2,1,0:T(8,128)(2,1)}, u32[]{:S(2)}, u32[]{:S(2)}) async-start(bf16[128,8,2304]{2,1,0:T(8,128)(2,1)} %bitcast.20), calls=%async_computation.4 | async-start | bytes 9437184 | tf_op jit(solution)/shard_map/all_to_all | solution.py:615
  211.1 62.8 %all-to-all-start.5 = ((bf16[128,8,2304]{2,1,0:T(8,128)(2,1)}), bf16[128,8,2304]{2,1,0:T(8,128)(2,1)}, u32[]{:S(2)}, u32[]{:S(2)}) async-start(bf16[128,8,2304]{2,1,0:T(8,128)(2,1)} %bitcast.25), calls=%async_computation.5 | async-start | bytes 9437184 | tf_op jit(solution)/shard_map/all_to_all | solution.py:615
